TPU v7x, 256 devices: a whole 4x4x8 slice. The times are simulated.
256 devices in a mesh: pre: 16 (over x_lo, z), tp: 8 (over x_hi, y), dec: 2 (over core).
Axes of the slice: x: 4 (x_hi: 2, x_lo: 2; x = x_hi * 2 + x_lo), y: 4, z: 8, core: 2. Of those that a mesh axis runs over, the one named last changes fastest.
Arguments:
- tokens: bfloat16 [16384, 2048], P(('pre', 'tp', 'dec')), may hold values from -6 to 6
- route_ids: int32 [16384, 6], P(('pre', 'tp', 'dec')), may hold values from 0 to 63, all different within a row; in each aligned block of 64 rows (0 to 63, 64 to 127, ...) at most 12 rows name the same one
- route_weights: float32 [16384, 6], P(('pre', 'tp', 'dec')), may hold values from 0.05 to 0.4
- gate_weight: bfloat16 [2048, 90112], P(None, ('pre', 'tp')), may hold values from -0.125 to 0.125
- up_weight: bfloat16 [2048, 90112], P(None, ('pre', 'tp')), may hold values from -0.125 to 0.125
- down_weight: bfloat16 [90112, 2048], P(('pre', 'tp')), may hold values from -0.15625 to 0.15625
- prefill_cache: bfloat16 [2, 8, 256, 64, 1024], P(None, 'tp', 'pre', None, 'dec'), may hold values from -6 to 6
- handover_table: int32 [8, 256], replicated, may hold values from 0 to 255, as said below
Outputs:
- moe_output: bfloat16 [16384, 2048], P(('pre', 'tp', 'dec'))
- decode_cache: bfloat16 [2, 8, 256, 64, 1024], P(None, 'tp', 'pre', None, 'dec')
Inputs may be any that keep to these rules, and one draw needn't show every extreme that they name: `route_ids`: each token names 6 different experts; within the rows of one device (64 consecutive tokens) no expert is named by more than 12 routes, a bound that some block reaches. `handover_table`: each row is a permutation of 0 to 255. The 16 slots g with g // 16 = s (one prefill device) map to at most 2 slots q with q // 16 = p (one decode device), for every s and p, and to exactly 2 for some pair.
All inputs are finite; a program needn't handle non-finite values.
Results may differ from a plain program's by a relative error of at most 0.0085.
Values may be sent and summed in bfloat16 or wider, within the bound.
No kernel may reach another device: no remote copies, remote signals or barrier semaphores. Data moves between devices by JAX's collectives and lax.ppermute only.
A program may use at most 128 MiB of HBM per device.

v0:
```python
import jax
import jax.numpy as jnp
from jax import lax
from jax.sharding import PartitionSpec as P


def slot_ranks(labels, count):
    onehot = (labels[:, None] == jnp.arange(count, dtype=jnp.int32)[None, :]).astype(jnp.int32)
    before = jnp.cumsum(onehot, axis=0) - onehot
    return jnp.sum(before * onehot, axis=1)


def shards(
    tokens,
    route_ids,
    route_weights,
    gate_weight,
    up_weight,
    down_weight,
    prefill_cache,
    handover_table,
):
    tok_dev, width = tokens.shape
    top_count = route_ids.shape[1]
    groups = lax.axis_size("pre") * lax.axis_size("tp")
    experts_all = groups // 2
    most = min(tok_dev, 2 * tok_dev * top_count // experts_all)
    ids_flat = route_ids.reshape(-1)
    positions = slot_ranks(ids_flat, experts_all)
    dest_row = ids_flat * most + positions
    source_rows = jnp.repeat(jnp.arange(tok_dev, dtype=jnp.int32), top_count)
    packed = (
        jnp.zeros((experts_all * most, width), jnp.bfloat16).at[dest_row].set(tokens[source_rows])
    )
    outgoing = jnp.broadcast_to(
        packed.reshape(experts_all, 1, most, width), (experts_all, 2, most, width)
    )
    outgoing = outgoing.reshape(groups, most, width)
    received = lax.all_to_all(outgoing, ("pre", "tp"), split_axis=0, concat_axis=0, tiled=True)
    flat = received.reshape(-1, width)
    gate = jnp.dot(flat, gate_weight, preferred_element_type=jnp.float32)
    upper = jnp.dot(flat, up_weight, preferred_element_type=jnp.float32)
    hidden = (jax.nn.silu(gate) * upper).astype(jnp.bfloat16)
    result = jnp.dot(hidden, down_weight, preferred_element_type=jnp.float32)
    partial_out = result.reshape(received.shape[0], received.shape[1], width)
    returned = lax.all_to_all(partial_out, ("pre", "tp"), split_axis=0, concat_axis=0, tiled=True)
    expert_rows = jnp.sum(returned.reshape(experts_all, 2, most, width), axis=1).astype(
        jnp.bfloat16
    )
    picked = expert_rows.reshape(-1, width)[dest_row].reshape(tok_dev, top_count, width)
    moe_output = jnp.einsum("tk,tkd->td", route_weights, picked.astype(jnp.float32)).astype(
        jnp.bfloat16
    )
    layers, _, blk_dev, blk, half_width = prefill_cache.shape
    sources = lax.axis_size("pre")
    spare = blk_dev // sources + 1
    column = lax.dynamic_index_in_dim(handover_table, lax.axis_index("tp"), 0, keepdims=False)
    dest_dev = (column // blk_dev).reshape(sources, blk_dev)
    onehot = (dest_dev[:, :, None] == jnp.arange(sources, dtype=jnp.int32)[None, None, :]).astype(
        jnp.int32
    )
    rank_all = jnp.sum((jnp.cumsum(onehot, axis=1) - onehot) * onehot, axis=2)
    here = lax.axis_index("pre")
    my_dest = lax.dynamic_index_in_dim(dest_dev, here, 0, keepdims=False)
    my_rank = lax.dynamic_index_in_dim(rank_all, here, 0, keepdims=False)
    blocks_out = jnp.zeros((layers, sources, spare, blk, half_width), jnp.bfloat16)
    blocks_out = blocks_out.at[:, my_dest, my_rank].set(prefill_cache[:, 0])
    arrived = lax.all_to_all(blocks_out, "pre", split_axis=1, concat_axis=1, tiled=True)
    pool_size = column.shape[0]
    inverse = (
        jnp.zeros((pool_size,), jnp.int32).at[column].set(jnp.arange(pool_size, dtype=jnp.int32))
    )
    anchor = lax.dynamic_slice_in_dim(inverse, here * blk_dev, blk_dev)
    pick = anchor // blk_dev * spare + rank_all.reshape(-1)[anchor]
    decode_cache = arrived.reshape(layers, sources * spare, blk, half_width)[:, pick][:, None]
    return (moe_output, decode_cache)


def solution(mesh):
    return jax.shard_map(
        shards,
        mesh=mesh,
        in_specs=(
            P(("pre", "tp", "dec"), None),
            P(("pre", "tp", "dec"), None),
            P(("pre", "tp", "dec"), None),
            P(None, ("pre", "tp")),
            P(None, ("pre", "tp")),
            P(("pre", "tp"), None),
            P(None, "tp", "pre", None, "dec"),
            P(),
        ),
        out_specs=(P(("pre", "tp", "dec"), None), P(None, "tp", "pre", None, "dec")),
        check_vma=False,
    )
```

profile of v0, /device:TPU:96, one launch (start us, length us, event | category | flops | bytes accessed | tf_op | source)
XLA Modules:
  0.0 748.9 jit_solution(11944358911356710262)
XLA Ops:
  4.3 10.4 %scatter_custom_fusion = bf16[768,2048]{1,0:T(8,128)(2,1)} fusion(s32[384]{0:T(512)S(1)} %fusion.13, bf16[64,2048]{1,0:T(8,128)(2,1)} %param.8, s32[1024]{0:T(1024)S(1)} %pad_clamp_fusion.3, bf16[]{:T(256)} %constant.63.clone.1), kind=kCustom, calls=%fused_computation.9 | custom fusion | bytes 3146240 | tf_op jit(solution)/shard_map/scatter | solution.py:33
  14.7 6.1 broadcast_in_dim.35
  20.8 6.7 broadcast_in_dim.36
  27.5 14.6 %all-to-all-start = ((bf16[128,12,2048]{2,1,0:T(8,128)(2,1)}), bf16[128,12,2048]{2,1,0:T(8,128)(2,1)}, u32[]{:S(2)}, u32[]{:S(2)}) async-start(bf16[128,12,2048]{2,1,0:T(8,128)(2,1)} %bitcast.56), calls=%async_computation | async-start | bytes 16777216 | tf_op jit(solution)/shard_map/all_to_all | solution.py:39
  43.0 3.1 copy.32
  46.8 2.4 broadcast_in_dim.37
  49.3 6.1 scatter_fusion
  55.3 4.6 copy.33
  60.0 168.8 %all-to-all-done = bf16[128,12,2048]{2,1,0:T(8,128)(2,1)} async-done(((bf16[128,12,2048]{2,1,0:T(8,128)(2,1)}), bf16[128,12,2048]{2,1,0:T(8,128)(2,1)}, u32[]{:S(2)}, u32[]{:S(2)}) %all-to-all-start) | async-done | bytes 6291488 | tf_op jit(solution)/shard_map/all_to_all | solution.py:39
  228.8 5.7 all-to-all-start.2
  234.5 10.7 %reshape.224 = bf16[1536,2048]{1,0:T(8,128)(2,1)} reshape(bf16[128,12,2048]{2,1,0:T(8,128)(2,1)} %all-to-all-done) | data formatting | bytes 12582912 | tf_op jit(solution)/shard_map/reshape | solution.py:40
  245.2 10.3 %fusion.23 = f32[1536,704]{0,1:T(8,128)} fusion(bf16[1536,2048]{1,0:T(8,128)(2,1)} %reshape.224, bf16[2048,704]{0,1:T(8,128)(2,1)} %param.11), kind=kOutput, calls=%fused_computation.67 | convolution fusion | flops 4429185024 | bytes 13500416 | tf_op jit(solution)/shard_map/dot_general | solution.py:41
  255.5 19.1 %fusion.4 = f32[1536,2048]{1,0:T(8,128)} fusion(bf16[704,2048]{1,0:T(8,128)(2,1)S(1)} %copy-done, f32[1536,704]{0,1:T(8,128)} %fusion.23, bf16[1536,2048]{1,0:T(8,128)(2,1)} %reshape.224, bf16[2048,704]{0,1:T(8,128)(2,1)} %param.12), kind=kOutput, calls=%fused_computation.14 | convolution fusion | flops 8864858112 | bytes 28966912 | tf_op jit(solution)/shard_map/dot_general | solution.py:44
  274.6 14.9 %reshape.225 = f32[128,12,2048]{2,1,0:T(8,128)} reshape(f32[1536,2048]{1,0:T(8,128)} %fusion.4) | data formatting | bytes 25165824 | tf_op jit(solution)/shard_map/reshape | solution.py:45
  289.5 38.4 %all-to-all-done.2 = bf16[2,16,2,64,512]{4,3,2,0,1:T(8,128)(2,1)} async-done(((bf16[2,16,2,64,512]{4,3,2,0,1:T(8,128)(2,1)}), bf16[2,16,2,64,512]{4,3,2,0,1:T(8,128)(2,1)}, u32[]{:S(2)}, u32[]{:S(2)}) %all-to-all-start.2) | async-done | bytes 4194336 | tf_op jit(solution)/shard_map/all_to_all | solution.py:68
  327.9 13.0 %all-to-all-start.1 = ((f32[128,12,2048]{2,1,0:T(8,128)}), f32[128,12,2048]{2,1,0:T(8,128)}, u32[]{:S(2)}, u32[]{:S(2)}) async-start(f32[128,12,2048]{2,1,0:T(8,128)} %reshape.225), calls=%async_computation.1 | async-start | bytes 33554432 | tf_op jit(solution)/shard_map/all_to_all | solution.py:46
  344.2 4.6 copy.34
  348.8 2.9 gather_fusion.2
  353.2 365.6 %all-to-all-done.1 = f32[128,12,2048]{2,1,0:T(8,128)} async-done(((f32[128,12,2048]{2,1,0:T(8,128)}), f32[128,12,2048]{2,1,0:T(8,128)}, u32[]{:S(2)}, u32[]{:S(2)}) %all-to-all-start.1) | async-done | bytes 12582944 | tf_op jit(solution)/shard_map/all_to_all | solution.py:46
  718.8 9.6 %bitcast_reduce_fusion = bf16[64,12,2048]{2,1,0:T(8,128)(2,1)} fusion(f32[128,12,2048]{2,1,0:T(8,128)} %all-to-all-done.1), kind=kLoop, calls=%fused_computation.7 | loop fusion | flops 1572864 | bytes 15728640 | tf_op jit(solution)/shard_map/reduce_sum | solution.py:47
  728.4 6.2 convert_element_type.28
  734.5 7.5 %gather_fusion = bf16[384,2048]{1,0:T(8,128)(2,1)} fusion(bf16[768,2048]{1,0:T(8,128)(2,1)} %convert_element_type.28, s32[1024]{0:T(1024)S(1)} %pad_clamp_fusion.2), kind=kCustom, calls=%fused_computation.1 | custom fusion | bytes 3147264 | tf_op jit(solution)/shard_map/gather | solution.py:50
  742.0 3.7 reshape.227
  745.7 2.3 fusion.24
  (43 shorter events, 10.8 us)
Async XLA Ops:
  0.6 254.8 %copy-start = (bf16[704,2048]{1,0:T(8,128)(2,1)S(1)}, bf16[704,2048]{1,0:T(8,128)(2,1)}, u32[]{:S(2)}) copy-start(bf16[704,2048]{1,0:T(8,128)(2,1)} %param.13) | copy-start | bytes 8650756
  27.5 201.3 %all-to-all-start = ((bf16[128,12,2048]{2,1,0:T(8,128)(2,1)}), bf16[128,12,2048]{2,1,0:T(8,128)(2,1)}, u32[]{:S(2)}, u32[]{:S(2)}) async-start(bf16[128,12,2048]{2,1,0:T(8,128)(2,1)} %bitcast.56), calls=%async_computation | async-start | bytes 16777216 | tf_op jit(solution)/shard_map/all_to_all | solution.py:39
  228.8 99.1 %all-to-all-start.2 = ((bf16[2,16,2,64,512]{4,3,2,0,1:T(8,128)(2,1)}), bf16[2,16,2,64,512]{4,3,2,0,1:T(8,128)(2,1)}, u32[]{:S(2)}, u32[]{:S(2)}) async-start(bf16[2,16,2,64,512]{4,3,2,0,1:T(8,128)(2,1)} %copy.33), calls=%async_computation.2 | async-start | bytes 8388608 | tf_op jit(solution)/shard_map/all_to_all | solution.py:68
  289.5 51.5 %copy-start.2 = (f32[64,6]{0,1:T(8,128)S(1)}, f32[64,6]{0,1:T(8,128)}, u32[]{:S(2)}) copy-start(f32[64,6]{0,1:T(8,128)} %param.10) | copy-start | bytes 4612
  327.9 390.9 %all-to-all-start.1 = ((f32[128,12,2048]{2,1,0:T(8,128)}), f32[128,12,2048]{2,1,0:T(8,128)}, u32[]{:S(2)}, u32[]{:S(2)}) async-start(f32[128,12,2048]{2,1,0:T(8,128)} %reshape.225), calls=%async_computation.1 | async-start | bytes 33554432 | tf_op jit(solution)/shard_map/all_to_all | solution.py:46
  734.5 14.3 %copy-start.1 = (bf16[704,2048]{1,0:T(8,128)(2,1)S(1)}, bf16[704,2048]{1,0:T(8,128)(2,1)}, u32[]{:S(2)}) copy-start(bf16[704,2048]{1,0:T(8,128)(2,1)} %param.13) | copy-start | bytes 8650756
where the time goes:
time: 751 us; the launch traced here: 749 us
  waiting for transfers between devices  573 us (76%)
  local copies, waits for them, and re-layouts  97.3 us (13%)
  starting transfers between devices  33.4 us (4%)
  matrix products  31.7 us (4%)
  other arithmetic  12.9 us (2%)
    all_to_all x1, waiting for transfers between devices, shards(): lax.all_to_all(partial_out, ('pre', 'tp'), split_axis=0, concat_axis=0, t...  366 us
    all_to_all x1, waiting for transfers between devices, shards(): lax.all_to_all(outgoing, ('pre', 'tp'), split_axis=0, concat_axis=0, tile...  169 us
    all_to_all x1, waiting for transfers between devices, shards(): lax.all_to_all(blocks_out, 'pre', split_axis=1, concat_axis=1, tiled=True)  38.4 us
    dot_general x1, matrix products, shards(): result = jnp.dot(hidden, down_weight, preferred_element_type=jnp.float32)  19.1 us
  transfers between devices with their start and end apart: 3, of which 3 were waited for; matrix products, arithmetic and copies ran while one was open for 11% of the time, Pallas kernels for 0%

commit v1 on v0

v1 whole, which is shorter than its diff:
```python
import functools

import jax
import jax.numpy as jnp
from jax import lax
from jax.experimental import pallas as pl
from jax.experimental.pallas import tpu as pltpu
from jax.sharding import PartitionSpec as P

F32 = jnp.float32
BF16 = jnp.bfloat16
PARTS = 4


def iota(shape, dim):
    return lax.broadcasted_iota(jnp.int32, shape, dim)


def divide(x, by):
    return ((x.astype(F32) + 0.5) * (1.0 / by)).astype(jnp.int32)


def dot(a, b, contract):
    return lax.dot_general(a, b, (contract, ((), ())), preferred_element_type=F32)


def pick_mask(subrow, part_lane, slot, rows, chunk):
    group = divide(subrow, chunk)
    within = subrow - group * chunk
    part = divide(within, rows)
    row = within - part * rows
    place = (group & 1) * rows + row
    return (slot == place.astype(F32)) & (part == part_lane)


def pack_kernel(rows, ids_ref, w_ref, tok_ref, out_ref, slot_ref, whi_ref, wlo_ref, tok_sc):
    step = pl.program_id(0)
    count = ids_ref.shape[0]
    toks = ids_ref.shape[1]
    experts = slot_ref.shape[0]
    width = tok_ref.shape[1] // PARTS
    chunk = PARTS * rows

    @pl.when(step == 0)
    def _():
        eids = iota((experts, toks), 0)
        named = jnp.zeros((experts, toks), F32)
        weight = jnp.zeros((experts, toks), F32)
        for k in range(count):
            hit = ids_ref[k : k + 1, :] == eids
            named = named + jnp.where(hit, 1.0, 0.0)
            weight = weight + jnp.where(hit, w_ref[k : k + 1, :], 0.0)
        earlier = (iota((toks, toks), 0) < iota((toks, toks), 1)).astype(BF16)
        rank = dot(named.astype(BF16), earlier, ((1,), (0,)))
        slot = jnp.where(named > 0.5, rank, 255.0)
        high = weight.astype(BF16)
        low = (weight - high.astype(F32)).astype(BF16)
        slot_b = slot.astype(BF16)
        for p in range(PARTS):
            slot_ref[:, p * toks : (p + 1) * toks] = slot_b
            whi_ref[:, p * toks : (p + 1) * toks] = high
            wlo_ref[:, p * toks : (p + 1) * toks] = low
            tok_sc[p * toks : (p + 1) * toks, :] = tok_ref[:, p * width : (p + 1) * width]

    block = out_ref.shape[0]
    base = step * block
    subrow_e = base + iota((block, experts), 0)
    spread = (divide(subrow_e, 2 * chunk) == iota((block, experts), 1)).astype(BF16)
    slot_q = dot(spread, slot_ref[...], ((1,), (0,)))
    subrow = base + iota((block, PARTS * toks), 0)
    lane_part = divide(iota((block, PARTS * toks), 1), toks)
    mask = pick_mask(subrow, lane_part, slot_q, rows, chunk)
    out_ref[...] = dot(mask.astype(BF16), tok_sc[...], ((1,), (0,))).astype(BF16)


def pack(ids_t, w_t, tokens, experts, rows):
    toks, wide = tokens.shape
    chunk = PARTS * rows
    total = experts * 2 * chunk
    steps = 8
    width = wide // PARTS
    whole = lambda i: (0, 0)
    small = jax.ShapeDtypeStruct((experts, PARTS * toks), BF16)
    small_spec = pl.BlockSpec((experts, PARTS * toks), whole)

    return pl.pallas_call(
        functools.partial(pack_kernel, rows),
        grid=(steps,),
        in_specs=[
            pl.BlockSpec(ids_t.shape, whole),
            pl.BlockSpec(w_t.shape, whole),
            pl.BlockSpec(tokens.shape, whole),
        ],
        out_specs=[
            pl.BlockSpec((total // steps, width), lambda i: (i, 0)),
            small_spec,
            small_spec,
            small_spec,
        ],
        out_shape=[jax.ShapeDtypeStruct((total, width), BF16), small, small, small],
        scratch_shapes=[pltpu.VMEM((PARTS * toks, width), BF16)],
        name="pack",
    )(ids_t, w_t, tokens)


def combine_kernel(rows, slot_ref, whi_ref, wlo_ref, ret_ref, out_ref, acc):
    step = pl.program_id(0)
    experts, lanes = slot_ref.shape
    toks = lanes // PARTS
    block, width = ret_ref.shape
    chunk = PARTS * rows
    base = step * block
    subrow_e = base + iota((experts, block), 1)
    spread = (divide(subrow_e, 2 * chunk) == iota((experts, block), 0)).astype(BF16)
    slot_q = dot(slot_ref[...], spread, ((0,), (0,)))
    high = dot(whi_ref[...], spread, ((0,), (0,)))
    low = dot(wlo_ref[...], spread, ((0,), (0,)))
    subrow = base + iota((lanes, block), 1)
    lane_part = divide(iota((lanes, block), 0), toks)
    mask = pick_mask(subrow, lane_part, slot_q, rows, chunk)
    left = jnp.concatenate(
        [jnp.where(mask, high, 0.0).astype(BF16), jnp.where(mask, low, 0.0).astype(BF16)], axis=0
    )
    both = dot(left, ret_ref[...], ((1,), (0,)))
    part = both[:lanes] + both[lanes:]

    @pl.when(step == 0)
    def _():
        acc[...] = part

    @pl.when(step > 0)
    def _():
        acc[...] = acc[...] + part

    @pl.when(step == pl.num_programs(0) - 1)
    def _():
        for p in range(PARTS):
            out_ref[:, p * width : (p + 1) * width] = acc[p * toks : (p + 1) * toks, :].astype(BF16)


def combine(slot, whi, wlo, returned, rows):

    experts, lanes = slot.shape
    toks = lanes // PARTS
    total, width = returned.shape
    steps = 8
    whole = lambda i: (0, 0)
    return pl.pallas_call(
        functools.partial(combine_kernel, rows),
        grid=(steps,),
        in_specs=[
            pl.BlockSpec(slot.shape, whole),
            pl.BlockSpec(slot.shape, whole),
            pl.BlockSpec(slot.shape, whole),
            pl.BlockSpec((total // steps, width), lambda i: (i, 0)),
        ],
        out_specs=pl.BlockSpec((toks, PARTS * width), whole),
        out_shape=jax.ShapeDtypeStruct((toks, PARTS * width), BF16),
        scratch_shapes=[pltpu.VMEM((lanes, width), F32)],
        name="combine",
    )(slot, whi, wlo, returned)


def expert_kernel(
    rows, x_ref, g0, u0, d0, g1, u1, d1, g2, u2, d2, o_ref, wg, wu, wd, xs, acc, perm, sems
):
    half = g0.shape[0]
    quarter = g1.shape[0]
    copies = []
    for i, (src, dst, start) in enumerate(
        [
            (g0, wg, 0),
            (u0, wu, 0),
            (d0, wd, 0),
            (g1, wg, half),
            (u1, wu, half),
            (g2, wg, half + quarter),
            (u2, wu, half + quarter),
            (d1, wd, half),
            (d2, wd, half + quarter),
        ]
    ):
        copy = pltpu.make_async_copy(src, dst.at[pl.ds(start, src.shape[0])], sems.at[i])
        copy.start()
        copies.append(copy)

    sources = 16
    chunk = PARTS * rows
    small = sources * rows
    big = sources * chunk
    width = x_ref.shape[1]
    index = iota((big, big), 0)
    part = divide(index, small)
    rest = index - part * small
    source = divide(rest, rows)
    row = rest - source * rows
    perm[...] = (source * chunk + part * rows + row == iota((big, big), 1)).astype(BF16)

    def unpack(b, _):
        y = dot(perm[...], x_ref[pl.ds(b * big, big), :], ((1,), (0,))).astype(BF16)
        for p in range(PARTS):
            xs[pl.ds(b * small, small), p * width : (p + 1) * width] = y[
                p * small : (p + 1) * small, :
            ]
        return 0

    blocks = x_ref.shape[0] // big
    lax.fori_loop(0, blocks, unpack, 0)
    for copy in copies:
        copy.wait()

    total = wg.shape[0]
    cuts = list(range(0, total, 512)) + [total]
    mrows = 4 * small

    def run(m, _):
        x = xs[pl.ds(m * mrows, mrows), :]
        for c in range(len(cuts) - 1):
            lo, hi = cuts[c], cuts[c + 1]
            gate = dot(x, wg[lo:hi, :], ((1,), (1,)))
            upper = dot(x, wu[lo:hi, :], ((1,), (1,)))
            hidden = (gate / (1.0 + jnp.exp(-gate)) * upper).astype(BF16)
            res = dot(hidden, wd[lo:hi, :], ((1,), (0,)))
            if c == 0:
                acc[...] = res
            elif c < len(cuts) - 2:
                acc[...] = acc[...] + res
            else:
                xs[pl.ds(m * mrows, mrows), :] = (acc[...] + res).astype(BF16)
        return 0

    lax.fori_loop(0, xs.shape[0] // mrows, run, 0)

    def repack(b, _):
        y = jnp.concatenate(
            [
                xs[pl.ds(b * small, small), p * width : (p + 1) * width]
                for p in range(PARTS)
            ],
            axis=0,
        )
        o_ref[pl.ds(b * big, big), :] = dot(perm[...], y, ((0,), (0,))).astype(BF16)
        return 0

    lax.fori_loop(0, blocks, repack, 0)


def expert(x, own, first, second, rows):

    half, wide = own[0].shape
    total = 2 * half
    count = x.shape[0] // PARTS
    anyspec = pl.BlockSpec(memory_space=pl.ANY)
    vm = pl.BlockSpec(memory_space=pltpu.VMEM)
    big = 16 * PARTS * rows
    return pl.pallas_call(
        functools.partial(expert_kernel, rows),
        in_specs=[vm] + [anyspec] * 9,
        out_specs=vm,
        out_shape=jax.ShapeDtypeStruct(x.shape, BF16),
        scratch_shapes=[
            pltpu.VMEM((total, wide), BF16),
            pltpu.VMEM((total, wide), BF16),
            pltpu.VMEM((total, wide), BF16),
            pltpu.VMEM((count, wide), BF16),
            pltpu.VMEM((64 * rows, wide), F32),
            pltpu.VMEM((big, big), BF16),
            pltpu.SemaphoreType.DMA((9,)),
        ],
        compiler_params=pltpu.CompilerParams(vmem_limit_bytes=60 * 1024 * 1024),
        cost_estimate=pl.CostEstimate(
            flops=6 * count * total * wide,
            bytes_accessed=6 * total * wide + 2 * x.size * 2,
            transcendentals=count * total,
        ),
        name="expert",
    )(x, *own, *first, *second)


def copy_kernel(index_ref, in_ref, out_ref):
    out_ref[...] = in_ref[...].reshape(out_ref.shape)


def gather_out(index, cache):
    layers, blk_dev, blk, wide = cache.shape
    slots = index.shape[0]
    return pl.pallas_call(
        copy_kernel,
        grid_spec=pltpu.PrefetchScalarGridSpec(
            num_scalar_prefetch=1,
            grid=(slots,),
            in_specs=[pl.BlockSpec((layers, 1, blk, wide), lambda i, n: (0, n[i], 0, 0))],
            out_specs=pl.BlockSpec((1, layers, blk, wide), lambda i, n: (i, 0, 0, 0)),
        ),
        out_shape=jax.ShapeDtypeStruct((slots, layers, blk, wide), cache.dtype),
        name="gather_out",
    )(index, cache)


def gather_in(index, arrived):
    slots = index.shape[0]
    _, layers, blk, wide = arrived.shape
    return pl.pallas_call(
        copy_kernel,
        grid_spec=pltpu.PrefetchScalarGridSpec(
            num_scalar_prefetch=1,
            grid=(slots,),
            in_specs=[pl.BlockSpec((1, layers, blk, wide), lambda i, n: (n[i], 0, 0, 0))],
            out_specs=pl.BlockSpec((layers, 1, blk, wide), lambda i, n: (0, i, 0, 0)),
        ),
        out_shape=jax.ShapeDtypeStruct((layers, slots, blk, wide), arrived.dtype),
        name="gather_in",
    )(index, arrived)


def handover_indices(handover_table, sources, blk_dev, spare):
    column = lax.dynamic_index_in_dim(handover_table, lax.axis_index("tp"), 0, keepdims=False)
    here = lax.axis_index("pre")
    table = column.reshape(sources, blk_dev)
    dest = table // blk_dev
    earlier = jnp.arange(blk_dev)[:, None] < jnp.arange(blk_dev)[None, :]
    same = dest[:, :, None] == dest[:, None, :]
    rank = jnp.sum((same & earlier[None]).astype(jnp.int32), axis=1)
    my_dest = lax.dynamic_index_in_dim(dest, here, 0, keepdims=False)
    my_rank = lax.dynamic_index_in_dim(rank, here, 0, keepdims=False)
    wanted = jnp.arange(sources * spare, dtype=jnp.int32)
    out_index = jnp.sum(
        jnp.where(
            wanted[:, None] == (my_dest * spare + my_rank)[None, :],
            jnp.arange(blk_dev, dtype=jnp.int32)[None, :],
            0,
        ),
        axis=1,
    )
    place = here * blk_dev + jnp.arange(blk_dev, dtype=jnp.int32)
    came = jnp.arange(sources, dtype=jnp.int32)[:, None] * spare + rank
    in_index = jnp.sum(
        jnp.where(place[:, None, None] == table[None], came[None], 0), axis=(1, 2)
    )
    return out_index, in_index


def shards(
    tokens,
    route_ids,
    route_weights,
    gate_weight,
    up_weight,
    down_weight,
    prefill_cache,
    handover_table,
):
    tok_dev, wide = tokens.shape
    top_count = route_ids.shape[1]
    groups = lax.axis_size("pre") * lax.axis_size("tp")
    tp = lax.axis_size("tp")
    experts_all = groups // 2
    most = min(tok_dev, 2 * tok_dev * top_count // experts_all)
    rows = most // 2

    half = down_weight.shape[0]
    quarter = half // 2
    own = (gate_weight.T, up_weight.T, down_weight)
    core = lax.axis_index("dec")
    swap = [(i, i ^ 1) for i in range(tp)]
    first, second = [], []
    for weight in own:
        piece = lax.dynamic_slice_in_dim(weight, core * quarter, quarter, 0)
        got = lax.ppermute(piece, "tp", swap)
        first.append(got)
        second.append(lax.ppermute(got, "dec", [(0, 1), (1, 0)]))

    packed, slot, whi, wlo = pack(route_ids.T, route_weights.T, tokens, experts_all, rows)
    chunk = PARTS * rows
    width = wide // PARTS
    received = lax.all_to_all(
        packed.reshape(groups, chunk, width), ("pre", "tp"), split_axis=0, concat_axis=0, tiled=True
    )
    result = expert(received.reshape(groups * chunk, width), own, first, second, rows)
    returned = lax.all_to_all(
        result.reshape(groups, chunk, width), ("pre", "tp"), split_axis=0, concat_axis=0, tiled=True
    )
    moe_output = combine(slot, whi, wlo, returned.reshape(groups * chunk, width), rows)

    layers, _, blk_dev, blk, half_width = prefill_cache.shape
    sources = lax.axis_size("pre")
    spare = blk_dev // sources + 1
    out_index, in_index = handover_indices(handover_table, sources, blk_dev, spare)
    leaving = gather_out(out_index, prefill_cache[:, 0])
    arrived = lax.all_to_all(leaving, "pre", split_axis=0, concat_axis=0, tiled=True)
    decode_cache = gather_in(in_index, arrived)[:, None]
    return (moe_output, decode_cache)


def solution(mesh):
    return jax.shard_map(
        shards,
        mesh=mesh,
        in_specs=(
            P(("pre", "tp", "dec"), None),
            P(("pre", "tp", "dec"), None),
            P(("pre", "tp", "dec"), None),
            P(None, ("pre", "tp")),
            P(None, ("pre", "tp")),
            P(("pre", "tp"), None),
            P(None, "tp", "pre", None, "dec"),
            P(),
        ),
        out_specs=(P(("pre", "tp", "dec"), None), P(None, "tp", "pre", None, "dec")),
        check_vma=False,
    )
```

time: 751 us -> 329 us (0.44)
  waiting for transfers between devices: 573 us -> 212 us
  local copies, waits for them, and re-layouts: 97.3 us -> 6.72 us
  Pallas kernels: 0 us -> 71.1 us
  matrix products: 31.7 us -> 0 us
  other arithmetic: 12.9 us -> 1.79 us
    all_to_all x3, waiting for transfers between devices: 573 us -> 119 us  [the longest x1 63.7 us: shards(): lax.all_to_all(result.reshape(groups, chunk, width), ('pre', 'tp'), split...]
    ppermute x0 -> x6, waiting for transfers between devices: none -> 92.7 us  [the longest x3 89.5 us: shards(): got = lax.ppermute(piece, 'tp', swap)]
    pallas_call x0 -> x5, Pallas kernels: none -> 71.1 us  [the longest x1 28.1 us: expert(): pl.pallas_call(functools.partial(expert_kernel, rows), in_specs=[vm] + [a...]
    dot_general x3 -> x0, matrix products: 31.7 us -> none  [the longest x1 19.1 us: shards(): result = jnp.dot(hidden, down_weight, preferred_element_type=jnp.float32)]
    reshape x5 -> x0, local copies, waits for them, and re-layouts: 29.5 us -> none  [the longest x1 14.9 us: shards(): partial_out = result.reshape(received.shape[0], received.shape[1], width)]
    scatter x4 -> x0, local copies, waits for them, and re-layouts: 22.4 us -> none  [the longest x2 10.7 us: shards(): blocks_out = blocks_out.at[:, my_dest, my_rank].set(prefill_cache[:, 0])]
    broadcast_in_dim x4 -> x0, local copies, waits for them, and re-layouts: 15.3 us -> none  [the longest x2 12.8 us: shards(): jnp.broadcast_to(packed.reshape(experts_all, 1, most, width), (experts_al...]
    gather x3 -> x0, local copies, waits for them, and re-layouts: 11 us -> none  [the longest x1 7.49 us: shards(): expert_rows.reshape(-1, width)[dest_row].reshape(tok_dev, top_count, width)]
  transfers between devices with their start and end apart: 3 -> 9, of which waited for: 3 -> 6; matrix products, arithmetic and copies ran while one was open for 11% -> 1% of each run, Pallas kernels for 0% -> 17%
where the time goes in v1:
time: 329 us; the launch traced here: 326 us
  waiting for transfers between devices  212 us (64%)
  Pallas kernels  71.1 us (22%)
  starting transfers between devices  33.7 us (10%)
  local copies, waits for them, and re-layouts  6.72 us (2%)
    ppermute x3, waiting for transfers between devices, shards(): got = lax.ppermute(piece, 'tp', swap)  89.5 us
    all_to_all x1, waiting for transfers between devices, shards(): lax.all_to_all(result.reshape(groups, chunk, width), ('pre', 'tp'), split...  63.7 us
    all_to_all x1, waiting for transfers between devices, shards(): lax.all_to_all(packed.reshape(groups, chunk, width), ('pre', 'tp'), split...  55.6 us
    pallas_call x1, Pallas kernels, expert(): pl.pallas_call(functools.partial(expert_kernel, rows), in_specs=[vm] + [a...  28.1 us
    pallas_call x1, Pallas kernels, gather_out(): pl.pallas_call(copy_kernel, grid_spec=pltpu.PrefetchScalarGridSpec(num_sc...  18.1 us
    all_to_all x1, starting transfers between devices, shards(): lax.all_to_all(packed.reshape(groups, chunk, width), ('pre', 'tp'), split...  14.1 us
    all_to_all x1, starting transfers between devices, shards(): lax.all_to_all(result.reshape(groups, chunk, width), ('pre', 'tp'), split...  11.3 us
    pallas_call x1, Pallas kernels, gather_in(): pl.pallas_call(copy_kernel, grid_spec=pltpu.PrefetchScalarGridSpec(num_sc...  10.1 us
  transfers between devices with their start and end apart: 9, of which 6 were waited for; matrix products, arithmetic and copies ran while one was open for 1% of the time, Pallas kernels for 17%

profile of v1, /device:TPU:96, one launch (start us, length us, event | category | flops | bytes accessed | tf_op | source)
XLA Modules:
  0.0 326.1 jit_solution(9412856582819910492)
XLA Ops:
  0.6 6.2 %pack.1 = (bf16[3072,512]{1,0:T(8,128)(2,1)}, bf16[64,256]{1,0:T(8,128)(2,1)}, bf16[64,256]{1,0:T(8,128)(2,1)}, bf16[64,256]{1,0:T(8,128)(2,1)}) custom-call(s32[6,64]{1,0:T(8,128)} %bitcast.26, f32[6,64]{1,0:T(8,128)} %bitcast.27, bf16[64,2048]{1,0:T(8,128)(2,1)} %tok_ref.1), custom_call_target="tpu_custom_call" | custom-call | tf_op jit(solution)/shard_map/pack/pallas_call | solution.py:86
  6.9 14.1 %all-to-all-start = ((bf16[128,24,512]{2,1,0:T(8,128)(2,1)}), bf16[128,24,512]{2,1,0:T(8,128)(2,1)S(1)}, u32[]{:S(2)}, u32[]{:S(2)}) async-start(bf16[128,24,512]{2,1,0:T(8,128)(2,1)} %bitcast.20), calls=%async_computation | async-start | bytes 6291456 | tf_op jit(solution)/shard_map/all_to_all | solution.py:376
  21.3 0.6 select_reduce_fusion.1.index_ref
  21.9 18.1 %gather_out.1 = bf16[32,2,64,512]{3,2,1,0:T(8,128)(2,1)} custom-call(s32[32]{0:T(128)} %select_reduce_fusion.1.index_ref, bf16[2,16,64,512]{3,2,1,0:T(8,128)(2,1)} %bitcast.22), custom_call_target="tpu_custom_call" | custom-call | tf_op jit(solution)/shard_map/gather_out/pallas_call | solution.py:287
  40.0 55.6 %all-to-all-done = bf16[128,24,512]{2,1,0:T(8,128)(2,1)S(1)} async-done(((bf16[128,24,512]{2,1,0:T(8,128)(2,1)}), bf16[128,24,512]{2,1,0:T(8,128)(2,1)S(1)}, u32[]{:S(2)}, u32[]{:S(2)}) %all-to-all-start) | async-done | bytes 3145760 | tf_op jit(solution)/shard_map/all_to_all | solution.py:376
  95.7 1.7 copy-done.2
  97.4 5.7 %all-to-all-start.2 = ((bf16[32,2,64,512]{3,2,1,0:T(8,128)(2,1)}), bf16[32,2,64,512]{3,2,1,0:T(8,128)(2,1)}, u32[]{:S(2)}, u32[]{:S(2)}) async-start(bf16[32,2,64,512]{3,2,1,0:T(8,128)(2,1)} %gather_out.1), calls=%async_computation.2 | async-start | bytes 8388608 | tf_op jit(solution)/shard_map/all_to_all | solution.py:390
  103.1 1.6 dynamic-slice_bitcast_fusion.1
  104.7 0.4 collective-permute-start
  105.1 0.2 copy-done.3
  105.5 1.6 collective-permute-start.1
  107.2 0.6 collective-permute-start.2
  107.8 31.4 %collective-permute-done.g1 = bf16[352,2048]{1,0:T(8,128)(2,1)S(1)} collective-permute-done((bf16[352,2048]{1,0:T(8,128)(2,1)S(1)}, bf16[352,2048]{1,0:T(8,128)(2,1)S(1)}, u32[]{:S(2)}, u32[]{:S(2)}) %collective-permute-start) | collective-permute-done | bytes 1441824 | tf_op jit(solution)/shard_map/ppermute | solution.py:369
  139.2 30.9 %collective-permute-done.1.u1 = bf16[352,2048]{1,0:T(8,128)(2,1)S(1)} collective-permute-done((bf16[352,2048]{1,0:T(8,128)(2,1)S(1)}, bf16[352,2048]{1,0:T(8,128)(2,1)S(1)}, u32[]{:S(2)}, u32[]{:S(2)}) %collective-permute-start.1) | collective-permute-done | bytes 1441824 | tf_op jit(solution)/shard_map/ppermute | solution.py:369
  170.1 27.2 %collective-permute-done.2.d1 = bf16[352,2048]{1,0:T(8,128)(2,1)S(1)} collective-permute-done((bf16[352,2048]{1,0:T(8,128)(2,1)S(1)}, bf16[352,2048]{1,0:T(8,128)(2,1)S(1)}, u32[]{:S(2)}, u32[]{:S(2)}) %collective-permute-start.2) | collective-permute-done | bytes 1441824 | tf_op jit(solution)/shard_map/ppermute | solution.py:369
  197.4 3.2 collective-permute-done.5.d2
  200.6 1.1 copy-done.10
  201.7 28.1 %expert.1 = bf16[3072,512]{1,0:T(8,128)(2,1)} custom-call(bf16[3072,512]{1,0:T(8,128)(2,1)} %bitcast.19, bf16[704,2048]{1,0:T(8,128)(2,1)} %bitcast.24, bf16[704,2048]{1,0:T(8,128)(2,1)} %bitcast.25, bf16[704,2048]{1,0:T(8,128)(2,1)} %d0.1, bf16[352,2048]{1,0:T(8,128)(2,1)} %copy-done.5, bf16[352,2048]{1,0:T(8,128)(2,1)} %copy-done.6, ...), custom_call_target="tpu_custom_call" | custom-call | flops 13287555072 | bytes 23592960 | tf_op jit(solution)/shard_map/expert/pallas_call | solution.py:256
  229.8 11.3 %all-to-all-start.1 = ((bf16[128,24,512]{2,1,0:T(8,128)(2,1)}), bf16[128,24,512]{2,1,0:T(8,128)(2,1)S(1)}, u32[]{:S(2)}, u32[]{:S(2)}) async-start(bf16[128,24,512]{2,1,0:T(8,128)(2,1)} %bitcast.21), calls=%async_computation.1 | async-start | bytes 6291456 | tf_op jit(solution)/shard_map/all_to_all | solution.py:380
  241.2 1.0 select_reduce_fusion.index_ref
  242.2 10.1 %gather_in.1 = bf16[2,16,64,512]{3,2,1,0:T(8,128)(2,1)} custom-call(s32[16]{0:T(128)} %select_reduce_fusion.index_ref, bf16[32,2,64,512]{3,2,1,0:T(8,128)(2,1)} %all-to-all-done.2.in_ref), custom_call_target="tpu_custom_call" | custom-call | tf_op jit(solution)/shard_map/gather_in/pallas_call | solution.py:303
  252.3 63.7 %all-to-all-done.1 = bf16[128,24,512]{2,1,0:T(8,128)(2,1)S(1)} async-done(((bf16[128,24,512]{2,1,0:T(8,128)(2,1)}), bf16[128,24,512]{2,1,0:T(8,128)(2,1)S(1)}, u32[]{:S(2)}, u32[]{:S(2)}) %all-to-all-start.1) | async-done | bytes 3145760 | tf_op jit(solution)/shard_map/all_to_all | solution.py:380
  316.0 1.6 copy-done.1
  317.6 8.4 %combine.1 = bf16[64,2048]{1,0:T(8,128)(2,1)} custom-call(bf16[64,256]{1,0:T(8,128)(2,1)} %get-tuple-element.6.slot_ref, bf16[64,256]{1,0:T(8,128)(2,1)} %get-tuple-element.7.whi_ref, bf16[64,256]{1,0:T(8,128)(2,1)} %get-tuple-element.8.wlo_ref, bf16[3072,512]{1,0:T(8,128)(2,1)} %bitcast.18), custom_call_target="tpu_custom_call" | custom-call | tf_op jit(solution)/shard_map/combine/pallas_call | solution.py:148
  (35 shorter events, 0.7 us)
Async XLA Ops:
  0.6 20.4 %copy-start = (s32[8,256]{1,0:T(8,128)S(1)}, s32[8,256]{1,0:T(8,128)}, u32[]{:S(2)}) copy-start(s32[8,256]{1,0:T(8,128)} %param.15) | copy-start | bytes 24580
  6.9 88.8 %all-to-all-start = ((bf16[128,24,512]{2,1,0:T(8,128)(2,1)}), bf16[128,24,512]{2,1,0:T(8,128)(2,1)S(1)}, u32[]{:S(2)}, u32[]{:S(2)}) async-start(bf16[128,24,512]{2,1,0:T(8,128)(2,1)} %bitcast.20), calls=%async_computation | async-start | bytes 6291456 | tf_op jit(solution)/shard_map/all_to_all | solution.py:376
  95.7 1.7 copy-start.2
  97.4 132.4 %all-to-all-start.2 = ((bf16[32,2,64,512]{3,2,1,0:T(8,128)(2,1)}), bf16[32,2,64,512]{3,2,1,0:T(8,128)(2,1)}, u32[]{:S(2)}, u32[]{:S(2)}) async-start(bf16[32,2,64,512]{3,2,1,0:T(8,128)(2,1)} %gather_out.1), calls=%async_computation.2 | async-start | bytes 8388608 | tf_op jit(solution)/shard_map/all_to_all | solution.py:390
  103.1 2.2 copy-start.3
  104.7 2.4 copy-start.4
  104.7 34.5 %collective-permute-start = (bf16[352,2048]{1,0:T(8,128)(2,1)S(1)}, bf16[352,2048]{1,0:T(8,128)(2,1)S(1)}, u32[]{:S(2)}, u32[]{:S(2)}) collective-permute-start(bf16[352,2048]{1,0:T(8,128)(2,1)S(1)} %dynamic-slice_bitcast_fusion.1), channel_id=1, source_target_pairs={{0,2},{2,0},{4,6},{6,4},{8,10},{10,8},{12,14},{14,12},{1,3},{3,1},... | collective-permute-start | bytes 4325384 | tf_op jit(solution)/shard_map/ppermute | solution.py:369
  105.5 64.7 %collective-permute-start.1 = (bf16[352,2048]{1,0:T(8,128)(2,1)S(1)}, bf16[352,2048]{1,0:T(8,128)(2,1)S(1)}, u32[]{:S(2)}, u32[]{:S(2)}) collective-permute-start(bf16[352,2048]{1,0:T(8,128)(2,1)S(1)} %dynamic-slice_bitcast_fusion), channel_id=1, source_target_pairs={{0,2},{2,0},{4,6},{6,4},{8,10},{10,8},{12,14},{14,12},{1,3},{3,1},... | collective-permute-start | bytes 4325384 | tf_op jit(solution)/shard_map/ppermute | solution.py:369
  107.2 90.1 %collective-permute-start.2 = (bf16[352,2048]{1,0:T(8,128)(2,1)S(1)}, bf16[352,2048]{1,0:T(8,128)(2,1)S(1)}, u32[]{:S(2)}, u32[]{:S(2)}) collective-permute-start(bf16[352,2048]{1,0:T(8,128)(2,1)S(1)} %constant_dynamic-slice_fusion.3), channel_id=1, source_target_pairs={{0,2},{2,0},{4,6},{6,4},{8,10},{10,8},{12,14},{14,12},{1,3},{3,1},... | collective-permute-start | bytes 4325384 | tf_op jit(solution)/shard_map/ppermute | solution.py:369
  139.2 58.1 %copy-start.5 = (bf16[352,2048]{1,0:T(8,128)(2,1)}, bf16[352,2048]{1,0:T(8,128)(2,1)S(1)}, u32[]{:S(2)}) copy-start(bf16[352,2048]{1,0:T(8,128)(2,1)S(1)} %collective-permute-done.g1) | copy-start | bytes 4325380
  139.2 58.1 %collective-permute-start.3 = (bf16[352,2048]{1,0:T(8,128)(2,1)S(1)}, bf16[352,2048]{1,0:T(8,128)(2,1)S(1)}, u32[]{:S(2)}, u32[]{:S(2)}) collective-permute-start(bf16[352,2048]{1,0:T(8,128)(2,1)S(1)} %collective-permute-done.g1), channel_id=1, source_target_pairs={{0,1},{1,0},{2,3},{3,2},{4,5},{5,4},{6,7},{7,6},{8,9},{9,8},{10,11... | collective-permute-start | bytes 4325384 | tf_op jit(solution)/shard_map/ppermute | solution.py:371
  170.1 31.6 %copy-start.6 = (bf16[352,2048]{1,0:T(8,128)(2,1)}, bf16[352,2048]{1,0:T(8,128)(2,1)S(1)}, u32[]{:S(2)}) copy-start(bf16[352,2048]{1,0:T(8,128)(2,1)S(1)} %collective-permute-done.1.u1) | copy-start | bytes 4325380
  170.1 27.2 %collective-permute-start.4 = (bf16[352,2048]{1,0:T(8,128)(2,1)S(1)}, bf16[352,2048]{1,0:T(8,128)(2,1)S(1)}, u32[]{:S(2)}, u32[]{:S(2)}) collective-permute-start(bf16[352,2048]{1,0:T(8,128)(2,1)S(1)} %collective-permute-done.1.u1), channel_id=1, source_target_pairs={{0,1},{1,0},{2,3},{3,2},{4,5},{5,4},{6,7},{7,6},{8,9},{9,8},{10,11... | collective-permute-start | bytes 4325384 | tf_op jit(solution)/shard_map/ppermute | solution.py:371
  197.3 4.3 %copy-start.7 = (bf16[352,2048]{1,0:T(8,128)(2,1)}, bf16[352,2048]{1,0:T(8,128)(2,1)S(1)}, u32[]{:S(2)}) copy-start(bf16[352,2048]{1,0:T(8,128)(2,1)S(1)} %collective-permute-done.2.d1) | copy-start | bytes 4325380
  197.3 3.2 collective-permute-start.5
  197.4 3.2 copy-start.8
  197.4 3.2 copy-start.9
  200.6 1.1 copy-start.10
  229.8 86.2 %all-to-all-start.1 = ((bf16[128,24,512]{2,1,0:T(8,128)(2,1)}), bf16[128,24,512]{2,1,0:T(8,128)(2,1)S(1)}, u32[]{:S(2)}, u32[]{:S(2)}) async-start(bf16[128,24,512]{2,1,0:T(8,128)(2,1)} %bitcast.21), calls=%async_computation.1 | async-start | bytes 6291456 | tf_op jit(solution)/shard_map/all_to_all | solution.py:380
  316.0 1.6 copy-start.1

commit v2 on v1

--- a/solution.py
+++ b/solution.py
@@ -7,9 +7,10 @@
 from jax.experimental.pallas import tpu as pltpu
 from jax.sharding import PartitionSpec as P
 
+
 F32 = jnp.float32
 BF16 = jnp.bfloat16
-PARTS = 4
+PARTS = 2
 
 
 def iota(shape, dim):
@@ -25,12 +26,10 @@
 
 
 def pick_mask(subrow, part_lane, slot, rows, chunk):
-    group = divide(subrow, chunk)
-    within = subrow - group * chunk
+    within = subrow - divide(subrow, chunk) * chunk
     part = divide(within, rows)
     row = within - part * rows
-    place = (group & 1) * rows + row
-    return (slot == place.astype(F32)) & (part == part_lane)
+    return (slot == row.astype(F32)) & (part == part_lane)
 
 
 def pack_kernel(rows, ids_ref, w_ref, tok_ref, out_ref, slot_ref, whi_ref, wlo_ref, tok_sc):
@@ -65,7 +64,7 @@
     block = out_ref.shape[0]
     base = step * block
     subrow_e = base + iota((block, experts), 0)
-    spread = (divide(subrow_e, 2 * chunk) == iota((block, experts), 1)).astype(BF16)
+    spread = (divide(subrow_e, chunk) == iota((block, experts), 1)).astype(BF16)
     slot_q = dot(spread, slot_ref[...], ((1,), (0,)))
     subrow = base + iota((block, PARTS * toks), 0)
     lane_part = divide(iota((block, PARTS * toks), 1), toks)
@@ -76,8 +75,8 @@
 def pack(ids_t, w_t, tokens, experts, rows):
     toks, wide = tokens.shape
     chunk = PARTS * rows
-    total = experts * 2 * chunk
-    steps = 8
+    total = experts * chunk
+    steps = 4
     width = wide // PARTS
     whole = lambda i: (0, 0)
     small = jax.ShapeDtypeStruct((experts, PARTS * toks), BF16)
@@ -111,7 +110,7 @@
     chunk = PARTS * rows
     base = step * block
     subrow_e = base + iota((experts, block), 1)
-    spread = (divide(subrow_e, 2 * chunk) == iota((experts, block), 0)).astype(BF16)
+    spread = (divide(subrow_e, chunk) == iota((experts, block), 0)).astype(BF16)
     slot_q = dot(slot_ref[...], spread, ((0,), (0,)))
     high = dot(whi_ref[...], spread, ((0,), (0,)))
     low = dot(wlo_ref[...], spread, ((0,), (0,)))
@@ -140,10 +139,10 @@
 
 def combine(slot, whi, wlo, returned, rows):
 
-    experts, lanes = slot.shape
+    _, lanes = slot.shape
     toks = lanes // PARTS
     total, width = returned.shape
-    steps = 8
+    steps = 4
     whole = lambda i: (0, 0)
     return pl.pallas_call(
         functools.partial(combine_kernel, rows),
@@ -211,7 +210,7 @@
 
     total = wg.shape[0]
     cuts = list(range(0, total, 512)) + [total]
-    mrows = 4 * small
+    mrows = 2 * small
 
     def run(m, _):
         x = xs[pl.ds(m * mrows, mrows), :]
@@ -263,7 +262,7 @@
             pltpu.VMEM((total, wide), BF16),
             pltpu.VMEM((total, wide), BF16),
             pltpu.VMEM((count, wide), BF16),
-            pltpu.VMEM((64 * rows, wide), F32),
+            pltpu.VMEM((32 * rows, wide), F32),
             pltpu.VMEM((big, big), BF16),
             pltpu.SemaphoreType.DMA((9,)),
         ],
@@ -282,7 +281,7 @@
 
 
 def gather_out(index, cache):
-    layers, blk_dev, blk, wide = cache.shape
+    layers, _, blk, wide = cache.shape
     slots = index.shape[0]
     return pl.pallas_call(
         copy_kernel,
@@ -352,37 +351,45 @@
 ):
     tok_dev, wide = tokens.shape
     top_count = route_ids.shape[1]
-    groups = lax.axis_size("pre") * lax.axis_size("tp")
     tp = lax.axis_size("tp")
+    groups = lax.axis_size("pre") * tp
     experts_all = groups // 2
-    most = min(tok_dev, 2 * tok_dev * top_count // experts_all)
-    rows = most // 2
+    rows = min(tok_dev, 2 * tok_dev * top_count // experts_all)
 
     half = down_weight.shape[0]
     quarter = half // 2
-    own = (gate_weight.T, up_weight.T, down_weight)
     core = lax.axis_index("dec")
     swap = [(i, i ^ 1) for i in range(tp)]
     first, second = [], []
+    own = (gate_weight.T, up_weight.T, down_weight)
     for weight in own:
         piece = lax.dynamic_slice_in_dim(weight, core * quarter, quarter, 0)
         got = lax.ppermute(piece, "tp", swap)
         first.append(got)
         second.append(lax.ppermute(got, "dec", [(0, 1), (1, 0)]))
 
-    packed, slot, whi, wlo = pack(route_ids.T, route_weights.T, tokens, experts_all, rows)
+    kinds = [[g for g in range(groups) if (g ^ (g >> 1)) & 1 == kind] for kind in (0, 1)]
     chunk = PARTS * rows
     width = wide // PARTS
-    received = lax.all_to_all(
-        packed.reshape(groups, chunk, width), ("pre", "tp"), split_axis=0, concat_axis=0, tiled=True
-    )
-    result = expert(received.reshape(groups * chunk, width), own, first, second, rows)
-    returned = lax.all_to_all(
-        result.reshape(groups, chunk, width), ("pre", "tp"), split_axis=0, concat_axis=0, tiled=True
-    )
-    moe_output = combine(slot, whi, wlo, returned.reshape(groups * chunk, width), rows)
-
-    layers, _, blk_dev, blk, half_width = prefill_cache.shape
+
+    def exchange(rows_out):
+        moved = lax.all_to_all(
+            rows_out.reshape(experts_all, chunk, width),
+            ("pre", "tp"),
+            split_axis=0,
+            concat_axis=0,
+            axis_index_groups=kinds,
+            tiled=True,
+        )
+        return moved.reshape(experts_all * chunk, width)
+
+    packed, slot, whi, wlo = pack(route_ids.T, route_weights.T, tokens, experts_all, rows)
+    received = exchange(packed)
+    result = expert(received, own, first, second, rows)
+    returned = exchange(result)
+    moe_output = combine(slot, whi, wlo, returned, rows)
+
+    _, _, blk_dev, _, _ = prefill_cache.shape
     sources = lax.axis_size("pre")
     spare = blk_dev // sources + 1
     out_index, in_index = handover_indices(handover_table, sources, blk_dev, spare)

time: 329 us -> 320 us (0.973)
  Pallas kernels: 71.1 us -> 64.8 us
  starting transfers between devices: 33.7 us -> 30 us
    pallas_call x1, Pallas kernels: 8.42 us -> 5.06 us  [combine(): pl.pallas_call(functools.partial(combine_kernel, rows), grid=(steps,), in...]
where the time goes in v2:
time: 320 us; the launch traced here: 319 us
  waiting for transfers between devices  214 us (67%)
  Pallas kernels  64.8 us (20%)
  starting transfers between devices  30 us (9%)
  local copies, waits for them, and re-layouts  7.01 us (2%)
    all_to_all x2, waiting for transfers between devices, exchange(): lax.all_to_all(rows_out.reshape(experts_all, chunk, width), ('pre', 'tp')...  120 us
    ppermute x3, waiting for transfers between devices, shards(): got = lax.ppermute(piece, 'tp', swap)  91.5 us
    pallas_call x1, Pallas kernels, expert(): pl.pallas_call(functools.partial(expert_kernel, rows), in_specs=[vm] + [a...  27.4 us
    all_to_all x2, starting transfers between devices, exchange(): lax.all_to_all(rows_out.reshape(experts_all, chunk, width), ('pre', 'tp')...  22.2 us
    pallas_call x1, Pallas kernels, gather_out(): pl.pallas_call(copy_kernel, grid_spec=pltpu.PrefetchScalarGridSpec(num_sc...  17.8 us
    pallas_call x1, Pallas kernels, gather_in(): pl.pallas_call(copy_kernel, grid_spec=pltpu.PrefetchScalarGridSpec(num_sc...  10.1 us
  transfers between devices with their start and end apart: 9, of which 6 were waited for; matrix products, arithmetic and copies ran while one was open for 1% of the time, Pallas kernels for 17%

profile of v2, /device:TPU:96, one launch (start us, length us, event | category | flops | bytes accessed | tf_op | source)
XLA Modules:
  0.0 318.7 jit_solution(3568266548651385578)
XLA Ops:
  0.6 4.5 %pack.1 = (bf16[1536,1024]{1,0:T(8,128)(2,1)}, bf16[64,128]{1,0:T(8,128)(2,1)}, bf16[64,128]{1,0:T(8,128)(2,1)}, bf16[64,128]{1,0:T(8,128)(2,1)}) custom-call(s32[6,64]{1,0:T(8,128)} %bitcast.26, f32[6,64]{1,0:T(8,128)} %bitcast.27, bf16[64,2048]{1,0:T(8,128)(2,1)} %tok_ref.1), custom_call_target="tpu_custom_call" | custom-call | tf_op jit(solution)/shard_map/pack/pallas_call | solution.py:85
  5.1 13.1 %all-to-all-start = ((bf16[64,24,1024]{2,1,0:T(8,128)(2,1)}), bf16[64,24,1024]{2,1,0:T(8,128)(2,1)S(1)}, u32[]{:S(2)}, u32[]{:S(2)}) async-start(bf16[64,24,1024]{2,1,0:T(8,128)(2,1)} %bitcast.20), calls=%async_computation | async-start | bytes 6291456 | tf_op jit(solution)/shard_map/all_to_all | solution.py:376
  18.6 0.6 select_reduce_fusion.1.index_ref
  19.2 17.8 %gather_out.1 = bf16[32,2,64,512]{3,2,1,0:T(8,128)(2,1)} custom-call(s32[32]{0:T(128)} %select_reduce_fusion.1.index_ref, bf16[2,16,64,512]{3,2,1,0:T(8,128)(2,1)} %bitcast.22), custom_call_target="tpu_custom_call" | custom-call | tf_op jit(solution)/shard_map/gather_out/pallas_call | solution.py:286
  37.0 55.9 %all-to-all-done = bf16[64,24,1024]{2,1,0:T(8,128)(2,1)S(1)} async-done(((bf16[64,24,1024]{2,1,0:T(8,128)(2,1)}), bf16[64,24,1024]{2,1,0:T(8,128)(2,1)S(1)}, u32[]{:S(2)}, u32[]{:S(2)}) %all-to-all-start) | async-done | bytes 3145760 | tf_op jit(solution)/shard_map/all_to_all | solution.py:376
  92.9 1.7 copy-done.2
  94.6 5.5 %all-to-all-start.2 = ((bf16[32,2,64,512]{3,2,1,0:T(8,128)(2,1)}), bf16[32,2,64,512]{3,2,1,0:T(8,128)(2,1)}, u32[]{:S(2)}, u32[]{:S(2)}) async-start(bf16[32,2,64,512]{3,2,1,0:T(8,128)(2,1)} %gather_out.1), calls=%async_computation.2 | async-start | bytes 8388608 | tf_op jit(solution)/shard_map/all_to_all | solution.py:397
  100.1 1.6 dynamic-slice_bitcast_fusion.1
  101.8 0.5 copy-done.3
  102.5 1.6 collective-permute-start.1
  104.1 0.1 constant_dynamic-slice_fusion.3
  104.3 0.6 collective-permute-start.2
  104.9 31.4 %collective-permute-done.g1 = bf16[352,2048]{1,0:T(8,128)(2,1)S(1)} collective-permute-done((bf16[352,2048]{1,0:T(8,128)(2,1)S(1)}, bf16[352,2048]{1,0:T(8,128)(2,1)S(1)}, u32[]{:S(2)}, u32[]{:S(2)}) %collective-permute-start) | collective-permute-done | bytes 1441824 | tf_op jit(solution)/shard_map/ppermute | solution.py:367
  136.3 30.9 %collective-permute-done.1.u1 = bf16[352,2048]{1,0:T(8,128)(2,1)S(1)} collective-permute-done((bf16[352,2048]{1,0:T(8,128)(2,1)S(1)}, bf16[352,2048]{1,0:T(8,128)(2,1)S(1)}, u32[]{:S(2)}, u32[]{:S(2)}) %collective-permute-start.1) | collective-permute-done | bytes 1441824 | tf_op jit(solution)/shard_map/ppermute | solution.py:367
  167.2 29.2 %collective-permute-done.2.d1 = bf16[352,2048]{1,0:T(8,128)(2,1)S(1)} collective-permute-done((bf16[352,2048]{1,0:T(8,128)(2,1)S(1)}, bf16[352,2048]{1,0:T(8,128)(2,1)S(1)}, u32[]{:S(2)}, u32[]{:S(2)}) %collective-permute-start.2) | collective-permute-done | bytes 1441824 | tf_op jit(solution)/shard_map/ppermute | solution.py:367
  196.4 3.2 collective-permute-done.5.d2
  199.6 1.1 copy-done.10
  200.7 27.4 %expert.1 = bf16[1536,1024]{1,0:T(8,128)(2,1)} custom-call(bf16[1536,1024]{1,0:T(8,128)(2,1)} %bitcast.19, bf16[704,2048]{1,0:T(8,128)(2,1)} %bitcast.24, bf16[704,2048]{1,0:T(8,128)(2,1)} %bitcast.25, bf16[704,2048]{1,0:T(8,128)(2,1)} %d0.1, bf16[352,2048]{1,0:T(8,128)(2,1)} %copy-done.5, bf16[352,2048]{1,0:T(8,128)(2,1)} %copy-done.6, ...), custom_call_target="tpu_custom_call" | custom-call | flops 13287555072 | bytes 23592960 | tf_op jit(solution)/shard_map/expert/pallas_call | solution.py:255
  228.1 9.0 %all-to-all-start.1 = ((bf16[64,24,1024]{2,1,0:T(8,128)(2,1)}), bf16[64,24,1024]{2,1,0:T(8,128)(2,1)S(1)}, u32[]{:S(2)}, u32[]{:S(2)}) async-start(bf16[64,24,1024]{2,1,0:T(8,128)(2,1)} %bitcast.21), calls=%async_computation.1 | async-start | bytes 6291456 | tf_op jit(solution)/shard_map/all_to_all | solution.py:376
  237.2 1.0 select_reduce_fusion.index_ref
  238.2 10.1 %gather_in.1 = bf16[2,16,64,512]{3,2,1,0:T(8,128)(2,1)} custom-call(s32[16]{0:T(128)} %select_reduce_fusion.index_ref, bf16[32,2,64,512]{3,2,1,0:T(8,128)(2,1)} %all-to-all-done.2.in_ref), custom_call_target="tpu_custom_call" | custom-call | tf_op jit(solution)/shard_map/gather_in/pallas_call | solution.py:302
  248.3 63.7 %all-to-all-done.1 = bf16[64,24,1024]{2,1,0:T(8,128)(2,1)S(1)} async-done(((bf16[64,24,1024]{2,1,0:T(8,128)(2,1)}), bf16[64,24,1024]{2,1,0:T(8,128)(2,1)S(1)}, u32[]{:S(2)}, u32[]{:S(2)}) %all-to-all-start.1) | async-done | bytes 3145760 | tf_op jit(solution)/shard_map/all_to_all | solution.py:376
  312.0 1.6 copy-done.1
  313.6 5.1 %combine.1 = bf16[64,2048]{1,0:T(8,128)(2,1)} custom-call(bf16[64,128]{1,0:T(8,128)(2,1)} %get-tuple-element.6.slot_ref, bf16[64,128]{1,0:T(8,128)(2,1)} %get-tuple-element.7.whi_ref, bf16[64,128]{1,0:T(8,128)(2,1)} %get-tuple-element.8.wlo_ref, bf16[1536,1024]{1,0:T(8,128)(2,1)} %bitcast.18), custom_call_target="tpu_custom_call" | custom-call | tf_op jit(solution)/shard_map/combine/pallas_call | solution.py:147
  (35 shorter events, 0.6 us)
Async XLA Ops:
  0.6 17.7 %copy-start = (s32[8,256]{1,0:T(8,128)S(1)}, s32[8,256]{1,0:T(8,128)}, u32[]{:S(2)}) copy-start(s32[8,256]{1,0:T(8,128)} %param.15) | copy-start | bytes 24580
  5.1 87.7 %all-to-all-start = ((bf16[64,24,1024]{2,1,0:T(8,128)(2,1)}), bf16[64,24,1024]{2,1,0:T(8,128)(2,1)S(1)}, u32[]{:S(2)}, u32[]{:S(2)}) async-start(bf16[64,24,1024]{2,1,0:T(8,128)(2,1)} %bitcast.20), calls=%async_computation | async-start | bytes 6291456 | tf_op jit(solution)/shard_map/all_to_all | solution.py:376
  92.9 1.7 copy-start.2
  94.6 133.5 %all-to-all-start.2 = ((bf16[32,2,64,512]{3,2,1,0:T(8,128)(2,1)}), bf16[32,2,64,512]{3,2,1,0:T(8,128)(2,1)}, u32[]{:S(2)}, u32[]{:S(2)}) async-start(bf16[32,2,64,512]{3,2,1,0:T(8,128)(2,1)} %gather_out.1), calls=%async_computation.2 | async-start | bytes 8388608 | tf_op jit(solution)/shard_map/all_to_all | solution.py:397
  100.1 2.2 copy-start.3
  101.7 2.4 copy-start.4
  101.7 34.5 %collective-permute-start = (bf16[352,2048]{1,0:T(8,128)(2,1)S(1)}, bf16[352,2048]{1,0:T(8,128)(2,1)S(1)}, u32[]{:S(2)}, u32[]{:S(2)}) collective-permute-start(bf16[352,2048]{1,0:T(8,128)(2,1)S(1)} %dynamic-slice_bitcast_fusion.1), channel_id=1, source_target_pairs={{0,2},{2,0},{4,6},{6,4},{8,10},{10,8},{12,14},{14,12},{1,3},{3,1},... | collective-permute-start | bytes 4325384 | tf_op jit(solution)/shard_map/ppermute | solution.py:367
  102.5 64.7 %collective-permute-start.1 = (bf16[352,2048]{1,0:T(8,128)(2,1)S(1)}, bf16[352,2048]{1,0:T(8,128)(2,1)S(1)}, u32[]{:S(2)}, u32[]{:S(2)}) collective-permute-start(bf16[352,2048]{1,0:T(8,128)(2,1)S(1)} %dynamic-slice_bitcast_fusion), channel_id=1, source_target_pairs={{0,2},{2,0},{4,6},{6,4},{8,10},{10,8},{12,14},{14,12},{1,3},{3,1},... | collective-permute-start | bytes 4325384 | tf_op jit(solution)/shard_map/ppermute | solution.py:367
  104.3 92.1 %collective-permute-start.2 = (bf16[352,2048]{1,0:T(8,128)(2,1)S(1)}, bf16[352,2048]{1,0:T(8,128)(2,1)S(1)}, u32[]{:S(2)}, u32[]{:S(2)}) collective-permute-start(bf16[352,2048]{1,0:T(8,128)(2,1)S(1)} %constant_dynamic-slice_fusion.3), channel_id=1, source_target_pairs={{0,2},{2,0},{4,6},{6,4},{8,10},{10,8},{12,14},{14,12},{1,3},{3,1},... | collective-permute-start | bytes 4325384 | tf_op jit(solution)/shard_map/ppermute | solution.py:367
  136.3 60.1 %copy-start.5 = (bf16[352,2048]{1,0:T(8,128)(2,1)}, bf16[352,2048]{1,0:T(8,128)(2,1)S(1)}, u32[]{:S(2)}) copy-start(bf16[352,2048]{1,0:T(8,128)(2,1)S(1)} %collective-permute-done.g1) | copy-start | bytes 4325380
  136.3 60.1 %collective-permute-start.3 = (bf16[352,2048]{1,0:T(8,128)(2,1)S(1)}, bf16[352,2048]{1,0:T(8,128)(2,1)S(1)}, u32[]{:S(2)}, u32[]{:S(2)}) collective-permute-start(bf16[352,2048]{1,0:T(8,128)(2,1)S(1)} %collective-permute-done.g1), channel_id=1, source_target_pairs={{0,1},{1,0},{2,3},{3,2},{4,5},{5,4},{6,7},{7,6},{8,9},{9,8},{10,11... | collective-permute-start | bytes 4325384 | tf_op jit(solution)/shard_map/ppermute | solution.py:369
  167.2 33.5 %copy-start.6 = (bf16[352,2048]{1,0:T(8,128)(2,1)}, bf16[352,2048]{1,0:T(8,128)(2,1)S(1)}, u32[]{:S(2)}) copy-start(bf16[352,2048]{1,0:T(8,128)(2,1)S(1)} %collective-permute-done.1.u1) | copy-start | bytes 4325380
  167.2 29.2 %collective-permute-start.4 = (bf16[352,2048]{1,0:T(8,128)(2,1)S(1)}, bf16[352,2048]{1,0:T(8,128)(2,1)S(1)}, u32[]{:S(2)}, u32[]{:S(2)}) collective-permute-start(bf16[352,2048]{1,0:T(8,128)(2,1)S(1)} %collective-permute-done.1.u1), channel_id=1, source_target_pairs={{0,1},{1,0},{2,3},{3,2},{4,5},{5,4},{6,7},{7,6},{8,9},{9,8},{10,11... | collective-permute-start | bytes 4325384 | tf_op jit(solution)/shard_map/ppermute | solution.py:369
  196.4 4.3 %copy-start.7 = (bf16[352,2048]{1,0:T(8,128)(2,1)}, bf16[352,2048]{1,0:T(8,128)(2,1)S(1)}, u32[]{:S(2)}) copy-start(bf16[352,2048]{1,0:T(8,128)(2,1)S(1)} %collective-permute-done.2.d1) | copy-start | bytes 4325380
  196.4 3.2 %collective-permute-start.5 = (bf16[352,2048]{1,0:T(8,128)(2,1)S(1)}, bf16[352,2048]{1,0:T(8,128)(2,1)S(1)}, u32[]{:S(2)}, u32[]{:S(2)}) collective-permute-start(bf16[352,2048]{1,0:T(8,128)(2,1)S(1)} %collective-permute-done.2.d1), channel_id=1, source_target_pairs={{0,1},{1,0},{2,3},{3,2},{4,5},{5,4},{6,7},{7,6},{8,9},{9,8},{10,11... | collective-permute-start | bytes 4325384 | tf_op jit(solution)/shard_map/ppermute | solution.py:369
  196.4 3.2 %copy-start.8 = (bf16[352,2048]{1,0:T(8,128)(2,1)}, bf16[352,2048]{1,0:T(8,128)(2,1)S(1)}, u32[]{:S(2)}) copy-start(bf16[352,2048]{1,0:T(8,128)(2,1)S(1)} %collective-permute-done.3.g2) | copy-start | bytes 4325380
  196.4 3.2 %copy-start.9 = (bf16[352,2048]{1,0:T(8,128)(2,1)}, bf16[352,2048]{1,0:T(8,128)(2,1)S(1)}, u32[]{:S(2)}) copy-start(bf16[352,2048]{1,0:T(8,128)(2,1)S(1)} %collective-permute-done.4.u2) | copy-start | bytes 4325380
  199.6 1.1 copy-start.10
  228.1 83.9 %all-to-all-start.1 = ((bf16[64,24,1024]{2,1,0:T(8,128)(2,1)}), bf16[64,24,1024]{2,1,0:T(8,128)(2,1)S(1)}, u32[]{:S(2)}, u32[]{:S(2)}) async-start(bf16[64,24,1024]{2,1,0:T(8,128)(2,1)} %bitcast.21), calls=%async_computation.1 | async-start | bytes 6291456 | tf_op jit(solution)/shard_map/all_to_all | solution.py:376
  312.0 1.6 copy-start.1

commit v3 on v2

v3 whole, which is shorter than its diff:
```python
import functools

import jax
import jax.numpy as jnp
from jax import lax
from jax.experimental import pallas as pl
from jax.experimental.pallas import tpu as pltpu
from jax.sharding import PartitionSpec as P


F32 = jnp.float32
BF16 = jnp.bfloat16
TOP = 6
ZS = 8
PEERS = 8
OFFSETS = (0, 1, 2, 3, 4, -1, -2, -3)


def iota(shape, dim):
    return lax.broadcasted_iota(jnp.int32, shape, dim)


def divide(x, by):
    return ((x.astype(F32) + 0.5) * (1.0 / by)).astype(jnp.int32)


def dot(a, b, contract):
    return lax.dot_general(a, b, (contract, ((), ())), preferred_element_type=F32)


def pick_mask(subrow, part_lane, slot, rows, chunk):
    within = subrow - divide(subrow, chunk) * chunk
    part = divide(within, rows)
    row = within - part * rows
    return (slot == row.astype(F32)) & (part == part_lane)


def pack_kernel(rows, parts, place_ref, *refs):
    blocks = refs[:ZS]
    outs = refs[ZS:]
    toks = blocks[0].shape[0]
    width = outs[0].shape[2]
    wide = width * parts
    chunk = parts * rows
    experts = toks
    me, z = place_ref[0], place_ref[1]
    peers = len(outs)

    def expert_of(index):
        peer = divide(index, chunk) ^ me
        return (peer >> 2) * 32 + z * 4 + (peer & 3)

    total = peers * chunk
    spread = (expert_of(iota((total, experts), 0)) == iota((total, experts), 1)).astype(BF16)
    earlier = (iota((toks, toks), 1) < iota((toks, toks), 0)).astype(BF16)
    index = iota((total, parts * toks), 0)
    lane_part = divide(iota((total, parts * toks), 1), toks)
    eids = iota((toks, experts), 1).astype(F32)
    for o, block in enumerate(blocks):
        ids = block[:, wide : wide + 128].astype(F32)
        named = jnp.zeros((toks, experts), F32)
        for k in range(TOP):
            named = named + jnp.where(ids[:, k : k + 1] == eids, 1.0, 0.0)
        rank = dot(earlier, named.astype(BF16), ((1,), (0,)))
        slot = jnp.where(named > 0.5, rank, 255.0).astype(BF16)
        slot = jnp.concatenate([slot] * parts, axis=0)
        slot_q = dot(spread, slot, ((1,), (1,)))
        mask = pick_mask(index, lane_part, slot_q, rows, chunk)
        source = jnp.concatenate(
            [block[:, p * width : (p + 1) * width] for p in range(parts)], axis=0
        )
        y = dot(mask.astype(BF16), source, ((1,), (0,)))
        for m, out in enumerate(outs):
            out[o] = y[m * chunk : (m + 1) * chunk, :].astype(BF16)


def pack(place, blocks, wide, rows, parts):
    shape = jax.ShapeDtypeStruct((ZS, parts * rows, wide // parts), BF16)
    vm = pl.BlockSpec(memory_space=pltpu.VMEM)
    return pl.pallas_call(
        functools.partial(pack_kernel, rows, parts),
        in_specs=[pl.BlockSpec(memory_space=pltpu.SMEM)] + [vm] * ZS,
        out_specs=[vm] * PEERS,
        out_shape=[shape] * PEERS,
        name="pack",
    )(place, *blocks)


def combine_kernel(rows, parts, ids_ref, w_ref, ret_ref, out_ref, slot_ref, whi_ref, wlo_ref, acc):
    step = pl.program_id(0)
    count, toks = ids_ref.shape
    experts, lanes = slot_ref.shape
    block, width = ret_ref.shape
    chunk = parts * rows

    @pl.when(step == 0)
    def _():
        eids = iota((experts, toks), 0)
        named = jnp.zeros((experts, toks), F32)
        weight = jnp.zeros((experts, toks), F32)
        for k in range(count):
            hit = ids_ref[k : k + 1, :] == eids
            named = named + jnp.where(hit, 1.0, 0.0)
            weight = weight + jnp.where(hit, w_ref[k : k + 1, :], 0.0)
        earlier = (iota((toks, toks), 0) < iota((toks, toks), 1)).astype(BF16)
        rank = dot(named.astype(BF16), earlier, ((1,), (0,)))
        slot = jnp.where(named > 0.5, rank, 255.0).astype(BF16)
        high = weight.astype(BF16)
        low = (weight - high.astype(F32)).astype(BF16)
        for p in range(parts):
            slot_ref[:, p * toks : (p + 1) * toks] = slot
            whi_ref[:, p * toks : (p + 1) * toks] = high
            wlo_ref[:, p * toks : (p + 1) * toks] = low

    base = step * block
    subrow_e = base + iota((experts, block), 1)
    spread = (divide(subrow_e, chunk) == iota((experts, block), 0)).astype(BF16)
    slot_q = dot(slot_ref[...], spread, ((0,), (0,)))
    high = dot(whi_ref[...], spread, ((0,), (0,)))
    low = dot(wlo_ref[...], spread, ((0,), (0,)))
    subrow = base + iota((lanes, block), 1)
    lane_part = divide(iota((lanes, block), 0), toks)
    mask = pick_mask(subrow, lane_part, slot_q, rows, chunk)
    left = jnp.concatenate(
        [jnp.where(mask, high, 0.0).astype(BF16), jnp.where(mask, low, 0.0).astype(BF16)], axis=0
    )
    both = dot(left, ret_ref[...], ((1,), (0,)))
    part = both[:lanes] + both[lanes:]

    @pl.when(step == 0)
    def _():
        acc[...] = part

    @pl.when(step > 0)
    def _():
        acc[...] = acc[...] + part

    @pl.when(step == pl.num_programs(0) - 1)
    def _():
        for p in range(parts):
            out_ref[:, p * width : (p + 1) * width] = acc[p * toks : (p + 1) * toks, :].astype(BF16)


def combine(ids_t, w_t, returned, experts, rows, parts):
    toks = ids_t.shape[1]
    lanes = parts * toks
    total, width = returned.shape
    steps = 4
    whole = lambda i: (0, 0)
    return pl.pallas_call(
        functools.partial(combine_kernel, rows, parts),
        grid=(steps,),
        in_specs=[
            pl.BlockSpec(ids_t.shape, whole),
            pl.BlockSpec(w_t.shape, whole),
            pl.BlockSpec((total // steps, width), lambda i: (i, 0)),
        ],
        out_specs=pl.BlockSpec((toks, parts * width), whole),
        out_shape=jax.ShapeDtypeStruct((toks, parts * width), BF16),
        scratch_shapes=[pltpu.VMEM((experts, lanes), BF16)] * 3 + [pltpu.VMEM((lanes, width), F32)],
        name="combine",
    )(ids_t, w_t, returned)


def permutation(size, items, parts, rows):
    small = items * rows
    index = iota((size, size), 0)
    part = divide(index, small)
    rest = index - part * small
    item = divide(rest, rows)
    row = rest - item * rows
    return (item * (parts * rows) + part * rows + row == iota((size, size), 1)).astype(BF16)


def expert_kernel(rows, parts, back, place_ref, *refs):
    xin = refs[:PEERS]
    g0, u0, d0, g1, u1, d1, g2, u2, d2 = refs[PEERS : PEERS + 9]
    o_ref, wg, wu, wd, xs, acc, perm, perm_back, sems = refs[PEERS + 9 :]
    half = g0.shape[0]
    quarter = g1.shape[0]
    copies = []
    for i, (src, dst, start) in enumerate(
        [
            (g0, wg, 0),
            (u0, wu, 0),
            (d0, wd, 0),
            (g1, wg, half),
            (u1, wu, half),
            (g2, wg, half + quarter),
            (u2, wu, half + quarter),
            (d1, wd, half),
            (d2, wd, half + quarter),
        ]
    ):
        copy = pltpu.make_async_copy(src, dst.at[pl.ds(start, src.shape[0])], sems.at[i])
        copy.start()
        copies.append(copy)

    small = ZS * rows
    wide = xs.shape[1]
    width = wide // parts
    perm[...] = permutation(parts * small, ZS, parts, rows)
    perm_back[...] = permutation(back * small, ZS, back, rows)
    for m in range(PEERS):
        y = dot(perm[...], xin[m][...], ((1,), (0,))).astype(BF16)
        for p in range(parts):
            xs[m * small : (m + 1) * small, p * width : (p + 1) * width] = y[
                p * small : (p + 1) * small, :
            ]
    for copy in copies:
        copy.wait()

    total = wg.shape[0]
    cuts = list(range(0, total, 512)) + [total]
    mrows = acc.shape[0]

    def run(m, _):
        x = xs[pl.ds(m * mrows, mrows), :]
        for c in range(len(cuts) - 1):
            lo, hi = cuts[c], cuts[c + 1]
            gate = dot(x, wg[lo:hi, :], ((1,), (1,)))
            upper = dot(x, wu[lo:hi, :], ((1,), (1,)))
            hidden = (gate / (1.0 + jnp.exp(-gate)) * upper).astype(BF16)
            res = dot(hidden, wd[lo:hi, :], ((1,), (0,)))
            if c == 0:
                acc[...] = res
            elif c < len(cuts) - 2:
                acc[...] = acc[...] + res
            else:
                xs[pl.ds(m * mrows, mrows), :] = (acc[...] + res).astype(BF16)
        return 0

    lax.fori_loop(0, xs.shape[0] // mrows, run, 0)

    me, z = place_ref[0], place_ref[1]
    width = wide // back
    chunk = back * rows
    for m in range(PEERS):
        y = jnp.concatenate(
            [
                xs[m * small : (m + 1) * small, p * width : (p + 1) * width]
                for p in range(back)
            ],
            axis=0,
        )
        y = dot(perm_back[...], y, ((0,), (0,)))
        peer = me ^ m
        for o in range(ZS):
            home = (peer >> 2) * 32 + ((z - OFFSETS[o]) & (ZS - 1)) * 4 + (peer & 3)
            o_ref[home] = y[o * chunk : (o + 1) * chunk, :].astype(BF16)


def expert(place, x, own, first, second, rows, parts, back):
    half, wide = own[0].shape
    total = 2 * half
    count = PEERS * ZS * rows
    anyspec = pl.BlockSpec(memory_space=pl.ANY)
    vm = pl.BlockSpec(memory_space=pltpu.VMEM)
    return pl.pallas_call(
        functools.partial(expert_kernel, rows, parts, back),
        in_specs=[pl.BlockSpec(memory_space=pltpu.SMEM)] + [vm] * PEERS + [anyspec] * 9,
        out_specs=vm,
        out_shape=jax.ShapeDtypeStruct((PEERS * ZS, back * rows, wide // back), BF16),
        scratch_shapes=[
            pltpu.VMEM((total, wide), BF16),
            pltpu.VMEM((total, wide), BF16),
            pltpu.VMEM((total, wide), BF16),
            pltpu.VMEM((count, wide), BF16),
            pltpu.VMEM((count // 2, wide), F32),
            pltpu.VMEM((parts * ZS * rows, parts * ZS * rows), BF16),
            pltpu.VMEM((back * ZS * rows, back * ZS * rows), BF16),
            pltpu.SemaphoreType.DMA((9,)),
        ],
        compiler_params=pltpu.CompilerParams(vmem_limit_bytes=60 * 1024 * 1024),
        cost_estimate=pl.CostEstimate(
            flops=6 * count * total * wide,
            bytes_accessed=6 * total * wide + 4 * count * wide,
            transcendentals=count * total,
        ),
        name="expert",
    )(place, *x, *own, *first, *second)


def out_kernel(index_ref, in_ref, out_ref):
    def one(i, _):
        out_ref[i] = in_ref[:, index_ref[i]]
        return 0

    lax.fori_loop(0, out_ref.shape[0], one, 0)


def gather_out(index, cache):
    layers, _, blk, wide = cache.shape
    slots = index.shape[0]
    vm = pl.BlockSpec(memory_space=pltpu.VMEM)
    return pl.pallas_call(
        out_kernel,
        in_specs=[pl.BlockSpec(memory_space=pltpu.SMEM), vm],
        out_specs=vm,
        out_shape=jax.ShapeDtypeStruct((slots, layers, blk, wide), cache.dtype),
        name="gather_out",
    )(index, cache)


def in_kernel(index_ref, in_ref, out_ref):
    def one(i, _):
        out_ref[:, i] = in_ref[index_ref[i]]
        return 0

    lax.fori_loop(0, out_ref.shape[1], one, 0)


def gather_in(index, arrived):
    slots = index.shape[0]
    _, layers, blk, wide = arrived.shape
    vm = pl.BlockSpec(memory_space=pltpu.VMEM)
    return pl.pallas_call(
        in_kernel,
        in_specs=[pl.BlockSpec(memory_space=pltpu.SMEM), vm],
        out_specs=vm,
        out_shape=jax.ShapeDtypeStruct((layers, slots, blk, wide), arrived.dtype),
        name="gather_in",
    )(index, arrived)


def handover_indices(handover_table, sources, blk_dev, spare):
    column = lax.dynamic_index_in_dim(handover_table, lax.axis_index("tp"), 0, keepdims=False)
    here = lax.axis_index("pre")
    table = column.reshape(sources, blk_dev)
    dest = table // blk_dev
    earlier = jnp.arange(blk_dev)[:, None] < jnp.arange(blk_dev)[None, :]
    same = dest[:, :, None] == dest[:, None, :]
    rank = jnp.sum((same & earlier[None]).astype(jnp.int32), axis=1)
    my_dest = lax.dynamic_index_in_dim(dest, here, 0, keepdims=False)
    my_rank = lax.dynamic_index_in_dim(rank, here, 0, keepdims=False)
    wanted = jnp.arange(sources * spare, dtype=jnp.int32)
    out_index = jnp.sum(
        jnp.where(
            wanted[:, None] == (my_dest * spare + my_rank)[None, :],
            jnp.arange(blk_dev, dtype=jnp.int32)[None, :],
            0,
        ),
        axis=1,
    )
    place = here * blk_dev + jnp.arange(blk_dev, dtype=jnp.int32)
    came = jnp.arange(sources, dtype=jnp.int32)[:, None] * spare + rank
    in_index = jnp.sum(
        jnp.where(place[:, None, None] == table[None], came[None], 0), axis=(1, 2)
    )
    return out_index, in_index


def shards(
    tokens,
    route_ids,
    route_weights,
    gate_weight,
    up_weight,
    down_weight,
    prefill_cache,
    handover_table,
):
    tok_dev, wide = tokens.shape
    top_count = route_ids.shape[1]
    tp = lax.axis_size("tp")
    groups = lax.axis_size("pre") * tp
    experts_all = groups // 2
    rows = min(tok_dev, 2 * tok_dev * top_count // experts_all)

    half = down_weight.shape[0]
    quarter = half // 2
    core = lax.axis_index("dec")
    swap = [(i, i ^ 1) for i in range(tp)]
    first, second = [], []
    own = (gate_weight.T, up_weight.T, down_weight)
    for weight in own:
        piece = lax.dynamic_slice_in_dim(weight, core * quarter, quarter, 0)
        got = lax.ppermute(piece, "tp", swap)
        first.append(got)
        second.append(lax.ppermute(got, "dec", [(0, 1), (1, 0)]))

    pre = lax.axis_size("pre")
    lanes = jnp.pad(route_ids.astype(BF16), ((0, 0), (0, 128 - top_count)))
    block = jnp.concatenate([tokens, lanes], axis=1)
    up = [(i, i // ZS * ZS + (i + 1) % ZS) for i in range(pre)]
    down = [(j, i) for i, j in up]
    forward, backward = [block], [block]
    for n in range(4):
        forward.append(lax.ppermute(forward[-1], "pre", up))
        if n < 3:
            backward.append(lax.ppermute(backward[-1], "pre", down))
    blocks = forward + backward[1:]

    here = lax.axis_index("pre")
    there = lax.axis_index("tp")
    me = (here // ZS) * 4 + there // 2
    place = jnp.stack([me, here % ZS]).astype(jnp.int32)
    parts, back = 4, 2
    packed = pack(place, blocks, wide, rows, parts)

    def peer_of(group, flip):
        p, t = group // tp, group % tp
        kind = (t ^ (t >> 1)) & 1
        peer = ((p // ZS) * 4 + t // 2) ^ flip
        high = peer & 1
        return ((peer >> 2) * ZS + p % ZS) * tp + ((peer >> 1) & 1) * 4 + high * 2 + (high ^ kind)

    came = [packed[0]]
    for m in range(1, PEERS):
        came.append(
            lax.ppermute(packed[m], ("pre", "tp"), [(g, peer_of(g, m)) for g in range(groups)])
        )
    came = [c.reshape(-1, wide // parts) for c in came]
    result = expert(place, came, own, first, second, rows, parts, back)

    kinds = [[g for g in range(groups) if (g ^ (g >> 1)) & 1 == kind] for kind in (0, 1)]
    returned = lax.all_to_all(
        result, ("pre", "tp"), split_axis=0, concat_axis=0, axis_index_groups=kinds, tiled=True
    )
    moe_output = combine(
        route_ids.T, route_weights.T, returned.reshape(-1, wide // back), experts_all, rows, back
    )

    _, _, blk_dev, _, _ = prefill_cache.shape
    sources = lax.axis_size("pre")
    spare = blk_dev // sources + 1
    out_index, in_index = handover_indices(handover_table, sources, blk_dev, spare)
    leaving = gather_out(out_index, prefill_cache[:, 0])
    arrived = lax.all_to_all(leaving, "pre", split_axis=0, concat_axis=0, tiled=True)
    decode_cache = gather_in(in_index, arrived)[:, None]
    return (moe_output, decode_cache)


def solution(mesh):
    return jax.shard_map(
        shards,
        mesh=mesh,
        in_specs=(
            P(("pre", "tp", "dec"), None),
            P(("pre", "tp", "dec"), None),
            P(("pre", "tp", "dec"), None),
            P(None, ("pre", "tp")),
            P(None, ("pre", "tp")),
            P(("pre", "tp"), None),
            P(None, "tp", "pre", None, "dec"),
            P(),
        ),
        out_specs=(P(("pre", "tp", "dec"), None), P(None, "tp", "pre", None, "dec")),
        check_vma=False,
    )
```

time: 320 us -> 322 us (level)
  starting transfers between devices: 30 us -> 56.6 us
  Pallas kernels: 64.8 us -> 45.6 us
  waiting for transfers between devices: 214 us -> 208 us
    ppermute x0 -> x14, waiting for transfers between devices: none -> 140 us  [the longest x4 103 us: shards(): forward.append(lax.ppermute(forward[-1], 'pre', up))]
    ppermute x3, waiting for transfers between devices: 91.5 us -> 0.01 us  [shards(): got = lax.ppermute(piece, 'tp', swap)]
    all_to_all x2 -> x1, waiting for transfers between devices: 120 us -> 68.4 us  [shards(): lax.all_to_all(result, ('pre', 'tp'), split_axis=0, concat_axis=0, axis_i...]
    ppermute x0 -> x14, starting transfers between devices: none -> 31.7 us  [the longest x7 19.8 us: shards(): lax.ppermute(packed[m], ('pre', 'tp'), [(g, peer_of(g, m)) for g in range...]
    pallas_call x5, Pallas kernels: 64.8 us -> 45.6 us  [the longest x1 25.9 us: expert(): pl.pallas_call(functools.partial(expert_kernel, rows, parts, back), in_sp...]
    all_to_all x2 -> x1, starting transfers between devices: 22.2 us -> 11.5 us  [shards(): lax.all_to_all(result, ('pre', 'tp'), split_axis=0, concat_axis=0, axis_i...]
    all_to_all x1, starting transfers between devices: 5.51 us -> 8.87 us  [shards(): lax.all_to_all(leaving, 'pre', split_axis=0, concat_axis=0, tiled=True)]
  transfers between devices with their start and end apart: 9 -> 22, of which waited for: 6 -> 15; matrix products, arithmetic and copies ran while one was open for 1% -> 1% of each run, Pallas kernels for 17% -> 11%
where the time goes in v3:
time: 322 us; the launch traced here: 321 us
  waiting for transfers between devices  208 us (65%)
  starting transfers between devices  56.6 us (18%)
  Pallas kernels  45.6 us (14%)
  local copies, waits for them, and re-layouts  7 us (2%)
    ppermute x4, waiting for transfers between devices, shards(): forward.append(lax.ppermute(forward[-1], 'pre', up))  103 us
    all_to_all x1, waiting for transfers between devices, shards(): lax.all_to_all(result, ('pre', 'tp'), split_axis=0, concat_axis=0, axis_i...  68.4 us
    ppermute x7, waiting for transfers between devices, shards(): lax.ppermute(packed[m], ('pre', 'tp'), [(g, peer_of(g, m)) for g in range...  35.4 us
    pallas_call x1, Pallas kernels, expert(): pl.pallas_call(functools.partial(expert_kernel, rows, parts, back), in_sp...  25.9 us
    ppermute x7, starting transfers between devices, shards(): lax.ppermute(packed[m], ('pre', 'tp'), [(g, peer_of(g, m)) for g in range...  19.8 us
    ppermute x4, starting transfers between devices, shards(): forward.append(lax.ppermute(forward[-1], 'pre', up))  11.8 us
    all_to_all x1, starting transfers between devices, shards(): lax.all_to_all(result, ('pre', 'tp'), split_axis=0, concat_axis=0, axis_i...  11.5 us
    all_to_all x1, starting transfers between devices, shards(): lax.all_to_all(leaving, 'pre', split_axis=0, concat_axis=0, tiled=True)  8.87 us
  transfers between devices with their start and end apart: 22, of which 15 were waited for; matrix products, arithmetic and copies ran while one was open for 1% of the time, Pallas kernels for 11%

profile of v3, /device:TPU:96, one launch (start us, length us, event | category | flops | bytes accessed | tf_op | source)
XLA Modules:
  0.0 320.8 jit_solution(17056563222750651588)
XLA Ops:
  2.2 4.0 %gather_out.1 = bf16[32,2,64,512]{3,2,1,0:T(8,128)(2,1)} custom-call(s32[32]{0:T(128)} %select_reduce_fusion.1.index_ref, bf16[2,16,64,512]{3,2,1,0:T(8,128)(2,1)} %bitcast.26), custom_call_target="tpu_custom_call" | custom-call | tf_op jit(solution)/shard_map/gather_out/pallas_call | solution.py:296
  6.2 8.9 %all-to-all-start.1 = ((bf16[32,2,64,512]{3,2,1,0:T(8,128)(2,1)}), bf16[32,2,64,512]{3,2,1,0:T(8,128)(2,1)}, u32[]{:S(2)}, u32[]{:S(2)}) async-start(bf16[32,2,64,512]{3,2,1,0:T(8,128)(2,1)} %gather_out.1), calls=%async_computation.1 | async-start | bytes 8388608 | tf_op jit(solution)/shard_map/all_to_all | solution.py:429
  21.9 2.8 collective-permute-start
  24.6 88.8 %collective-permute-done.refs_1_ = bf16[64,2176]{1,0:T(8,128)(2,1)S(1)} collective-permute-done((bf16[64,2176]{1,0:T(8,128)(2,1)S(1)}, bf16[64,2176]{1,0:T(8,128)(2,1)S(1)}, u32[]{:S(2)}, u32[]{:S(2)}) %collective-permute-start) | collective-permute-done | bytes 278560 | tf_op jit(solution)/shard_map/ppermute | solution.py:389
  115.8 6.2 %collective-permute-done.1.refs_2_ = bf16[64,2176]{1,0:T(8,128)(2,1)S(1)} collective-permute-done((bf16[64,2176]{1,0:T(8,128)(2,1)S(1)}, bf16[64,2176]{1,0:T(8,128)(2,1)S(1)}, u32[]{:S(2)}, u32[]{:S(2)}) %collective-permute-start.1) | collective-permute-done | bytes 278560 | tf_op jit(solution)/shard_map/ppermute | solution.py:389
  122.0 3.2 %collective-permute-start.2 = (bf16[64,2176]{1,0:T(8,128)(2,1)S(1)}, bf16[64,2176]{1,0:T(8,128)(2,1)}, u32[]{:S(2)}, u32[]{:S(2)}) collective-permute-start(bf16[64,2176]{1,0:T(8,128)(2,1)S(1)} %collective-permute-done.1.refs_2_), channel_id=1, source_target_pairs={{0,16},{16,32},{32,48},{48,64},{64,80},{80,96},{96,112},{112,0},{1... | collective-permute-start | bytes 835592 | tf_op jit(solution)/shard_map/ppermute | solution.py:389
  125.9 4.6 %collective-permute-done.2.refs_3_ = bf16[64,2176]{1,0:T(8,128)(2,1)} collective-permute-done((bf16[64,2176]{1,0:T(8,128)(2,1)S(1)}, bf16[64,2176]{1,0:T(8,128)(2,1)}, u32[]{:S(2)}, u32[]{:S(2)}) %collective-permute-start.2) | collective-permute-done | bytes 278560 | tf_op jit(solution)/shard_map/ppermute | solution.py:389
  130.5 3.8 %collective-permute-start.3 = (bf16[64,2176]{1,0:T(8,128)(2,1)}, bf16[64,2176]{1,0:T(8,128)(2,1)}, u32[]{:S(2)}, u32[]{:S(2)}) collective-permute-start(bf16[64,2176]{1,0:T(8,128)(2,1)} %collective-permute-done.2.refs_3_), channel_id=1, source_target_pairs={{0,16},{16,32},{32,48},{48,64},{64,80},{80,96},{96,112},{112,0},{1... | collective-permute-start | bytes 835592 | tf_op jit(solution)/shard_map/ppermute | solution.py:389
  135.1 3.8 %collective-permute-done.3.refs_4_ = bf16[64,2176]{1,0:T(8,128)(2,1)} collective-permute-done((bf16[64,2176]{1,0:T(8,128)(2,1)}, bf16[64,2176]{1,0:T(8,128)(2,1)}, u32[]{:S(2)}, u32[]{:S(2)}) %collective-permute-start.3) | collective-permute-done | bytes 278560 | tf_op jit(solution)/shard_map/ppermute | solution.py:389
  139.0 6.6 %pack.1 = (bf16[8,48,512]{2,1,0:T(8,128)(2,1)}, bf16[8,48,512]{2,1,0:T(8,128)(2,1)}, bf16[8,48,512]{2,1,0:T(8,128)(2,1)}, bf16[8,48,512]{2,1,0:T(8,128)(2,1)}, b...) custom-call(s32[2]{0:T(128)} %pad_add_fusion.place_ref, ...), custom_call_target="tpu_custom_call" | custom-call | tf_op jit(solution)/shard_map/pack/pallas_call | solution.py:80
  145.6 3.0 collective-permute-start.7
  149.4 2.7 collective-permute-start.8
  152.1 3.4 %collective-permute-done.7 = bf16[8,48,512]{2,1,0:T(8,128)(2,1)S(1)} collective-permute-done((bf16[8,48,512]{2,1,0:T(8,128)(2,1)}, bf16[8,48,512]{2,1,0:T(8,128)(2,1)S(1)}, u32[]{:S(2)}, u32[]{:S(2)}) %collective-permute-start.7) | collective-permute-done | bytes 393248 | tf_op jit(solution)/shard_map/ppermute | solution.py:411
  155.5 5.1 %collective-permute-start.9 = (bf16[8,48,512]{2,1,0:T(8,128)(2,1)}, bf16[8,48,512]{2,1,0:T(8,128)(2,1)S(1)}, u32[]{:S(2)}, u32[]{:S(2)}) collective-permute-start(bf16[8,48,512]{2,1,0:T(8,128)(2,1)} %get-tuple-element.13), channel_id=1, source_target_pairs={{0,14},{2,12},{4,10},{6,8},{8,6},{10,4},{12,2},{14,0},{16,30},{18,... | collective-permute-start | bytes 1179656 | tf_op jit(solution)/shard_map/ppermute | solution.py:411
  165.0 6.3 %collective-permute-done.9 = bf16[8,48,512]{2,1,0:T(8,128)(2,1)S(1)} collective-permute-done((bf16[8,48,512]{2,1,0:T(8,128)(2,1)}, bf16[8,48,512]{2,1,0:T(8,128)(2,1)S(1)}, u32[]{:S(2)}, u32[]{:S(2)}) %collective-permute-start.9) | collective-permute-done | bytes 393248 | tf_op jit(solution)/shard_map/ppermute | solution.py:411
  171.3 4.3 %collective-permute-start.11 = (bf16[8,48,512]{2,1,0:T(8,128)(2,1)}, bf16[8,48,512]{2,1,0:T(8,128)(2,1)S(1)}, u32[]{:S(2)}, u32[]{:S(2)}) collective-permute-start(bf16[8,48,512]{2,1,0:T(8,128)(2,1)} %get-tuple-element.15), channel_id=1, source_target_pairs={{0,134},{2,132},{4,130},{6,128},{8,142},{10,140},{12,138},{14,136}... | collective-permute-start | bytes 1179656 | tf_op jit(solution)/shard_map/ppermute | solution.py:411
  175.7 4.9 %collective-permute-done.10 = bf16[8,48,512]{2,1,0:T(8,128)(2,1)S(1)} collective-permute-done((bf16[8,48,512]{2,1,0:T(8,128)(2,1)}, bf16[8,48,512]{2,1,0:T(8,128)(2,1)S(1)}, u32[]{:S(2)}, u32[]{:S(2)}) %collective-permute-start.10) | collective-permute-done | bytes 393248 | tf_op jit(solution)/shard_map/ppermute | solution.py:411
  180.8 7.0 %collective-permute-done.11 = bf16[8,48,512]{2,1,0:T(8,128)(2,1)S(1)} collective-permute-done((bf16[8,48,512]{2,1,0:T(8,128)(2,1)}, bf16[8,48,512]{2,1,0:T(8,128)(2,1)S(1)}, u32[]{:S(2)}, u32[]{:S(2)}) %collective-permute-start.11) | collective-permute-done | bytes 393248 | tf_op jit(solution)/shard_map/ppermute | solution.py:411
  191.4 10.1 %collective-permute-done.13 = bf16[8,48,512]{2,1,0:T(8,128)(2,1)S(1)} collective-permute-done((bf16[8,48,512]{2,1,0:T(8,128)(2,1)}, bf16[8,48,512]{2,1,0:T(8,128)(2,1)S(1)}, u32[]{:S(2)}, u32[]{:S(2)}) %collective-permute-start.13) | collective-permute-done | bytes 393248 | tf_op jit(solution)/shard_map/ppermute | solution.py:411
  203.3 25.9 %expert.1 = bf16[64,24,1024]{2,1,0:T(8,128)(2,1)} custom-call(s32[2]{0:T(128)} %pad_add_fusion.place_ref, bf16[384,512]{1,0:T(8,128)(2,1)} %bitcast.32, bf16[384,512]{1,0:T(8,128)(2,1)} %bitcast.33, bf16[384,512]{1,0:T(8,128)(2,1)} %bitcast.34, bf16[384,512]{1,0:T(8,128)(2,1)} %bitcast.35, bf16[384,512]{1,0:T(8,128)(2,1)} %bitcast.36, ...), custom_call_target="tpu_custom_call" | custom-call | flops 13287555072 | bytes 23592960 | tf_op jit(solution)/shard_map/expert/pallas_call | solution.py:259
  229.2 11.5 %all-to-all-start = ((bf16[64,24,1024]{2,1,0:T(8,128)(2,1)}), bf16[64,24,1024]{2,1,0:T(8,128)(2,1)S(1)}, u32[]{:S(2)}, u32[]{:S(2)}) async-start(bf16[64,24,1024]{2,1,0:T(8,128)(2,1)} %expert.1), calls=%async_computation | async-start | bytes 6291456 | tf_op jit(solution)/shard_map/all_to_all | solution.py:417
  241.8 3.7 %gather_in.1 = bf16[2,16,64,512]{3,2,1,0:T(8,128)(2,1)} custom-call(s32[16]{0:T(128)} %select_reduce_fusion.index_ref, bf16[32,2,64,512]{3,2,1,0:T(8,128)(2,1)} %all-to-all-done.1.in_ref), custom_call_target="tpu_custom_call" | custom-call | tf_op jit(solution)/shard_map/gather_in/pallas_call | solution.py:317
  245.5 68.4 %all-to-all-done = bf16[64,24,1024]{2,1,0:T(8,128)(2,1)S(1)} async-done(((bf16[64,24,1024]{2,1,0:T(8,128)(2,1)}), bf16[64,24,1024]{2,1,0:T(8,128)(2,1)S(1)}, u32[]{:S(2)}, u32[]{:S(2)}) %all-to-all-start) | async-done | bytes 3145760 | tf_op jit(solution)/shard_map/all_to_all | solution.py:417
  315.5 5.3 %combine.1 = bf16[64,2048]{1,0:T(8,128)(2,1)} custom-call(s32[6,64]{1,0:T(8,128)} %bitcast.30, f32[6,64]{1,0:T(8,128)} %bitcast.31, bf16[1536,1024]{1,0:T(8,128)(2,1)} %bitcast.25), custom_call_target="tpu_custom_call" | custom-call | tf_op jit(solution)/shard_map/combine/pallas_call | solution.py:150
  (81 shorter events, 25.5 us)
Async XLA Ops:
  6.2 223.0 %all-to-all-start.1 = ((bf16[32,2,64,512]{3,2,1,0:T(8,128)(2,1)}), bf16[32,2,64,512]{3,2,1,0:T(8,128)(2,1)}, u32[]{:S(2)}, u32[]{:S(2)}) async-start(bf16[32,2,64,512]{3,2,1,0:T(8,128)(2,1)} %gather_out.1), calls=%async_computation.1 | async-start | bytes 8388608 | tf_op jit(solution)/shard_map/all_to_all | solution.py:429
  16.3 132.3 %collective-permute-start.16 = (bf16[352,2048]{1,0:T(8,128)(2,1)}, bf16[352,2048]{1,0:T(8,128)(2,1)}, u32[]{:S(2)}, u32[]{:S(2)}) collective-permute-start(bf16[352,2048]{1,0:T(8,128)(2,1)} %constant_dynamic-slice_fusion.3), channel_id=1, source_target_pairs={{0,2},{2,0},{4,6},{6,4},{8,10},{10,8},{12,14},{14,12},{1,3},{3,1},... | collective-permute-start | bytes 4325384 | tf_op jit(solution)/shard_map/ppermute | solution.py:378
  19.4 129.2 %collective-permute-start.15 = (bf16[352,2048]{1,0:T(8,128)(2,1)S(1)}, bf16[352,2048]{1,0:T(8,128)(2,1)}, u32[]{:S(2)}, u32[]{:S(2)}) collective-permute-start(bf16[352,2048]{1,0:T(8,128)(2,1)S(1)} %dynamic-slice_bitcast_fusion), channel_id=1, source_target_pairs={{0,2},{2,0},{4,6},{6,4},{8,10},{10,8},{12,14},{14,12},{1,3},{3,1},... | collective-permute-start | bytes 4325384 | tf_op jit(solution)/shard_map/ppermute | solution.py:378
  20.3 128.8 %collective-permute-start.14 = (bf16[352,2048]{1,0:T(8,128)(2,1)S(1)}, bf16[352,2048]{1,0:T(8,128)(2,1)}, u32[]{:S(2)}, u32[]{:S(2)}) collective-permute-start(bf16[352,2048]{1,0:T(8,128)(2,1)S(1)} %dynamic-slice_bitcast_fusion.1), channel_id=1, source_target_pairs={{0,2},{2,0},{4,6},{6,4},{8,10},{10,8},{12,14},{14,12},{1,3},{3,1},... | collective-permute-start | bytes 4325384 | tf_op jit(solution)/shard_map/ppermute | solution.py:378
  21.9 117.1 %copy-start.2 = (bf16[64,2176]{1,0:T(8,128)(2,1)}, bf16[64,2176]{1,0:T(8,128)(2,1)S(1)}, u32[]{:S(2)}) copy-start(bf16[64,2176]{1,0:T(8,128)(2,1)S(1)} %fusion.1.refs_0_) | copy-start | bytes 835588
  21.9 91.5 %collective-permute-start = (bf16[64,2176]{1,0:T(8,128)(2,1)S(1)}, bf16[64,2176]{1,0:T(8,128)(2,1)S(1)}, u32[]{:S(2)}, u32[]{:S(2)}) collective-permute-start(bf16[64,2176]{1,0:T(8,128)(2,1)S(1)} %fusion.1.refs_0_), channel_id=1, source_target_pairs={{0,16},{16,32},{32,48},{48,64},{64,80},{80,96},{96,112},{112,0},{1... | collective-permute-start | bytes 835592 | tf_op jit(solution)/shard_map/ppermute | solution.py:389
  24.6 91.2 %collective-permute-start.4 = (bf16[64,2176]{1,0:T(8,128)(2,1)S(1)}, bf16[64,2176]{1,0:T(8,128)(2,1)S(1)}, u32[]{:S(2)}, u32[]{:S(2)}) collective-permute-start(bf16[64,2176]{1,0:T(8,128)(2,1)S(1)} %fusion.1.refs_0_), channel_id=1, source_target_pairs={{16,0},{32,16},{48,32},{64,48},{80,64},{96,80},{112,96},{0,112},{1... | collective-permute-start | bytes 835592 | tf_op jit(solution)/shard_map/ppermute | solution.py:391
  113.4 8.6 %collective-permute-start.1 = (bf16[64,2176]{1,0:T(8,128)(2,1)S(1)}, bf16[64,2176]{1,0:T(8,128)(2,1)S(1)}, u32[]{:S(2)}, u32[]{:S(2)}) collective-permute-start(bf16[64,2176]{1,0:T(8,128)(2,1)S(1)} %collective-permute-done.refs_1_), channel_id=1, source_target_pairs={{0,16},{16,32},{32,48},{48,64},{64,80},{80,96},{96,112},{112,0},{1... | collective-permute-start | bytes 835592 | tf_op jit(solution)/shard_map/ppermute | solution.py:389
  115.8 10.0 %collective-permute-start.5 = (bf16[64,2176]{1,0:T(8,128)(2,1)S(1)}, bf16[64,2176]{1,0:T(8,128)(2,1)}, u32[]{:S(2)}, u32[]{:S(2)}) collective-permute-start(bf16[64,2176]{1,0:T(8,128)(2,1)S(1)} %collective-permute-done.4.refs_5_), channel_id=1, source_target_pairs={{16,0},{32,16},{48,32},{64,48},{80,64},{96,80},{112,96},{0,112},{1... | collective-permute-start | bytes 835592 | tf_op jit(solution)/shard_map/ppermute | solution.py:391
  122.0 8.5 %collective-permute-start.2 = (bf16[64,2176]{1,0:T(8,128)(2,1)S(1)}, bf16[64,2176]{1,0:T(8,128)(2,1)}, u32[]{:S(2)}, u32[]{:S(2)}) collective-permute-start(bf16[64,2176]{1,0:T(8,128)(2,1)S(1)} %collective-permute-done.1.refs_2_), channel_id=1, source_target_pairs={{0,16},{16,32},{32,48},{48,64},{64,80},{80,96},{96,112},{112,0},{1... | collective-permute-start | bytes 835592 | tf_op jit(solution)/shard_map/ppermute | solution.py:389
  125.9 9.3 %collective-permute-start.6 = (bf16[64,2176]{1,0:T(8,128)(2,1)}, bf16[64,2176]{1,0:T(8,128)(2,1)}, u32[]{:S(2)}, u32[]{:S(2)}) collective-permute-start(bf16[64,2176]{1,0:T(8,128)(2,1)} %collective-permute-done.5.refs_6_), channel_id=1, source_target_pairs={{16,0},{32,16},{48,32},{64,48},{80,64},{96,80},{112,96},{0,112},{1... | collective-permute-start | bytes 835592 | tf_op jit(solution)/shard_map/ppermute | solution.py:391
  130.5 8.5 %collective-permute-start.3 = (bf16[64,2176]{1,0:T(8,128)(2,1)}, bf16[64,2176]{1,0:T(8,128)(2,1)}, u32[]{:S(2)}, u32[]{:S(2)}) collective-permute-start(bf16[64,2176]{1,0:T(8,128)(2,1)} %collective-permute-done.2.refs_3_), channel_id=1, source_target_pairs={{0,16},{16,32},{32,48},{48,64},{64,80},{80,96},{96,112},{112,0},{1... | collective-permute-start | bytes 835592 | tf_op jit(solution)/shard_map/ppermute | solution.py:389
  145.6 9.9 %collective-permute-start.7 = (bf16[8,48,512]{2,1,0:T(8,128)(2,1)}, bf16[8,48,512]{2,1,0:T(8,128)(2,1)S(1)}, u32[]{:S(2)}, u32[]{:S(2)}) collective-permute-start(bf16[8,48,512]{2,1,0:T(8,128)(2,1)} %get-tuple-element.11), channel_id=1, source_target_pairs={{0,6},{2,4},{4,2},{6,0},{8,14},{10,12},{12,10},{14,8},{16,22},{18,... | collective-permute-start | bytes 1179656 | tf_op jit(solution)/shard_map/ppermute | solution.py:411
  148.6 53.0 %collective-permute-start.19 = (bf16[352,2048]{1,0:T(8,128)(2,1)}, bf16[352,2048]{1,0:T(8,128)(2,1)}, u32[]{:S(2)}, u32[]{:S(2)}) collective-permute-start(bf16[352,2048]{1,0:T(8,128)(2,1)} %collective-permute-done.16.refs_13_), channel_id=1, source_target_pairs={{0,1},{1,0},{2,3},{3,2},{4,5},{5,4},{6,7},{7,6},{8,9},{9,8},{10,11... | collective-permute-start | bytes 4325384 | tf_op jit(solution)/shard_map/ppermute | solution.py:380
  148.6 53.0 %collective-permute-start.18 = (bf16[352,2048]{1,0:T(8,128)(2,1)}, bf16[352,2048]{1,0:T(8,128)(2,1)S(1)}, u32[]{:S(2)}, u32[]{:S(2)}) collective-permute-start(bf16[352,2048]{1,0:T(8,128)(2,1)} %collective-permute-done.15.refs_12_), channel_id=1, source_target_pairs={{0,1},{1,0},{2,3},{3,2},{4,5},{5,4},{6,7},{7,6},{8,9},{9,8},{10,11... | collective-permute-start | bytes 4325384 | tf_op jit(solution)/shard_map/ppermute | solution.py:380
  149.1 52.5 %collective-permute-start.17 = (bf16[352,2048]{1,0:T(8,128)(2,1)}, bf16[352,2048]{1,0:T(8,128)(2,1)S(1)}, u32[]{:S(2)}, u32[]{:S(2)}) collective-permute-start(bf16[352,2048]{1,0:T(8,128)(2,1)} %collective-permute-done.14.refs_11_), channel_id=1, source_target_pairs={{0,1},{1,0},{2,3},{3,2},{4,5},{5,4},{6,7},{7,6},{8,9},{9,8},{10,11... | collective-permute-start | bytes 4325384 | tf_op jit(solution)/shard_map/ppermute | solution.py:380
  149.4 13.7 %collective-permute-start.8 = (bf16[8,48,512]{2,1,0:T(8,128)(2,1)}, bf16[8,48,512]{2,1,0:T(8,128)(2,1)S(1)}, u32[]{:S(2)}, u32[]{:S(2)}) collective-permute-start(bf16[8,48,512]{2,1,0:T(8,128)(2,1)} %get-tuple-element.12), channel_id=1, source_target_pairs={{0,8},{2,10},{4,12},{6,14},{8,0},{10,2},{12,4},{14,6},{16,24},{18,... | collective-permute-start | bytes 1179656 | tf_op jit(solution)/shard_map/ppermute | solution.py:411
  155.5 46.8 %copy-start.12 = (bf16[8,48,512]{2,1,0:T(8,128)(2,1)}, bf16[8,48,512]{2,1,0:T(8,128)(2,1)S(1)}, u32[]{:S(2)}) copy-start(bf16[8,48,512]{2,1,0:T(8,128)(2,1)S(1)} %collective-permute-done.7) | copy-start | bytes 1179652
  155.5 15.8 %collective-permute-start.9 = (bf16[8,48,512]{2,1,0:T(8,128)(2,1)}, bf16[8,48,512]{2,1,0:T(8,128)(2,1)S(1)}, u32[]{:S(2)}, u32[]{:S(2)}) collective-permute-start(bf16[8,48,512]{2,1,0:T(8,128)(2,1)} %get-tuple-element.13), channel_id=1, source_target_pairs={{0,14},{2,12},{4,10},{6,8},{8,6},{10,4},{12,2},{14,0},{16,30},{18,... | collective-permute-start | bytes 1179656 | tf_op jit(solution)/shard_map/ppermute | solution.py:411
  163.1 17.5 %collective-permute-start.10 = (bf16[8,48,512]{2,1,0:T(8,128)(2,1)}, bf16[8,48,512]{2,1,0:T(8,128)(2,1)S(1)}, u32[]{:S(2)}, u32[]{:S(2)}) collective-permute-start(bf16[8,48,512]{2,1,0:T(8,128)(2,1)} %get-tuple-element.14), channel_id=1, source_target_pairs={{0,128},{2,130},{4,132},{6,134},{8,136},{10,138},{12,140},{14,142}... | collective-permute-start | bytes 1179656 | tf_op jit(solution)/shard_map/ppermute | solution.py:411
  171.3 16.5 %collective-permute-start.11 = (bf16[8,48,512]{2,1,0:T(8,128)(2,1)}, bf16[8,48,512]{2,1,0:T(8,128)(2,1)S(1)}, u32[]{:S(2)}, u32[]{:S(2)}) collective-permute-start(bf16[8,48,512]{2,1,0:T(8,128)(2,1)} %get-tuple-element.15), channel_id=1, source_target_pairs={{0,134},{2,132},{4,130},{6,128},{8,142},{10,140},{12,138},{14,136}... | collective-permute-start | bytes 1179656 | tf_op jit(solution)/shard_map/ppermute | solution.py:411
  180.6 10.9 %collective-permute-start.12 = (bf16[8,48,512]{2,1,0:T(8,128)(2,1)}, bf16[8,48,512]{2,1,0:T(8,128)(2,1)S(1)}, u32[]{:S(2)}, u32[]{:S(2)}) collective-permute-start(bf16[8,48,512]{2,1,0:T(8,128)(2,1)} %get-tuple-element.16), channel_id=1, source_target_pairs={{0,136},{2,138},{4,140},{6,142},{8,128},{10,130},{12,132},{14,134}... | collective-permute-start | bytes 1179656 | tf_op jit(solution)/shard_map/ppermute | solution.py:411
  187.8 13.8 %collective-permute-start.13 = (bf16[8,48,512]{2,1,0:T(8,128)(2,1)}, bf16[8,48,512]{2,1,0:T(8,128)(2,1)S(1)}, u32[]{:S(2)}, u32[]{:S(2)}) collective-permute-start(bf16[8,48,512]{2,1,0:T(8,128)(2,1)} %get-tuple-element.17), channel_id=1, source_target_pairs={{0,142},{2,140},{4,138},{6,136},{8,134},{10,132},{12,130},{14,128}... | collective-permute-start | bytes 1179656 | tf_op jit(solution)/shard_map/ppermute | solution.py:411
  229.2 84.7 %all-to-all-start = ((bf16[64,24,1024]{2,1,0:T(8,128)(2,1)}), bf16[64,24,1024]{2,1,0:T(8,128)(2,1)S(1)}, u32[]{:S(2)}, u32[]{:S(2)}) async-start(bf16[64,24,1024]{2,1,0:T(8,128)(2,1)} %expert.1), calls=%async_computation | async-start | bytes 6291456 | tf_op jit(solution)/shard_map/all_to_all | solution.py:417
  (17 other events, 173.9 us)

commit v4 on v3

v4 whole, which is shorter than its diff:
```python
import functools

import jax
import jax.numpy as jnp
from jax import lax
from jax.experimental import pallas as pl
from jax.experimental.pallas import tpu as pltpu
from jax.sharding import PartitionSpec as P


F32 = jnp.float32
BF16 = jnp.bfloat16
TOP = 6
ZS = 8
PEERS = 8
NEAR = ZS // 2


def iota(shape, dim):
    return lax.broadcasted_iota(jnp.int32, shape, dim)


def divide(x, by):
    return ((x.astype(F32) + 0.5) * (1.0 / by)).astype(jnp.int32)


def dot(a, b, contract):
    return lax.dot_general(a, b, (contract, ((), ())), preferred_element_type=F32)


def expert_of(peer, z):
    return (peer >> 2) * 32 + z * 4 + (peer & 3)


def row_keys(group, rows, lanes):
    index = iota((NEAR * rows, lanes), 0)
    source = divide(index, rows)
    return ((group * NEAR + source) * 16 + index - source * rows).astype(F32)


def pack_kernel(rows, place_ref, *refs):
    blocks = refs[:ZS]
    outs = refs[ZS : ZS + PEERS]
    key_ref, whi_ref, wlo_ref, tok = refs[ZS + PEERS :]
    toks = blocks[0].shape[0]
    wide = tok.shape[1]
    experts = key_ref.shape[0]
    me, z = place_ref[0], place_ref[1]
    before, after = iota((toks, toks), 0), iota((toks, toks), 1)
    same = before == after
    tally = jnp.where(same, 64.0, jnp.where(before < after, 1.0, 0.0)).astype(BF16)
    same = same.astype(BF16)
    eids = iota((toks, experts), 1).astype(F32)
    for o, block in enumerate(blocks):
        lanes = block[:, wide : wide + 128].astype(F32)
        named = jnp.zeros((toks, experts), F32)
        high = jnp.zeros((toks, experts), F32)
        low = jnp.zeros((toks, experts), F32)
        for k in range(TOP):
            hit = lanes[:, k : k + 1] == eids
            named = named + jnp.where(hit, 1.0, 0.0)
            high = high + jnp.where(hit, lanes[:, TOP + k : TOP + k + 1], 0.0)
            low = low + jnp.where(hit, lanes[:, 2 * TOP + k : 2 * TOP + k + 1], 0.0)
        rank = dot(named.astype(BF16), tally, ((0,), (0,))) - 64.0
        here = slice(o * toks, (o + 1) * toks)
        key_ref[:, here] = jnp.where((rank > -0.5) & (rank < rows), rank + 16.0 * o, -1.0)
        whi_ref[:, here] = dot(high.astype(BF16), same, ((0,), (0,)))
        wlo_ref[:, here] = dot(low.astype(BF16), same, ((0,), (0,)))
        tok[here, :] = block[:, :wide]

    span = NEAR * toks
    part = NEAR * rows
    for g in range(ZS // NEAR):
        keys = row_keys(g, rows, span)
        masks = []
        for m in range(PEERS):
            row = key_ref[pl.ds(expert_of(me ^ m, z), 1), g * span : (g + 1) * span]
            masks.append(jnp.where(row == keys, 1.0, 0.0).astype(BF16))
        mask = jnp.concatenate(masks, axis=0)

        def columns(c, _):
            here = pl.ds(pl.multiple_of(c * 512, 512), 512)
            y = dot(mask, tok[g * span : (g + 1) * span, here], ((1,), (0,)))
            for m, out in enumerate(outs):
                out[g * part : (g + 1) * part, here] = y[m * part : (m + 1) * part, :].astype(BF16)
            return 0

        lax.fori_loop(0, wide // 512, columns, 0)


def pack(place, blocks, wide, experts, rows):
    toks = blocks[0].shape[0]
    shape = jax.ShapeDtypeStruct((ZS * rows, wide), BF16)
    small = jax.ShapeDtypeStruct((experts, ZS * toks), F32)
    vm = pl.BlockSpec(memory_space=pltpu.VMEM)
    return pl.pallas_call(
        functools.partial(pack_kernel, rows),
        in_specs=[pl.BlockSpec(memory_space=pltpu.SMEM)] + [vm] * ZS,
        out_specs=[vm] * (PEERS + 3),
        out_shape=[shape] * PEERS + [small] * 3,
        scratch_shapes=[pltpu.VMEM((ZS * toks, wide), BF16)],
        name="pack",
    )(place, *blocks)


def weigh_kernel(rows, group, place_ref, key_ref, whi_ref, wlo_ref, ret_ref, *outs):
    z = place_ref[1]
    span = key_ref.shape[1]
    toks = outs[0].shape[0]
    keys = row_keys(group, rows, span)
    pieces = []
    for j in range(PEERS):
        e = expert_of(j, z)
        hit = key_ref[pl.ds(e, 1), :] == keys
        high = jnp.where(hit, whi_ref[pl.ds(e, 1), :], 0.0).astype(BF16)
        low = jnp.where(hit, wlo_ref[pl.ds(e, 1), :], 0.0).astype(BF16)
        pieces.append(jnp.concatenate([high, low], axis=1))
    left = jnp.concatenate(pieces, axis=0)

    def columns(c, _):
        here = pl.ds(pl.multiple_of(c * 512, 512), 512)
        y = dot(left, ret_ref[:, here], ((0,), (0,)))
        y = y[:span] + y[span:]
        for o, out in enumerate(outs):
            out[:, here] = y[o * toks : (o + 1) * toks, :].astype(out.dtype)
        return 0

    lax.fori_loop(0, ret_ref.shape[1] // 512, columns, 0)


def weigh(place, keys, whi, wlo, ret, group, rows, kinds):
    experts, lanes = keys.shape
    toks = lanes // ZS
    small = pl.BlockSpec((experts, lanes * NEAR // ZS), lambda i: (0, group))
    wide = ret.shape[1]
    return pl.pallas_call(
        functools.partial(weigh_kernel, rows, group),
        grid=(1,),
        in_specs=[
            pl.BlockSpec(memory_space=pltpu.SMEM),
            small,
            small,
            small,
            pl.BlockSpec(ret.shape, lambda i: (0, 0)),
        ],
        out_specs=[pl.BlockSpec((toks, wide), lambda i: (0, 0))] * NEAR,
        out_shape=[jax.ShapeDtypeStruct((toks, wide), kind) for kind in kinds],
        name="weigh",
    )(place, keys, whi, wlo, ret)


def expert_kernel(place_ref, *refs):
    xin = refs[:PEERS]
    g0, u0, d0, g1, u1, d1, g2, u2, d2 = refs[PEERS : PEERS + 9]
    o_ref, wg, wu, wd, xs, acc, sems = refs[PEERS + 9 :]
    half = g0.shape[0]
    quarter = g1.shape[0]
    copies = []
    for i, (src, dst, start) in enumerate(
        [
            (g0, wg, 0),
            (u0, wu, 0),
            (d0, wd, 0),
            (g1, wg, half),
            (u1, wu, half),
            (g2, wg, half + quarter),
            (u2, wu, half + quarter),
            (d1, wd, half),
            (d2, wd, half + quarter),
        ]
    ):
        copy = pltpu.make_async_copy(src, dst.at[pl.ds(start, src.shape[0])], sems.at[i])
        copy.start()
        copies.append(copy)

    part = xin[0].shape[0]
    for m in range(PEERS):
        xs[m * part : (m + 1) * part, :] = xin[m][...]

    me = place_ref[0]
    total = wg.shape[0]
    cuts = [(0, 512), (512, half), (half, half + 512), (half + 512, total)]
    for n, (lo, hi) in enumerate(cuts):
        if n == 0:
            for copy in copies[:3]:
                copy.wait()
        if n == 2:
            for copy in copies[3:]:
                copy.wait()
        x = xs[...]
        gate = dot(x, wg[lo:hi, :], ((1,), (1,)))
        upper = dot(x, wu[lo:hi, :], ((1,), (1,)))
        hidden = (gate / (1.0 + jnp.exp(-gate)) * upper).astype(BF16)
        res = dot(hidden, wd[lo:hi, :], ((1,), (0,)))
        if n == 0:
            acc[...] = res
        elif n < len(cuts) - 1:
            acc[...] = acc[...] + res
        else:
            acc[...] = acc[...] + res
            for m in range(PEERS):
                o_ref[me ^ m] = acc[m * part : (m + 1) * part, :].astype(BF16)


def expert(place, x, own, first, second, group, rows):
    half, wide = own[0].shape
    total = 2 * half
    part = NEAR * rows
    count = PEERS * part
    anyspec = pl.BlockSpec(memory_space=pl.ANY)
    return pl.pallas_call(
        expert_kernel,
        grid=(1,),
        in_specs=[pl.BlockSpec(memory_space=pltpu.SMEM)]
        + [pl.BlockSpec((part, wide), lambda i: (group, 0))] * PEERS
        + [anyspec] * 9,
        out_specs=pl.BlockSpec((PEERS, part, wide), lambda i: (0, 0, 0)),
        out_shape=jax.ShapeDtypeStruct((PEERS, part, wide), BF16),
        scratch_shapes=[
            pltpu.VMEM((total, wide), BF16),
            pltpu.VMEM((total, wide), BF16),
            pltpu.VMEM((total, wide), BF16),
            pltpu.VMEM((count, wide), BF16),
            pltpu.VMEM((count, wide), F32),
            pltpu.SemaphoreType.DMA((9,)),
        ],
        compiler_params=pltpu.CompilerParams(vmem_limit_bytes=60 * 1024 * 1024),
        cost_estimate=pl.CostEstimate(
            flops=6 * count * total * wide,
            bytes_accessed=6 * total * wide + 4 * count * wide,
            transcendentals=count * total,
        ),
        name="expert",
    )(place, *x, *own, *first, *second)


def out_kernel(index_ref, in_ref, out_ref):
    def one(i, _):
        out_ref[i] = in_ref[:, index_ref[i]]
        return 0

    lax.fori_loop(0, out_ref.shape[0], one, 0)


def gather_out(index, cache):
    layers, _, blk, wide = cache.shape
    slots = index.shape[0]
    vm = pl.BlockSpec(memory_space=pltpu.VMEM)
    return pl.pallas_call(
        out_kernel,
        in_specs=[pl.BlockSpec(memory_space=pltpu.SMEM), vm],
        out_specs=vm,
        out_shape=jax.ShapeDtypeStruct((slots, layers, blk, wide), cache.dtype),
        name="gather_out",
    )(index, cache)


def in_kernel(index_ref, in_ref, out_ref):
    def one(i, _):
        out_ref[:, i] = in_ref[index_ref[i]]
        return 0

    lax.fori_loop(0, out_ref.shape[1], one, 0)


def gather_in(index, arrived):
    slots = index.shape[0]
    _, layers, blk, wide = arrived.shape
    vm = pl.BlockSpec(memory_space=pltpu.VMEM)
    return pl.pallas_call(
        in_kernel,
        in_specs=[pl.BlockSpec(memory_space=pltpu.SMEM), vm],
        out_specs=vm,
        out_shape=jax.ShapeDtypeStruct((layers, slots, blk, wide), arrived.dtype),
        name="gather_in",
    )(index, arrived)


def handover_indices(handover_table, sources, blk_dev, spare):
    column = lax.dynamic_index_in_dim(handover_table, lax.axis_index("tp"), 0, keepdims=False)
    here = lax.axis_index("pre")
    table = column.reshape(sources, blk_dev)
    dest = table // blk_dev
    earlier = jnp.arange(blk_dev)[:, None] < jnp.arange(blk_dev)[None, :]
    same = dest[:, :, None] == dest[:, None, :]
    rank = jnp.sum((same & earlier[None]).astype(jnp.int32), axis=1)
    my_dest = lax.dynamic_index_in_dim(dest, here, 0, keepdims=False)
    my_rank = lax.dynamic_index_in_dim(rank, here, 0, keepdims=False)
    wanted = jnp.arange(sources * spare, dtype=jnp.int32)
    out_index = jnp.sum(
        jnp.where(
            wanted[:, None] == (my_dest * spare + my_rank)[None, :],
            jnp.arange(blk_dev, dtype=jnp.int32)[None, :],
            0,
        ),
        axis=1,
    )
    place = here * blk_dev + jnp.arange(blk_dev, dtype=jnp.int32)
    came = jnp.arange(sources, dtype=jnp.int32)[:, None] * spare + rank
    in_index = jnp.sum(
        jnp.where(place[:, None, None] == table[None], came[None], 0), axis=(1, 2)
    )
    return out_index, in_index


def shards(
    tokens,
    route_ids,
    route_weights,
    gate_weight,
    up_weight,
    down_weight,
    prefill_cache,
    handover_table,
):
    tok_dev, wide = tokens.shape
    top_count = route_ids.shape[1]
    tp = lax.axis_size("tp")
    groups = lax.axis_size("pre") * tp
    experts_all = groups // 2
    rows = min(tok_dev, 2 * tok_dev * top_count // experts_all)

    half = down_weight.shape[0]
    quarter = half // 2
    core = lax.axis_index("dec")
    swap = [(i, i ^ 1) for i in range(tp)]
    first, second = [], []
    own = (gate_weight.T, up_weight.T, down_weight)
    for weight in own:
        piece = lax.dynamic_slice_in_dim(weight, core * quarter, quarter, 0)
        got = lax.ppermute(piece, "tp", swap)
        first.append(got)
        second.append(lax.ppermute(got, "dec", [(0, 1), (1, 0)]))

    pre = lax.axis_size("pre")
    high = route_weights.astype(BF16)
    low = (route_weights - high.astype(F32)).astype(BF16)
    lanes = jnp.concatenate([route_ids.astype(BF16), high, low], axis=1)
    lanes = jnp.pad(lanes, ((0, 0), (0, 128 - 3 * top_count)))
    block = jnp.concatenate([tokens, lanes], axis=1)
    up = [(i, i // ZS * ZS + (i + 1) % ZS) for i in range(pre)]
    down = [(j, i) for i, j in up]
    below, above = [block], [block]
    for n in range(4):
        below.append(lax.ppermute(below[-1], "pre", up))
        if n < 3:
            above.append(lax.ppermute(above[-1], "pre", down))
    blocks = [below[4], below[3], above[3], below[2], above[2], below[1], above[1], block]

    here = lax.axis_index("pre")
    there = lax.axis_index("tp")
    me = (here // ZS) * 4 + there // 2
    place = jnp.stack([me, here % ZS]).astype(jnp.int32)
    *packed, keys, whi, wlo = pack(place, blocks, wide, experts_all, rows)

    def kind_of(group):
        return (group ^ (group >> 1)) & 1

    def peer_of(group, flip):
        p, t = group // tp, group % tp
        peer = ((p // ZS) * 4 + t // 2) ^ flip
        last = peer & 1
        return ((peer >> 2) * ZS + p % ZS) * tp + (peer & 2) * 2 + last * 2 + (last ^ kind_of(t))

    came = [packed[0]]
    for m in range(1, PEERS):
        came.append(
            lax.ppermute(packed[m], ("pre", "tp"), [(g, peer_of(g, m)) for g in range(groups)])
        )

    planes = [
        [g for g in range(groups) if g // tp % ZS == z and kind_of(g) == kind]
        for z in range(ZS)
        for kind in (0, 1)
    ]
    sums = []
    results = []
    for group in range(ZS // NEAR):
        results.append(expert(place, came, own, first, second, group, rows))
    for group, result in enumerate(results):
        back = lax.all_to_all(
            result,
            ("pre", "tp"),
            split_axis=0,
            concat_axis=0,
            axis_index_groups=planes,
            tiled=True,
        )
        kinds = (BF16, BF16, F32, F32) if group == 0 else (F32,) * NEAR
        sums += weigh(place, keys, whi, wlo, back.reshape(-1, wide), group, rows, kinds)

    rising, falling = sums[0], sums[1]
    for local in (sums[2], sums[4], sums[6], None):
        rising = lax.ppermute(rising, "pre", up)
        if local is not None:
            rising = (rising.astype(F32) + local).astype(BF16)
    for local in (sums[3], sums[5], None):
        falling = lax.ppermute(falling, "pre", down)
        if local is not None:
            falling = (falling.astype(F32) + local).astype(BF16)
    moe_output = (rising.astype(F32) + falling.astype(F32) + sums[7]).astype(BF16)

    _, _, blk_dev, _, _ = prefill_cache.shape
    sources = lax.axis_size("pre")
    spare = blk_dev // sources + 1
    out_index, in_index = handover_indices(handover_table, sources, blk_dev, spare)
    leaving = gather_out(out_index, prefill_cache[:, 0])
    arrived = lax.all_to_all(leaving, "pre", split_axis=0, concat_axis=0, tiled=True)
    decode_cache = gather_in(in_index, arrived)[:, None]
    return (moe_output, decode_cache)


def solution(mesh):


    return jax.shard_map(
        shards,
        mesh=mesh,
        in_specs=(
            P(("pre", "tp", "dec"), None),
            P(("pre", "tp", "dec"), None),
            P(("pre", "tp", "dec"), None),
            P(None, ("pre", "tp")),
            P(None, ("pre", "tp")),
            P(("pre", "tp"), None),
            P(None, "tp", "pre", None, "dec"),
            P(),
        ),
        out_specs=(P(("pre", "tp", "dec"), None), P(None, "tp", "pre", None, "dec")),
        check_vma=False,
    )
```

time: 322 us -> 357 us (1.11)
  waiting for transfers between devices: 208 us -> 235 us
  Pallas kernels: 45.6 us -> 53.6 us
    ppermute x3, waiting for transfers between devices: 0.01 us -> 48.7 us  [shards(): got = lax.ppermute(piece, 'tp', swap)]
    all_to_all x1 -> x2, waiting for transfers between devices: 68.4 us -> 23.4 us  [shards(): lax.all_to_all(result, ('pre', 'tp'), split_axis=0, concat_axis=0, axis_i...]
    ppermute x7 -> x14, starting transfers between devices: 11.8 us -> 24.6 us  [the longest x4 14.4 us: shards(): below.append(lax.ppermute(below[-1], 'pre', up))]
    ppermute x7 -> x14, waiting for transfers between devices: 105 us -> 117 us  [the longest x4 99.5 us: shards(): rising = lax.ppermute(rising, 'pre', up)]
    ppermute x7, waiting for transfers between devices: 35.4 us -> 45.9 us  [shards(): lax.ppermute(packed[m], ('pre', 'tp'), [(g, peer_of(g, m)) for g in range...]
    ppermute x7, starting transfers between devices: 19.8 us -> 11.5 us  [shards(): lax.ppermute(packed[m], ('pre', 'tp'), [(g, peer_of(g, m)) for g in range...]
    pallas_call x3 -> x5, Pallas kernels: 37.8 us -> 45.8 us  [the longest x2 28.6 us: expert(): pl.pallas_call(expert_kernel, grid=(1,), in_specs=[pl.BlockSpec(memory_sp...]
    all_to_all x1 -> x2, starting transfers between devices: 11.5 us -> 7.39 us  [shards(): lax.all_to_all(result, ('pre', 'tp'), split_axis=0, concat_axis=0, axis_i...]
  transfers between devices with their start and end apart: 22 -> 30, of which waited for: 15 -> 18; matrix products, arithmetic and copies ran while one was open for 1% -> 1% of each run, Pallas kernels for 11% -> 10%
where the time goes in v4:
time: 357 us; the launch traced here: 355 us
  waiting for transfers between devices  235 us (66%)
  starting transfers between devices  55 us (15%)
  Pallas kernels  53.6 us (15%)
  local copies, waits for them, and re-layouts  7.39 us (2%)
    ppermute x4, waiting for transfers between devices, shards(): rising = lax.ppermute(rising, 'pre', up)  99.5 us
    ppermute x3, waiting for transfers between devices, shards(): got = lax.ppermute(piece, 'tp', swap)  48.7 us
    ppermute x7, waiting for transfers between devices, shards(): lax.ppermute(packed[m], ('pre', 'tp'), [(g, peer_of(g, m)) for g in range...  45.9 us
    pallas_call x2, Pallas kernels, expert(): pl.pallas_call(expert_kernel, grid=(1,), in_specs=[pl.BlockSpec(memory_sp...  28.6 us
    all_to_all x2, waiting for transfers between devices, shards(): lax.all_to_all(result, ('pre', 'tp'), split_axis=0, concat_axis=0, axis_i...  23.4 us
    ppermute x4, waiting for transfers between devices, shards(): below.append(lax.ppermute(below[-1], 'pre', up))  17.3 us
    ppermute x4, starting transfers between devices, shards(): below.append(lax.ppermute(below[-1], 'pre', up))  14.4 us
    ppermute x7, starting transfers between devices, shards(): lax.ppermute(packed[m], ('pre', 'tp'), [(g, peer_of(g, m)) for g in range...  11.5 us
  transfers between devices with their start and end apart: 30, of which 18 were waited for; matrix products, arithmetic and copies ran while one was open for 1% of the time, Pallas kernels for 10%

profile of v4, /device:TPU:96, one launch (start us, length us, event | category | flops | bytes accessed | tf_op | source)
XLA Modules:
  0.0 355.2 jit_solution(6189610491201316224)
XLA Ops:
  11.0 5.1 %collective-permute-done.refs_5_ = bf16[64,2176]{1,0:T(8,128)(2,1)S(1)} collective-permute-done((bf16[64,2176]{1,0:T(8,128)(2,1)S(1)}, bf16[64,2176]{1,0:T(8,128)(2,1)S(1)}, u32[]{:S(2)}, u32[]{:S(2)}) %collective-permute-start) | collective-permute-done | bytes 278560 | tf_op jit(solution)/shard_map/ppermute | solution.py:345
  19.8 4.3 %collective-permute-done.1.refs_3_ = bf16[64,2176]{1,0:T(8,128)(2,1)S(1)} collective-permute-done((bf16[64,2176]{1,0:T(8,128)(2,1)S(1)}, bf16[64,2176]{1,0:T(8,128)(2,1)S(1)}, u32[]{:S(2)}, u32[]{:S(2)}) %collective-permute-start.1) | collective-permute-done | bytes 278560 | tf_op jit(solution)/shard_map/ppermute | solution.py:345
  27.8 4.1 %collective-permute-done.2.refs_1_ = bf16[64,2176]{1,0:T(8,128)(2,1)} collective-permute-done((bf16[64,2176]{1,0:T(8,128)(2,1)S(1)}, bf16[64,2176]{1,0:T(8,128)(2,1)}, u32[]{:S(2)}, u32[]{:S(2)}) %collective-permute-start.2) | collective-permute-done | bytes 278560 | tf_op jit(solution)/shard_map/ppermute | solution.py:345
  36.2 3.8 %collective-permute-done.3.refs_0_ = bf16[64,2176]{1,0:T(8,128)(2,1)} collective-permute-done((bf16[64,2176]{1,0:T(8,128)(2,1)}, bf16[64,2176]{1,0:T(8,128)(2,1)}, u32[]{:S(2)}, u32[]{:S(2)}) %collective-permute-start.3) | collective-permute-done | bytes 278560 | tf_op jit(solution)/shard_map/ppermute | solution.py:345
  40.0 7.9 %pack.1 = (bf16[96,2048]{1,0:T(8,128)(2,1)}, bf16[96,2048]{1,0:T(8,128)(2,1)}, bf16[96,2048]{1,0:T(8,128)(2,1)}, bf16[96,2048]{1,0:T(8,128)(2,1)}, bf16[96,2048]...) custom-call(s32[2]{0:T(128)} %pad_add_fusion.place_ref, ...), custom_call_target="tpu_custom_call" | custom-call | tf_op jit(solution)/shard_map/pack/pallas_call | solution.py:96
  50.2 18.9 %collective-permute-done.15.refs_12_ = bf16[352,2048]{1,0:T(8,128)(2,1)} collective-permute-done((bf16[352,2048]{1,0:T(8,128)(2,1)S(1)}, bf16[352,2048]{1,0:T(8,128)(2,1)}, u32[]{:S(2)}, u32[]{:S(2)}) %collective-permute-start.15) | collective-permute-done | bytes 1441824 | tf_op jit(solution)/shard_map/ppermute | solution.py:331
  69.1 29.8 %collective-permute-done.14.refs_11_ = bf16[352,2048]{1,0:T(8,128)(2,1)} collective-permute-done((bf16[352,2048]{1,0:T(8,128)(2,1)S(1)}, bf16[352,2048]{1,0:T(8,128)(2,1)}, u32[]{:S(2)}, u32[]{:S(2)}) %collective-permute-start.14) | collective-permute-done | bytes 1441824 | tf_op jit(solution)/shard_map/ppermute | solution.py:331
  104.9 7.7 %collective-permute-done.8.refs_2_ = bf16[96,2048]{1,0:T(8,128)(2,1)S(1)} collective-permute-done((bf16[96,2048]{1,0:T(8,128)(2,1)}, bf16[96,2048]{1,0:T(8,128)(2,1)S(1)}, u32[]{:S(2)}, u32[]{:S(2)}) %collective-permute-start.8) | collective-permute-done | bytes 393248 | tf_op jit(solution)/shard_map/ppermute | solution.py:368
  114.1 9.4 %collective-permute-done.9.refs_3_ = bf16[96,2048]{1,0:T(8,128)(2,1)S(1)} collective-permute-done((bf16[96,2048]{1,0:T(8,128)(2,1)}, bf16[96,2048]{1,0:T(8,128)(2,1)S(1)}, u32[]{:S(2)}, u32[]{:S(2)}) %collective-permute-start.9) | collective-permute-done | bytes 393248 | tf_op jit(solution)/shard_map/ppermute | solution.py:368
  124.6 4.9 %collective-permute-done.10.refs_4_ = bf16[96,2048]{1,0:T(8,128)(2,1)S(1)} collective-permute-done((bf16[96,2048]{1,0:T(8,128)(2,1)}, bf16[96,2048]{1,0:T(8,128)(2,1)S(1)}, u32[]{:S(2)}, u32[]{:S(2)}) %collective-permute-start.10) | collective-permute-done | bytes 393248 | tf_op jit(solution)/shard_map/ppermute | solution.py:368
  130.0 9.9 %collective-permute-done.11.refs_5_ = bf16[96,2048]{1,0:T(8,128)(2,1)S(1)} collective-permute-done((bf16[96,2048]{1,0:T(8,128)(2,1)}, bf16[96,2048]{1,0:T(8,128)(2,1)S(1)}, u32[]{:S(2)}, u32[]{:S(2)}) %collective-permute-start.11) | collective-permute-done | bytes 393248 | tf_op jit(solution)/shard_map/ppermute | solution.py:368
  141.2 13.0 %collective-permute-done.13.refs_7_ = bf16[96,2048]{1,0:T(8,128)(2,1)S(1)} collective-permute-done((bf16[96,2048]{1,0:T(8,128)(2,1)}, bf16[96,2048]{1,0:T(8,128)(2,1)S(1)}, u32[]{:S(2)}, u32[]{:S(2)}) %collective-permute-start.13) | collective-permute-done | bytes 393248 | tf_op jit(solution)/shard_map/ppermute | solution.py:368
  155.9 14.3 %expert.2 = bf16[8,48,2048]{2,1,0:T(8,128)(2,1)} custom-call(s32[2]{0:T(128)} %pad_add_fusion.place_ref, bf16[96,2048]{1,0:T(8,128)(2,1)} %get-tuple-element.24.refs_0_, bf16[96,2048]{1,0:T(8,128)(2,1)} %copy-done.20, bf16[96,2048]{1,0:T(8,128)(2,1)} %copy-done.21, bf16[96,2048]{1,0:T(8,128)(2,1)} %copy-done.22, bf16[96,2048]{1,0:T(8,128)(2,1)} %copy-done.23, ...), custom_call_target="tpu_custom_call" | custom-call | flops 6643777536 | bytes 20447232 | tf_op jit(solution)/shard_map/expert/pallas_call | solution.py:211
  170.3 3.8 %all-to-all-start = ((bf16[8,48,2048]{2,1,0:T(8,128)(2,1)}), bf16[8,48,2048]{2,1,0:T(8,128)(2,1)S(1)}, u32[]{:S(2)}, u32[]{:S(2)}) async-start(bf16[8,48,2048]{2,1,0:T(8,128)(2,1)} %expert.2), calls=%async_computation | async-start | bytes 3145728 | tf_op jit(solution)/shard_map/all_to_all | solution.py:381
  174.1 14.3 %expert.3 = bf16[8,48,2048]{2,1,0:T(8,128)(2,1)} custom-call(s32[2]{0:T(128)} %pad_add_fusion.place_ref, bf16[96,2048]{1,0:T(8,128)(2,1)} %get-tuple-element.24.refs_0_, bf16[96,2048]{1,0:T(8,128)(2,1)} %copy-done.20, bf16[96,2048]{1,0:T(8,128)(2,1)} %copy-done.21, bf16[96,2048]{1,0:T(8,128)(2,1)} %copy-done.22, bf16[96,2048]{1,0:T(8,128)(2,1)} %copy-done.23, ...), custom_call_target="tpu_custom_call" | custom-call | flops 6643777536 | bytes 20447232 | tf_op jit(solution)/shard_map/expert/pallas_call | solution.py:211
  188.4 7.2 %all-to-all-done = bf16[8,48,2048]{2,1,0:T(8,128)(2,1)S(1)} async-done(((bf16[8,48,2048]{2,1,0:T(8,128)(2,1)}), bf16[8,48,2048]{2,1,0:T(8,128)(2,1)S(1)}, u32[]{:S(2)}, u32[]{:S(2)}) %all-to-all-start) | async-done | bytes 1572896 | tf_op jit(solution)/shard_map/all_to_all | solution.py:381
  201.2 4.0 %gather_out.1 = bf16[32,2,64,512]{3,2,1,0:T(8,128)(2,1)} custom-call(s32[32]{0:T(128)} %select_reduce_fusion.1.index_ref, bf16[2,16,64,512]{3,2,1,0:T(8,128)(2,1)} %bitcast.18), custom_call_target="tpu_custom_call" | custom-call | tf_op jit(solution)/shard_map/gather_out/pallas_call | solution.py:249
  205.2 16.3 %all-to-all-done.1 = bf16[8,48,2048]{2,1,0:T(8,128)(2,1)S(1)} async-done(((bf16[8,48,2048]{2,1,0:T(8,128)(2,1)}), bf16[8,48,2048]{2,1,0:T(8,128)(2,1)S(1)}, u32[]{:S(2)}, u32[]{:S(2)}) %all-to-all-start.1) | async-done | bytes 1572896 | tf_op jit(solution)/shard_map/all_to_all | solution.py:381
  222.7 7.7 %all-to-all-start.2 = ((bf16[32,2,64,512]{3,2,1,0:T(8,128)(2,1)}), bf16[32,2,64,512]{3,2,1,0:T(8,128)(2,1)}, u32[]{:S(2)}, u32[]{:S(2)}) async-start(bf16[32,2,64,512]{3,2,1,0:T(8,128)(2,1)} %gather_out.1), calls=%async_computation.2 | async-start | bytes 8388608 | tf_op jit(solution)/shard_map/all_to_all | solution.py:408
  230.3 4.5 %weigh.2 = (bf16[64,2048]{1,0:T(8,128)(2,1)}, bf16[64,2048]{1,0:T(8,128)(2,1)}, f32[64,2048]{1,0:T(8,128)}, f32[64,2048]{1,0:T(8,128)}) custom-call(s32[2]{0:T(128)} %pad_add_fusion.place_ref, f32[64,512]{1,0:T(8,128)} %get-tuple-element.21.key_ref, f32[64,512]{1,0:T(8,128)} %get-tuple-element.22.whi_ref, f32[64,512]{1,0:T(8,128)} %get-tuple-element.23.wlo_ref, ...), custom_call_target="tpu_custom_call" | custom-call | tf_op jit(solution)/shard_map/weigh/pallas_call | solution.py:136
  237.6 4.7 %weigh.3 = (f32[64,2048]{1,0:T(8,128)}, f32[64,2048]{1,0:T(8,128)}, f32[64,2048]{1,0:T(8,128)}, f32[64,2048]{1,0:T(8,128)}) custom-call(s32[2]{0:T(128)} %pad_add_fusion.place_ref, f32[64,512]{1,0:T(8,128)} %get-tuple-element.21.key_ref, f32[64,512]{1,0:T(8,128)} %get-tuple-element.22.whi_ref, f32[64,512]{1,0:T(8,128)} %get-tuple-element.23.wlo_ref, ...), custom_call_target="tpu_custom_call" | custom-call | tf_op jit(solution)/shard_map/weigh/pallas_call | solution.py:136
  242.4 86.1 %collective-permute-done.20 = bf16[64,2048]{1,0:T(8,128)(2,1)S(1)} collective-permute-done((bf16[64,2048]{1,0:T(8,128)(2,1)}, bf16[64,2048]{1,0:T(8,128)(2,1)S(1)}, u32[]{:S(2)}, u32[]{:S(2)}) %collective-permute-start.20) | collective-permute-done | bytes 262176 | tf_op jit(solution)/shard_map/ppermute | solution.py:394
  330.8 5.7 %collective-permute-done.21 = bf16[64,2048]{1,0:T(8,128)(2,1)S(1)} collective-permute-done((bf16[64,2048]{1,0:T(8,128)(2,1)S(1)}, bf16[64,2048]{1,0:T(8,128)(2,1)S(1)}, u32[]{:S(2)}, u32[]{:S(2)}) %collective-permute-start.21) | collective-permute-done | bytes 262176 | tf_op jit(solution)/shard_map/ppermute | solution.py:394
  338.8 4.8 %collective-permute-done.22 = bf16[64,2048]{1,0:T(8,128)(2,1)S(1)} collective-permute-done((bf16[64,2048]{1,0:T(8,128)(2,1)S(1)}, bf16[64,2048]{1,0:T(8,128)(2,1)S(1)}, u32[]{:S(2)}, u32[]{:S(2)}) %collective-permute-start.22) | collective-permute-done | bytes 262176 | tf_op jit(solution)/shard_map/ppermute | solution.py:394
  (125 shorter events, 62.0 us)
Async XLA Ops:
  3.4 46.8 %collective-permute-start.16 = (bf16[352,2048]{1,0:T(8,128)(2,1)}, bf16[352,2048]{1,0:T(8,128)(2,1)}, u32[]{:S(2)}, u32[]{:S(2)}) collective-permute-start(bf16[352,2048]{1,0:T(8,128)(2,1)} %constant_dynamic-slice_fusion.3), channel_id=1, source_target_pairs={{0,2},{2,0},{4,6},{6,4},{8,10},{10,8},{12,14},{14,12},{1,3},{3,1},... | collective-permute-start | bytes 4325384 | tf_op jit(solution)/shard_map/ppermute | solution.py:331
  5.2 63.9 %collective-permute-start.15 = (bf16[352,2048]{1,0:T(8,128)(2,1)S(1)}, bf16[352,2048]{1,0:T(8,128)(2,1)}, u32[]{:S(2)}, u32[]{:S(2)}) collective-permute-start(bf16[352,2048]{1,0:T(8,128)(2,1)S(1)} %dynamic-slice_bitcast_fusion), channel_id=1, source_target_pairs={{0,2},{2,0},{4,6},{6,4},{8,10},{10,8},{12,14},{14,12},{1,3},{3,1},... | collective-permute-start | bytes 4325384 | tf_op jit(solution)/shard_map/ppermute | solution.py:331
  5.9 93.0 %collective-permute-start.14 = (bf16[352,2048]{1,0:T(8,128)(2,1)S(1)}, bf16[352,2048]{1,0:T(8,128)(2,1)}, u32[]{:S(2)}, u32[]{:S(2)}) collective-permute-start(bf16[352,2048]{1,0:T(8,128)(2,1)S(1)} %dynamic-slice_bitcast_fusion.1), channel_id=1, source_target_pairs={{0,2},{2,0},{4,6},{6,4},{8,10},{10,8},{12,14},{14,12},{1,3},{3,1},... | collective-permute-start | bytes 4325384 | tf_op jit(solution)/shard_map/ppermute | solution.py:331
  7.8 8.3 %collective-permute-start = (bf16[64,2176]{1,0:T(8,128)(2,1)S(1)}, bf16[64,2176]{1,0:T(8,128)(2,1)S(1)}, u32[]{:S(2)}, u32[]{:S(2)}) collective-permute-start(bf16[64,2176]{1,0:T(8,128)(2,1)S(1)} %fusion.1.refs_7_), channel_id=1, source_target_pairs={{0,16},{16,32},{32,48},{48,64},{64,80},{80,96},{96,112},{112,0},{1... | collective-permute-start | bytes 835592 | tf_op jit(solution)/shard_map/ppermute | solution.py:345
  11.0 8.8 %collective-permute-start.4 = (bf16[64,2176]{1,0:T(8,128)(2,1)S(1)}, bf16[64,2176]{1,0:T(8,128)(2,1)S(1)}, u32[]{:S(2)}, u32[]{:S(2)}) collective-permute-start(bf16[64,2176]{1,0:T(8,128)(2,1)S(1)} %fusion.1.refs_7_), channel_id=1, source_target_pairs={{16,0},{32,16},{48,32},{64,48},{80,64},{96,80},{112,96},{0,112},{1... | collective-permute-start | bytes 835592 | tf_op jit(solution)/shard_map/ppermute | solution.py:347
  27.8 8.4 %collective-permute-start.6 = (bf16[64,2176]{1,0:T(8,128)(2,1)}, bf16[64,2176]{1,0:T(8,128)(2,1)}, u32[]{:S(2)}, u32[]{:S(2)}) collective-permute-start(bf16[64,2176]{1,0:T(8,128)(2,1)} %collective-permute-done.5.refs_4_), channel_id=1, source_target_pairs={{16,0},{32,16},{48,32},{64,48},{80,64},{96,80},{112,96},{0,112},{1... | collective-permute-start | bytes 835592 | tf_op jit(solution)/shard_map/ppermute | solution.py:347
  31.8 8.2 %collective-permute-start.3 = (bf16[64,2176]{1,0:T(8,128)(2,1)}, bf16[64,2176]{1,0:T(8,128)(2,1)}, u32[]{:S(2)}, u32[]{:S(2)}) collective-permute-start(bf16[64,2176]{1,0:T(8,128)(2,1)} %collective-permute-done.2.refs_1_), channel_id=1, source_target_pairs={{0,16},{16,32},{32,48},{48,64},{64,80},{80,96},{96,112},{112,0},{1... | collective-permute-start | bytes 835592 | tf_op jit(solution)/shard_map/ppermute | solution.py:345
  48.0 53.9 %collective-permute-start.7 = (bf16[96,2048]{1,0:T(8,128)(2,1)}, bf16[96,2048]{1,0:T(8,128)(2,1)S(1)}, u32[]{:S(2)}, u32[]{:S(2)}) collective-permute-start(bf16[96,2048]{1,0:T(8,128)(2,1)} %get-tuple-element.25), channel_id=1, source_target_pairs={{0,6},{2,4},{4,2},{6,0},{8,14},{10,12},{12,10},{14,8},{16,22},{18,... | collective-permute-start | bytes 1179656 | tf_op jit(solution)/shard_map/ppermute | solution.py:368
  50.2 103.9 %collective-permute-start.19 = (bf16[352,2048]{1,0:T(8,128)(2,1)}, bf16[352,2048]{1,0:T(8,128)(2,1)}, u32[]{:S(2)}, u32[]{:S(2)}) collective-permute-start(bf16[352,2048]{1,0:T(8,128)(2,1)} %collective-permute-done.16.refs_13_), channel_id=1, source_target_pairs={{0,1},{1,0},{2,3},{3,2},{4,5},{5,4},{6,7},{7,6},{8,9},{9,8},{10,11... | collective-permute-start | bytes 4325384 | tf_op jit(solution)/shard_map/ppermute | solution.py:333
  69.1 85.0 %collective-permute-start.18 = (bf16[352,2048]{1,0:T(8,128)(2,1)}, bf16[352,2048]{1,0:T(8,128)(2,1)S(1)}, u32[]{:S(2)}, u32[]{:S(2)}) collective-permute-start(bf16[352,2048]{1,0:T(8,128)(2,1)} %collective-permute-done.15.refs_12_), channel_id=1, source_target_pairs={{0,1},{1,0},{2,3},{3,2},{4,5},{5,4},{6,7},{7,6},{8,9},{9,8},{10,11... | collective-permute-start | bytes 4325384 | tf_op jit(solution)/shard_map/ppermute | solution.py:333
  98.9 55.3 %collective-permute-start.17 = (bf16[352,2048]{1,0:T(8,128)(2,1)}, bf16[352,2048]{1,0:T(8,128)(2,1)S(1)}, u32[]{:S(2)}, u32[]{:S(2)}) collective-permute-start(bf16[352,2048]{1,0:T(8,128)(2,1)} %collective-permute-done.14.refs_11_), channel_id=1, source_target_pairs={{0,1},{1,0},{2,3},{3,2},{4,5},{5,4},{6,7},{7,6},{8,9},{9,8},{10,11... | collective-permute-start | bytes 4325384 | tf_op jit(solution)/shard_map/ppermute | solution.py:333
  98.9 13.7 %collective-permute-start.8 = (bf16[96,2048]{1,0:T(8,128)(2,1)}, bf16[96,2048]{1,0:T(8,128)(2,1)S(1)}, u32[]{:S(2)}, u32[]{:S(2)}) collective-permute-start(bf16[96,2048]{1,0:T(8,128)(2,1)} %get-tuple-element.26), channel_id=1, source_target_pairs={{0,8},{2,10},{4,12},{6,14},{8,0},{10,2},{12,4},{14,6},{16,24},{18,... | collective-permute-start | bytes 1179656 | tf_op jit(solution)/shard_map/ppermute | solution.py:368
  101.9 21.6 %collective-permute-start.9 = (bf16[96,2048]{1,0:T(8,128)(2,1)}, bf16[96,2048]{1,0:T(8,128)(2,1)S(1)}, u32[]{:S(2)}, u32[]{:S(2)}) collective-permute-start(bf16[96,2048]{1,0:T(8,128)(2,1)} %get-tuple-element.27), channel_id=1, source_target_pairs={{0,14},{2,12},{4,10},{6,8},{8,6},{10,4},{12,2},{14,0},{16,30},{18,... | collective-permute-start | bytes 1179656 | tf_op jit(solution)/shard_map/ppermute | solution.py:368
  112.6 16.9 %collective-permute-start.10 = (bf16[96,2048]{1,0:T(8,128)(2,1)}, bf16[96,2048]{1,0:T(8,128)(2,1)S(1)}, u32[]{:S(2)}, u32[]{:S(2)}) collective-permute-start(bf16[96,2048]{1,0:T(8,128)(2,1)} %get-tuple-element.28), channel_id=1, source_target_pairs={{0,128},{2,130},{4,132},{6,134},{8,136},{10,138},{12,140},{14,142}... | collective-permute-start | bytes 1179656 | tf_op jit(solution)/shard_map/ppermute | solution.py:368
  123.5 16.5 %collective-permute-start.11 = (bf16[96,2048]{1,0:T(8,128)(2,1)}, bf16[96,2048]{1,0:T(8,128)(2,1)S(1)}, u32[]{:S(2)}, u32[]{:S(2)}) collective-permute-start(bf16[96,2048]{1,0:T(8,128)(2,1)} %get-tuple-element.29), channel_id=1, source_target_pairs={{0,134},{2,132},{4,130},{6,128},{8,142},{10,140},{12,138},{14,136}... | collective-permute-start | bytes 1179656 | tf_op jit(solution)/shard_map/ppermute | solution.py:368
  129.5 11.6 %collective-permute-start.12 = (bf16[96,2048]{1,0:T(8,128)(2,1)}, bf16[96,2048]{1,0:T(8,128)(2,1)S(1)}, u32[]{:S(2)}, u32[]{:S(2)}) collective-permute-start(bf16[96,2048]{1,0:T(8,128)(2,1)} %get-tuple-element.30), channel_id=1, source_target_pairs={{0,136},{2,138},{4,140},{6,142},{8,128},{10,130},{12,132},{14,134}... | collective-permute-start | bytes 1179656 | tf_op jit(solution)/shard_map/ppermute | solution.py:368
  139.9 14.2 %collective-permute-start.13 = (bf16[96,2048]{1,0:T(8,128)(2,1)}, bf16[96,2048]{1,0:T(8,128)(2,1)S(1)}, u32[]{:S(2)}, u32[]{:S(2)}) collective-permute-start(bf16[96,2048]{1,0:T(8,128)(2,1)} %get-tuple-element.31), channel_id=1, source_target_pairs={{0,142},{2,140},{4,138},{6,136},{8,134},{10,132},{12,130},{14,128}... | collective-permute-start | bytes 1179656 | tf_op jit(solution)/shard_map/ppermute | solution.py:368
  170.3 25.3 %all-to-all-start = ((bf16[8,48,2048]{2,1,0:T(8,128)(2,1)}), bf16[8,48,2048]{2,1,0:T(8,128)(2,1)S(1)}, u32[]{:S(2)}, u32[]{:S(2)}) async-start(bf16[8,48,2048]{2,1,0:T(8,128)(2,1)} %expert.2), calls=%async_computation | async-start | bytes 3145728 | tf_op jit(solution)/shard_map/all_to_all | solution.py:381
  196.7 24.8 %all-to-all-start.1 = ((bf16[8,48,2048]{2,1,0:T(8,128)(2,1)}), bf16[8,48,2048]{2,1,0:T(8,128)(2,1)S(1)}, u32[]{:S(2)}, u32[]{:S(2)}) async-start(bf16[8,48,2048]{2,1,0:T(8,128)(2,1)} %expert.3), calls=%async_computation.1 | async-start | bytes 3145728 | tf_op jit(solution)/shard_map/all_to_all | solution.py:381
  222.7 128.8 %all-to-all-start.2 = ((bf16[32,2,64,512]{3,2,1,0:T(8,128)(2,1)}), bf16[32,2,64,512]{3,2,1,0:T(8,128)(2,1)}, u32[]{:S(2)}, u32[]{:S(2)}) async-start(bf16[32,2,64,512]{3,2,1,0:T(8,128)(2,1)} %gather_out.1), calls=%async_computation.2 | async-start | bytes 8388608 | tf_op jit(solution)/shard_map/all_to_all | solution.py:408
  234.9 93.6 %collective-permute-start.20 = (bf16[64,2048]{1,0:T(8,128)(2,1)}, bf16[64,2048]{1,0:T(8,128)(2,1)S(1)}, u32[]{:S(2)}, u32[]{:S(2)}) collective-permute-start(bf16[64,2048]{1,0:T(8,128)(2,1)} %get-tuple-element.32), channel_id=1, source_target_pairs={{0,16},{16,32},{32,48},{48,64},{64,80},{80,96},{96,112},{112,0},{1... | collective-permute-start | bytes 786440 | tf_op jit(solution)/shard_map/ppermute | solution.py:394
  242.4 86.3 %collective-permute-start.24 = (bf16[64,2048]{1,0:T(8,128)(2,1)S(1)}, bf16[64,2048]{1,0:T(8,128)(2,1)S(1)}, u32[]{:S(2)}, u32[]{:S(2)}) collective-permute-start(bf16[64,2048]{1,0:T(8,128)(2,1)S(1)} %copy-done.27), channel_id=1, source_target_pairs={{16,0},{32,16},{48,32},{64,48},{80,64},{96,80},{112,96},{0,112},{1... | collective-permute-start | bytes 786440 | tf_op jit(solution)/shard_map/ppermute | solution.py:398
  328.7 9.4 %collective-permute-start.25 = (bf16[64,2048]{1,0:T(8,128)(2,1)S(1)}, bf16[64,2048]{1,0:T(8,128)(2,1)S(1)}, u32[]{:S(2)}, u32[]{:S(2)}) collective-permute-start(bf16[64,2048]{1,0:T(8,128)(2,1)S(1)} %add_convert_fusion.2), channel_id=1, source_target_pairs={{16,0},{32,16},{48,32},{64,48},{80,64},{96,80},{112,96},{0,112},{1... | collective-permute-start | bytes 786440 | tf_op jit(solution)/shard_map/ppermute | solution.py:398
  338.2 9.6 %collective-permute-start.26 = (bf16[64,2048]{1,0:T(8,128)(2,1)S(1)}, bf16[64,2048]{1,0:T(8,128)(2,1)S(1)}, u32[]{:S(2)}, u32[]{:S(2)}) collective-permute-start(bf16[64,2048]{1,0:T(8,128)(2,1)S(1)} %add_convert_fusion.1), channel_id=1, source_target_pairs={{16,0},{32,16},{48,32},{64,48},{80,64},{96,80},{112,96},{0,112},{1... | collective-permute-start | bytes 786440 | tf_op jit(solution)/shard_map/ppermute | solution.py:398
  (34 other events, 835.4 us)

commit v5 on v4

--- a/solution.py
+++ b/solution.py
@@ -41,7 +41,7 @@
 def pack_kernel(rows, place_ref, *refs):
     blocks = refs[:ZS]
     outs = refs[ZS : ZS + PEERS]
-    key_ref, whi_ref, wlo_ref, tok = refs[ZS + PEERS :]
+    key_ref, whi_ref, wlo_ref, tok, side = refs[ZS + PEERS :]
     toks = blocks[0].shape[0]
     wide = tok.shape[1]
     experts = key_ref.shape[0]
@@ -52,40 +52,57 @@
     same = same.astype(BF16)
     eids = iota((toks, experts), 1).astype(F32)
     for o, block in enumerate(blocks):
-        lanes = block[:, wide : wide + 128].astype(F32)
-        named = jnp.zeros((toks, experts), F32)
-        high = jnp.zeros((toks, experts), F32)
-        low = jnp.zeros((toks, experts), F32)
-        for k in range(TOP):
-            hit = lanes[:, k : k + 1] == eids
-            named = named + jnp.where(hit, 1.0, 0.0)
-            high = high + jnp.where(hit, lanes[:, TOP + k : TOP + k + 1], 0.0)
-            low = low + jnp.where(hit, lanes[:, 2 * TOP + k : 2 * TOP + k + 1], 0.0)
-        rank = dot(named.astype(BF16), tally, ((0,), (0,))) - 64.0
-        here = slice(o * toks, (o + 1) * toks)
-        key_ref[:, here] = jnp.where((rank > -0.5) & (rank < rows), rank + 16.0 * o, -1.0)
-        whi_ref[:, here] = dot(high.astype(BF16), same, ((0,), (0,)))
-        wlo_ref[:, here] = dot(low.astype(BF16), same, ((0,), (0,)))
-        tok[here, :] = block[:, :wide]
-
+        side[o] = block[:, wide : wide + 128].astype(F32)
+        tok[o * toks : (o + 1) * toks, :] = block[:, :wide]
+
+    def route(pair, _):
+        keys, highs, lows = [], [], []
+        for n in range(2):
+            lanes = side[pair * 2 + n]
+            named = jnp.zeros((toks, experts), F32)
+            high = jnp.zeros((toks, experts), F32)
+            low = jnp.zeros((toks, experts), F32)
+            for k in range(TOP):
+                hit = lanes[:, k : k + 1] == eids
+                named = named + jnp.where(hit, 1.0, 0.0)
+                high = high + jnp.where(hit, lanes[:, TOP + k : TOP + k + 1], 0.0)
+                low = low + jnp.where(hit, lanes[:, 2 * TOP + k : 2 * TOP + k + 1], 0.0)
+            rank = dot(named.astype(BF16), tally, ((0,), (0,))) - 64.0
+            first = (16 * (pair * 2 + n)).astype(F32)
+            keys.append(jnp.where((rank > -0.5) & (rank < rows), rank + first, -1.0))
+            highs.append(dot(high.astype(BF16), same, ((0,), (0,))))
+            lows.append(dot(low.astype(BF16), same, ((0,), (0,))))
+        here = pl.ds(pl.multiple_of(pair * 2 * toks, 2 * toks), 2 * toks)
+        key_ref[:, here] = jnp.concatenate(keys, axis=1)
+        whi_ref[:, here] = jnp.concatenate(highs, axis=1)
+        wlo_ref[:, here] = jnp.concatenate(lows, axis=1)
+        return 0
+
+    lax.fori_loop(0, ZS // 2, route, 0)
     span = NEAR * toks
     part = NEAR * rows
-    for g in range(ZS // NEAR):
+
+    def one(g, _):
         keys = row_keys(g, rows, span)
+        lanes = pl.ds(pl.multiple_of(g * span, span), span)
         masks = []
         for m in range(PEERS):
-            row = key_ref[pl.ds(expert_of(me ^ m, z), 1), g * span : (g + 1) * span]
+            row = key_ref[pl.ds(expert_of(me ^ m, z), 1), lanes]
             masks.append(jnp.where(row == keys, 1.0, 0.0).astype(BF16))
         mask = jnp.concatenate(masks, axis=0)
+        to = pl.ds(pl.multiple_of(g * part, part), part)
 
         def columns(c, _):
             here = pl.ds(pl.multiple_of(c * 512, 512), 512)
-            y = dot(mask, tok[g * span : (g + 1) * span, here], ((1,), (0,)))
+            y = dot(mask, tok[lanes, here], ((1,), (0,)))
             for m, out in enumerate(outs):
-                out[g * part : (g + 1) * part, here] = y[m * part : (m + 1) * part, :].astype(BF16)
+                out[to, here] = y[m * part : (m + 1) * part, :].astype(BF16)
             return 0
 
         lax.fori_loop(0, wide // 512, columns, 0)
+        return 0
+
+    lax.fori_loop(0, ZS // NEAR, one, 0)
 
 
 def pack(place, blocks, wide, experts, rows):
@@ -98,7 +115,7 @@
         in_specs=[pl.BlockSpec(memory_space=pltpu.SMEM)] + [vm] * ZS,
         out_specs=[vm] * (PEERS + 3),
         out_shape=[shape] * PEERS + [small] * 3,
-        scratch_shapes=[pltpu.VMEM((ZS * toks, wide), BF16)],
+        scratch_shapes=[pltpu.VMEM((ZS * toks, wide), BF16), pltpu.VMEM((ZS, toks, 128), F32)],
         name="pack",
     )(place, *blocks)
 
@@ -178,28 +195,27 @@
         xs[m * part : (m + 1) * part, :] = xin[m][...]
 
     me = place_ref[0]
-    total = wg.shape[0]
-    cuts = [(0, 512), (512, half), (half, half + 512), (half + 512, total)]
-    for n, (lo, hi) in enumerate(cuts):
-        if n == 0:
-            for copy in copies[:3]:
-                copy.wait()
-        if n == 2:
+    acc[...] = jnp.zeros_like(acc)
+    for copy in copies[:3]:
+        copy.wait()
+
+    def run(n, _):
+        @pl.when(n == 1)
+        def _():
             for copy in copies[3:]:
                 copy.wait()
+
+        here = pl.ds(pl.multiple_of(n * half, half), half)
         x = xs[...]
-        gate = dot(x, wg[lo:hi, :], ((1,), (1,)))
-        upper = dot(x, wu[lo:hi, :], ((1,), (1,)))
+        gate = dot(x, wg[here, :], ((1,), (1,)))
+        upper = dot(x, wu[here, :], ((1,), (1,)))
         hidden = (gate / (1.0 + jnp.exp(-gate)) * upper).astype(BF16)
-        res = dot(hidden, wd[lo:hi, :], ((1,), (0,)))
-        if n == 0:
-            acc[...] = res
-        elif n < len(cuts) - 1:
-            acc[...] = acc[...] + res
-        else:
-            acc[...] = acc[...] + res
-            for m in range(PEERS):
-                o_ref[me ^ m] = acc[m * part : (m + 1) * part, :].astype(BF16)
+        acc[...] = acc[...] + dot(hidden, wd[here, :], ((1,), (0,)))
+        return 0
+
+    lax.fori_loop(0, 2, run, 0)
+    for m in range(PEERS):
+        o_ref[me ^ m] = acc[m * part : (m + 1) * part, :].astype(BF16)
 
 
 def expert(place, x, own, first, second, group, rows):
@@ -234,49 +250,87 @@
     )(place, *x, *own, *first, *second)
 
 
-def out_kernel(index_ref, in_ref, out_ref):
+def leave_kernel(place_ref, table_ref, in_ref, same_ref, cross_ref, used):
+    z, x, column = place_ref[1], place_ref[2], place_ref[3]
+    blk_dev = in_ref.shape[1]
+
+    def clear(p, _):
+        used[p] = 0
+        return 0
+
+    lax.fori_loop(0, 2 * ZS, clear, 0)
+
     def one(i, _):
-        out_ref[i] = in_ref[:, index_ref[i]]
-        return 0
-
-    lax.fori_loop(0, out_ref.shape[0], one, 0)
-
-
-def gather_out(index, cache):
+        dest = table_ref[column, (x * ZS + z) * blk_dev + i] // blk_dev
+        rank = used[dest]
+        used[dest] = rank + 1
+        far = dest & (ZS - 1)
+
+        @pl.when(dest // ZS == x)
+        def _():
+            same_ref[far, rank] = in_ref[:, i]
+
+        @pl.when(dest // ZS != x)
+        def _():
+            cross_ref[(far - z) & (ZS - 1), rank] = in_ref[:, i]
+
+        return 0
+
+    lax.fori_loop(0, blk_dev, one, 0)
+
+
+def gather_out(place, table, cache, spare):
     layers, _, blk, wide = cache.shape
-    slots = index.shape[0]
+    smem = pl.BlockSpec(memory_space=pltpu.SMEM)
+    vm = pl.BlockSpec(memory_space=pltpu.VMEM)
+    shape = jax.ShapeDtypeStruct((ZS, spare, layers, blk, wide), cache.dtype)
+    return pl.pallas_call(
+        leave_kernel,
+        in_specs=[smem, smem, vm],
+        out_specs=[vm, vm],
+        out_shape=[shape, shape],
+        scratch_shapes=[pltpu.SMEM((2 * ZS,), jnp.int32)],
+        name="gather_out",
+    )(place, table, cache)
+
+
+def arrive_kernel(place_ref, slot_ref, same_ref, *refs):
+    crossed, out_ref = refs[:ZS], refs[ZS]
+    z, x = place_ref[1], place_ref[2]
+    spare = same_ref.shape[1]
+
+    def put(source, i, ref):
+        to = slot_ref[source * spare + i]
+
+        @pl.when(to >= 0)
+        def _():
+            out_ref[:, to] = ref[...]
+
+    def one(n, _):
+        for i in range(spare):
+            put(x * ZS + n, i, same_ref.at[n, i])
+        return 0
+
+    lax.fori_loop(0, ZS, one, 0)
+    for n in range(ZS):
+        for i in range(spare):
+            put((1 - x) * ZS + ((z - n) & (ZS - 1)), i, crossed[n].at[i])
+
+
+def gather_in(place, slots, same, crossed, blk_dev):
+    _, _, layers, blk, wide = same.shape
+    smem = pl.BlockSpec(memory_space=pltpu.SMEM)
     vm = pl.BlockSpec(memory_space=pltpu.VMEM)
     return pl.pallas_call(
-        out_kernel,
-        in_specs=[pl.BlockSpec(memory_space=pltpu.SMEM), vm],
+        arrive_kernel,
+        in_specs=[smem, smem] + [vm] * (ZS + 1),
         out_specs=vm,
-        out_shape=jax.ShapeDtypeStruct((slots, layers, blk, wide), cache.dtype),
-        name="gather_out",
-    )(index, cache)
-
-
-def in_kernel(index_ref, in_ref, out_ref):
-    def one(i, _):
-        out_ref[:, i] = in_ref[index_ref[i]]
-        return 0
-
-    lax.fori_loop(0, out_ref.shape[1], one, 0)
-
-
-def gather_in(index, arrived):
-    slots = index.shape[0]
-    _, layers, blk, wide = arrived.shape
-    vm = pl.BlockSpec(memory_space=pltpu.VMEM)
-    return pl.pallas_call(
-        in_kernel,
-        in_specs=[pl.BlockSpec(memory_space=pltpu.SMEM), vm],
-        out_specs=vm,
-        out_shape=jax.ShapeDtypeStruct((layers, slots, blk, wide), arrived.dtype),
+        out_shape=jax.ShapeDtypeStruct((layers, blk_dev, blk, wide), same.dtype),
         name="gather_in",
-    )(index, arrived)
-
-
-def handover_indices(handover_table, sources, blk_dev, spare):
+    )(place, slots, same, *crossed)
+
+
+def arrival_slots(handover_table, sources, blk_dev, spare):
     column = lax.dynamic_index_in_dim(handover_table, lax.axis_index("tp"), 0, keepdims=False)
     here = lax.axis_index("pre")
     table = column.reshape(sources, blk_dev)
@@ -284,23 +338,11 @@
     earlier = jnp.arange(blk_dev)[:, None] < jnp.arange(blk_dev)[None, :]
     same = dest[:, :, None] == dest[:, None, :]
     rank = jnp.sum((same & earlier[None]).astype(jnp.int32), axis=1)
-    my_dest = lax.dynamic_index_in_dim(dest, here, 0, keepdims=False)
-    my_rank = lax.dynamic_index_in_dim(rank, here, 0, keepdims=False)
     wanted = jnp.arange(sources * spare, dtype=jnp.int32)
-    out_index = jnp.sum(
-        jnp.where(
-            wanted[:, None] == (my_dest * spare + my_rank)[None, :],
-            jnp.arange(blk_dev, dtype=jnp.int32)[None, :],
-            0,
-        ),
-        axis=1,
-    )
-    place = here * blk_dev + jnp.arange(blk_dev, dtype=jnp.int32)
     came = jnp.arange(sources, dtype=jnp.int32)[:, None] * spare + rank
-    in_index = jnp.sum(
-        jnp.where(place[:, None, None] == table[None], came[None], 0), axis=(1, 2)
-    )
-    return out_index, in_index
+    came = jnp.where(dest == here, came, -1).reshape(-1)
+    slots = jnp.where(wanted[:, None] == came[None, :], (column % blk_dev + 1)[None, :], 0)
+    return jnp.sum(slots, axis=1) - 1
 
 
 def shards(
@@ -350,7 +392,7 @@
     here = lax.axis_index("pre")
     there = lax.axis_index("tp")
     me = (here // ZS) * 4 + there // 2
-    place = jnp.stack([me, here % ZS]).astype(jnp.int32)
+    place = jnp.stack([me, here % ZS, here // ZS, there]).astype(jnp.int32)
     *packed, keys, whi, wlo = pack(place, blocks, wide, experts_all, rows)
 
     def kind_of(group):
@@ -403,10 +445,25 @@
     _, _, blk_dev, _, _ = prefill_cache.shape
     sources = lax.axis_size("pre")
     spare = blk_dev // sources + 1
-    out_index, in_index = handover_indices(handover_table, sources, blk_dev, spare)
-    leaving = gather_out(out_index, prefill_cache[:, 0])
-    arrived = lax.all_to_all(leaving, "pre", split_axis=0, concat_axis=0, tiled=True)
-    decode_cache = gather_in(in_index, arrived)[:, None]
+    in_slots = arrival_slots(handover_table, sources, blk_dev, spare)
+    same, cross = gather_out(place, handover_table, prefill_cache[:, 0], spare)
+    cross = lax.ppermute(cross, "pre", [(i, (i + ZS) % sources) for i in range(sources)])
+    same = lax.all_to_all(
+        same,
+        "pre",
+        split_axis=0,
+        concat_axis=0,
+        axis_index_groups=[list(range(x * ZS, (x + 1) * ZS)) for x in range(sources // ZS)],
+        tiled=True,
+    )
+    crossed = [cross[0]]
+    for n in range(1, ZS):
+        crossed.append(
+            lax.ppermute(
+                cross[n], "pre", [(i, i // ZS * ZS + (i + n) % ZS) for i in range(sources)]
+            )
+        )
+    decode_cache = gather_in(place, in_slots, same, crossed, blk_dev)[:, None]
     return (moe_output, decode_cache)
 
 

time: 357 us -> 394 us (1.10)
  waiting for transfers between devices: 235 us -> 254 us
  starting transfers between devices: 55 us -> 62 us
  local copies, waits for them, and re-layouts: 7.39 us -> 13 us
    ppermute x4, waiting for transfers between devices: 99.5 us -> 27.8 us  [shards(): rising = lax.ppermute(rising, 'pre', up)]
    ppermute x0 -> x8, waiting for transfers between devices: none -> 50.7 us  [the longest x7 25.8 us: shards(): lax.ppermute(cross[n], 'pre', [(i, i // ZS * ZS + (i + n) % ZS) for i in...]
    ppermute x3, waiting for transfers between devices: 0.01 us -> 43.8 us  [shards(): falling = lax.ppermute(falling, 'pre', down)]
    ppermute x0 -> x8, starting transfers between devices: none -> 9.28 us  [the longest x7 7.34 us: shards(): lax.ppermute(cross[n], 'pre', [(i, i // ZS * ZS + (i + n) % ZS) for i in...]
  transfers between devices with their start and end apart: 30 -> 38, of which waited for: 18 -> 23; matrix products, arithmetic and copies ran while one was open for 1% -> 2% of each run, Pallas kernels for 10% -> 10%
where the time goes in v5:
time: 394 us; the launch traced here: 392 us
  waiting for transfers between devices  254 us (64%)
  starting transfers between devices  62 us (16%)
  Pallas kernels  54.9 us (14%)
  local copies, waits for them, and re-layouts  13 us (3%)
  other arithmetic  6.66 us (2%)
    ppermute x3, waiting for transfers between devices, shards(): got = lax.ppermute(piece, 'tp', swap)  47.7 us
    ppermute x7, waiting for transfers between devices, shards(): lax.ppermute(packed[m], ('pre', 'tp'), [(g, peer_of(g, m)) for g in range...  45.9 us
    ppermute x3, waiting for transfers between devices, shards(): falling = lax.ppermute(falling, 'pre', down)  43.8 us
    pallas_call x2, Pallas kernels, expert(): pl.pallas_call(expert_kernel, grid=(1,), in_specs=[pl.BlockSpec(memory_sp...  28.2 us
    ppermute x4, waiting for transfers between devices, shards(): rising = lax.ppermute(rising, 'pre', up)  27.8 us
    ppermute x7, waiting for transfers between devices, shards(): lax.ppermute(cross[n], 'pre', [(i, i // ZS * ZS + (i + n) % ZS) for i in...  25.8 us
    ppermute x1, waiting for transfers between devices, shards(): lax.ppermute(cross, 'pre', [(i, (i + ZS) % sources) for i in range(source...  24.8 us
    all_to_all x2, waiting for transfers between devices, shards(): lax.all_to_all(result, ('pre', 'tp'), split_axis=0, concat_axis=0, axis_i...  21.3 us
  transfers between devices with their start and end apart: 38, of which 23 were waited for; matrix products, arithmetic and copies ran while one was open for 2% of the time, Pallas kernels for 10%

profile of v5, /device:TPU:96, one launch (start us, length us, event | category | flops | bytes accessed | tf_op | source)
XLA Modules:
  0.0 391.8 jit_solution(2764210486722567154)
XLA Ops:
  11.0 5.1 %collective-permute-done.refs_5_ = bf16[64,2176]{1,0:T(8,128)(2,1)S(1)} collective-permute-done((bf16[64,2176]{1,0:T(8,128)(2,1)S(1)}, bf16[64,2176]{1,0:T(8,128)(2,1)S(1)}, u32[]{:S(2)}, u32[]{:S(2)}) %collective-permute-start) | collective-permute-done | bytes 278560 | tf_op jit(solution)/shard_map/ppermute | solution.py:387
  40.0 9.0 %pack.1 = (bf16[96,2048]{1,0:T(8,128)(2,1)}, bf16[96,2048]{1,0:T(8,128)(2,1)}, bf16[96,2048]{1,0:T(8,128)(2,1)}, bf16[96,2048]{1,0:T(8,128)(2,1)}, bf16[96,2048]...) custom-call(s32[4]{0:T(128)} %pad_add_fusion.place_ref, ...), custom_call_target="tpu_custom_call" | custom-call | tf_op jit(solution)/shard_map/pack/pallas_call | solution.py:113
  51.2 17.9 %collective-permute-done.15.refs_12_ = bf16[352,2048]{1,0:T(8,128)(2,1)} collective-permute-done((bf16[352,2048]{1,0:T(8,128)(2,1)S(1)}, bf16[352,2048]{1,0:T(8,128)(2,1)}, u32[]{:S(2)}, u32[]{:S(2)}) %collective-permute-start.15) | collective-permute-done | bytes 1441824 | tf_op jit(solution)/shard_map/ppermute | solution.py:373
  69.1 29.8 %collective-permute-done.14.refs_11_ = bf16[352,2048]{1,0:T(8,128)(2,1)} collective-permute-done((bf16[352,2048]{1,0:T(8,128)(2,1)S(1)}, bf16[352,2048]{1,0:T(8,128)(2,1)}, u32[]{:S(2)}, u32[]{:S(2)}) %collective-permute-start.14) | collective-permute-done | bytes 1441824 | tf_op jit(solution)/shard_map/ppermute | solution.py:373
  104.9 7.7 %collective-permute-done.8.refs_2_ = bf16[96,2048]{1,0:T(8,128)(2,1)S(1)} collective-permute-done((bf16[96,2048]{1,0:T(8,128)(2,1)}, bf16[96,2048]{1,0:T(8,128)(2,1)S(1)}, u32[]{:S(2)}, u32[]{:S(2)}) %collective-permute-start.8) | collective-permute-done | bytes 393248 | tf_op jit(solution)/shard_map/ppermute | solution.py:410
  114.1 9.4 %collective-permute-done.9.refs_3_ = bf16[96,2048]{1,0:T(8,128)(2,1)S(1)} collective-permute-done((bf16[96,2048]{1,0:T(8,128)(2,1)}, bf16[96,2048]{1,0:T(8,128)(2,1)S(1)}, u32[]{:S(2)}, u32[]{:S(2)}) %collective-permute-start.9) | collective-permute-done | bytes 393248 | tf_op jit(solution)/shard_map/ppermute | solution.py:410
  124.6 4.9 %collective-permute-done.10.refs_4_ = bf16[96,2048]{1,0:T(8,128)(2,1)S(1)} collective-permute-done((bf16[96,2048]{1,0:T(8,128)(2,1)}, bf16[96,2048]{1,0:T(8,128)(2,1)S(1)}, u32[]{:S(2)}, u32[]{:S(2)}) %collective-permute-start.10) | collective-permute-done | bytes 393248 | tf_op jit(solution)/shard_map/ppermute | solution.py:410
  130.0 9.9 %collective-permute-done.11.refs_5_ = bf16[96,2048]{1,0:T(8,128)(2,1)S(1)} collective-permute-done((bf16[96,2048]{1,0:T(8,128)(2,1)}, bf16[96,2048]{1,0:T(8,128)(2,1)S(1)}, u32[]{:S(2)}, u32[]{:S(2)}) %collective-permute-start.11) | collective-permute-done | bytes 393248 | tf_op jit(solution)/shard_map/ppermute | solution.py:410
  141.1 13.0 %collective-permute-done.13.refs_7_ = bf16[96,2048]{1,0:T(8,128)(2,1)S(1)} collective-permute-done((bf16[96,2048]{1,0:T(8,128)(2,1)}, bf16[96,2048]{1,0:T(8,128)(2,1)S(1)}, u32[]{:S(2)}, u32[]{:S(2)}) %collective-permute-start.13) | collective-permute-done | bytes 393248 | tf_op jit(solution)/shard_map/ppermute | solution.py:410
  155.9 14.1 %expert.2 = bf16[8,48,2048]{2,1,0:T(8,128)(2,1)} custom-call(s32[4]{0:T(128)} %pad_add_fusion.place_ref, bf16[96,2048]{1,0:T(8,128)(2,1)} %get-tuple-element.26.refs_0_, bf16[96,2048]{1,0:T(8,128)(2,1)} %copy-done.24, bf16[96,2048]{1,0:T(8,128)(2,1)} %copy-done.25, bf16[96,2048]{1,0:T(8,128)(2,1)} %copy-done.26, bf16[96,2048]{1,0:T(8,128)(2,1)} %copy-done.27, ...), custom_call_target="tpu_custom_call" | custom-call | flops 6643777536 | bytes 20447232 | tf_op jit(solution)/shard_map/expert/pallas_call | solution.py:227
  173.6 14.1 %expert.3 = bf16[8,48,2048]{2,1,0:T(8,128)(2,1)} custom-call(s32[4]{0:T(128)} %pad_add_fusion.place_ref, bf16[96,2048]{1,0:T(8,128)(2,1)} %get-tuple-element.26.refs_0_, bf16[96,2048]{1,0:T(8,128)(2,1)} %copy-done.24, bf16[96,2048]{1,0:T(8,128)(2,1)} %copy-done.25, bf16[96,2048]{1,0:T(8,128)(2,1)} %copy-done.26, bf16[96,2048]{1,0:T(8,128)(2,1)} %copy-done.27, ...), custom_call_target="tpu_custom_call" | custom-call | flops 6643777536 | bytes 20447232 | tf_op jit(solution)/shard_map/expert/pallas_call | solution.py:227
  187.7 7.6 %all-to-all-done = bf16[8,48,2048]{2,1,0:T(8,128)(2,1)S(1)} async-done(((bf16[8,48,2048]{2,1,0:T(8,128)(2,1)}), bf16[8,48,2048]{2,1,0:T(8,128)(2,1)S(1)}, u32[]{:S(2)}, u32[]{:S(2)}) %all-to-all-start) | async-done | bytes 1572896 | tf_op jit(solution)/shard_map/all_to_all | solution.py:423
  207.4 13.7 %all-to-all-done.1 = bf16[8,48,2048]{2,1,0:T(8,128)(2,1)S(1)} async-done(((bf16[8,48,2048]{2,1,0:T(8,128)(2,1)}), bf16[8,48,2048]{2,1,0:T(8,128)(2,1)S(1)}, u32[]{:S(2)}, u32[]{:S(2)}) %all-to-all-start.1) | async-done | bytes 1572896 | tf_op jit(solution)/shard_map/all_to_all | solution.py:423
  222.3 7.7 %all-to-all-start.2 = ((bf16[8,2,2,64,512]{4,3,2,1,0:T(8,128)(2,1)}), bf16[8,2,2,64,512]{4,3,2,1,0:T(8,128)(2,1)S(1)}, u32[]{:S(2)}, u32[]{:S(2)}) async-start(bf16[8,2,2,64,512]{4,3,2,1,0:T(8,128)(2,1)} %get-tuple-element.42), calls=%async_computation.2 | async-start | bytes 4194304 | tf_op jit(solution)/shard_map/all_to_all | solution.py:451
  238.1 24.8 %collective-permute-done.27 = bf16[8,2,2,64,512]{4,3,2,1,0:T(8,128)(2,1)} collective-permute-done((bf16[8,2,2,64,512]{4,3,2,1,0:T(8,128)(2,1)}, bf16[8,2,2,64,512]{4,3,2,1,0:T(8,128)(2,1)}, u32[]{:S(2)}, u32[]{:S(2)}) %collective-permute-start.27) | collective-permute-done | bytes 2097184 | tf_op jit(solution)/shard_map/ppermute | solution.py:450
  266.1 6.4 %collective-permute-start.32 = (bf16[2,2,64,512]{3,2,1,0:T(8,128)(2,1)}, bf16[2,2,64,512]{3,2,1,0:T(8,128)(2,1)}, u32[]{:S(2)}, u32[]{:S(2)}) collective-permute-start(bf16[2,2,64,512]{3,2,1,0:T(8,128)(2,1)} %get-tuple-element.56), channel_id=1, source_target_pairs={{0,80},{16,96},{32,112},{48,0},{64,16},{80,32},{96,48},{112,64},{1... | collective-permute-start | bytes 786440 | tf_op jit(solution)/shard_map/ppermute | solution.py:462
  272.9 4.8 %weigh.3 = (f32[64,2048]{1,0:T(8,128)}, f32[64,2048]{1,0:T(8,128)}, f32[64,2048]{1,0:T(8,128)}, f32[64,2048]{1,0:T(8,128)}) custom-call(s32[4]{0:T(128)} %pad_add_fusion.place_ref, f32[64,512]{1,0:T(8,128)} %get-tuple-element.23.key_ref, f32[64,512]{1,0:T(8,128)} %get-tuple-element.24.whi_ref, f32[64,512]{1,0:T(8,128)} %get-tuple-element.25.wlo_ref, ...), custom_call_target="tpu_custom_call" | custom-call | tf_op jit(solution)/shard_map/weigh/pallas_call | solution.py:153
  277.7 11.8 %collective-permute-done.20 = bf16[64,2048]{1,0:T(8,128)(2,1)} collective-permute-done((bf16[64,2048]{1,0:T(8,128)(2,1)}, bf16[64,2048]{1,0:T(8,128)(2,1)}, u32[]{:S(2)}, u32[]{:S(2)}) %collective-permute-start.20) | collective-permute-done | bytes 262176 | tf_op jit(solution)/shard_map/ppermute | solution.py:436
  290.6 35.6 %collective-permute-done.24 = bf16[64,2048]{1,0:T(8,128)(2,1)S(1)} collective-permute-done((bf16[64,2048]{1,0:T(8,128)(2,1)}, bf16[64,2048]{1,0:T(8,128)(2,1)S(1)}, u32[]{:S(2)}, u32[]{:S(2)}) %collective-permute-start.24) | collective-permute-done | bytes 262176 | tf_op jit(solution)/shard_map/ppermute | solution.py:440
  326.9 7.2 %collective-permute-done.21 = bf16[64,2048]{1,0:T(8,128)(2,1)S(1)} collective-permute-done((bf16[64,2048]{1,0:T(8,128)(2,1)S(1)}, bf16[64,2048]{1,0:T(8,128)(2,1)S(1)}, u32[]{:S(2)}, u32[]{:S(2)}) %collective-permute-start.21) | collective-permute-done | bytes 262176 | tf_op jit(solution)/shard_map/ppermute | solution.py:436
  334.1 8.1 %collective-permute-done.25 = bf16[64,2048]{1,0:T(8,128)(2,1)S(1)} collective-permute-done((bf16[64,2048]{1,0:T(8,128)(2,1)S(1)}, bf16[64,2048]{1,0:T(8,128)(2,1)S(1)}, u32[]{:S(2)}, u32[]{:S(2)}) %collective-permute-start.25) | collective-permute-done | bytes 262176 | tf_op jit(solution)/shard_map/ppermute | solution.py:440
  343.0 8.7 %collective-permute-done.22 = bf16[64,2048]{1,0:T(8,128)(2,1)S(1)} collective-permute-done((bf16[64,2048]{1,0:T(8,128)(2,1)S(1)}, bf16[64,2048]{1,0:T(8,128)(2,1)S(1)}, u32[]{:S(2)}, u32[]{:S(2)}) %collective-permute-start.22) | collective-permute-done | bytes 262176 | tf_op jit(solution)/shard_map/ppermute | solution.py:436
  358.3 13.3 %collective-permute-done.30.refs_3_ = bf16[2,2,64,512]{3,2,1,0:T(8,128)(2,1)S(1)} collective-permute-done((bf16[2,2,64,512]{3,2,1,0:T(8,128)(2,1)S(1)}, bf16[2,2,64,512]{3,2,1,0:T(8,128)(2,1)S(1)}, u32[]{:S(2)}, u32[]{:S(2)}) %collective-permute-start.30) | collective-permute-done | bytes 262176 | tf_op jit(solution)/shard_map/ppermute | solution.py:462
  371.6 8.2 %collective-permute-done.29.refs_2_ = bf16[2,2,64,512]{3,2,1,0:T(8,128)(2,1)S(1)} collective-permute-done((bf16[2,2,64,512]{3,2,1,0:T(8,128)(2,1)S(1)}, bf16[2,2,64,512]{3,2,1,0:T(8,128)(2,1)S(1)}, u32[]{:S(2)}, u32[]{:S(2)}) %collective-permute-start.29) | collective-permute-done | bytes 262176 | tf_op jit(solution)/shard_map/ppermute | solution.py:462
  (149 shorter events, 97.9 us)
Async XLA Ops:
  3.4 47.8 %collective-permute-start.16 = (bf16[352,2048]{1,0:T(8,128)(2,1)}, bf16[352,2048]{1,0:T(8,128)(2,1)}, u32[]{:S(2)}, u32[]{:S(2)}) collective-permute-start(bf16[352,2048]{1,0:T(8,128)(2,1)} %constant_dynamic-slice_fusion.1), channel_id=1, source_target_pairs={{0,2},{2,0},{4,6},{6,4},{8,10},{10,8},{12,14},{14,12},{1,3},{3,1},... | collective-permute-start | bytes 4325384 | tf_op jit(solution)/shard_map/ppermute | solution.py:373
  5.2 63.9 %collective-permute-start.15 = (bf16[352,2048]{1,0:T(8,128)(2,1)S(1)}, bf16[352,2048]{1,0:T(8,128)(2,1)}, u32[]{:S(2)}, u32[]{:S(2)}) collective-permute-start(bf16[352,2048]{1,0:T(8,128)(2,1)S(1)} %dynamic-slice_bitcast_fusion), channel_id=1, source_target_pairs={{0,2},{2,0},{4,6},{6,4},{8,10},{10,8},{12,14},{14,12},{1,3},{3,1},... | collective-permute-start | bytes 4325384 | tf_op jit(solution)/shard_map/ppermute | solution.py:373
  5.9 93.0 %collective-permute-start.14 = (bf16[352,2048]{1,0:T(8,128)(2,1)S(1)}, bf16[352,2048]{1,0:T(8,128)(2,1)}, u32[]{:S(2)}, u32[]{:S(2)}) collective-permute-start(bf16[352,2048]{1,0:T(8,128)(2,1)S(1)} %dynamic-slice_bitcast_fusion.1), channel_id=1, source_target_pairs={{0,2},{2,0},{4,6},{6,4},{8,10},{10,8},{12,14},{14,12},{1,3},{3,1},... | collective-permute-start | bytes 4325384 | tf_op jit(solution)/shard_map/ppermute | solution.py:373
  49.0 52.9 %collective-permute-start.7 = (bf16[96,2048]{1,0:T(8,128)(2,1)}, bf16[96,2048]{1,0:T(8,128)(2,1)S(1)}, u32[]{:S(2)}, u32[]{:S(2)}) collective-permute-start(bf16[96,2048]{1,0:T(8,128)(2,1)} %get-tuple-element.27), channel_id=1, source_target_pairs={{0,6},{2,4},{4,2},{6,0},{8,14},{10,12},{12,10},{14,8},{16,22},{18,... | collective-permute-start | bytes 1179656 | tf_op jit(solution)/shard_map/ppermute | solution.py:410
  51.2 102.9 %collective-permute-start.19 = (bf16[352,2048]{1,0:T(8,128)(2,1)}, bf16[352,2048]{1,0:T(8,128)(2,1)}, u32[]{:S(2)}, u32[]{:S(2)}) collective-permute-start(bf16[352,2048]{1,0:T(8,128)(2,1)} %collective-permute-done.16.refs_13_), channel_id=1, source_target_pairs={{0,1},{1,0},{2,3},{3,2},{4,5},{5,4},{6,7},{7,6},{8,9},{9,8},{10,11... | collective-permute-start | bytes 4325384 | tf_op jit(solution)/shard_map/ppermute | solution.py:375
  69.1 85.0 %collective-permute-start.18 = (bf16[352,2048]{1,0:T(8,128)(2,1)}, bf16[352,2048]{1,0:T(8,128)(2,1)S(1)}, u32[]{:S(2)}, u32[]{:S(2)}) collective-permute-start(bf16[352,2048]{1,0:T(8,128)(2,1)} %collective-permute-done.15.refs_12_), channel_id=1, source_target_pairs={{0,1},{1,0},{2,3},{3,2},{4,5},{5,4},{6,7},{7,6},{8,9},{9,8},{10,11... | collective-permute-start | bytes 4325384 | tf_op jit(solution)/shard_map/ppermute | solution.py:375
  98.9 55.3 %collective-permute-start.17 = (bf16[352,2048]{1,0:T(8,128)(2,1)}, bf16[352,2048]{1,0:T(8,128)(2,1)S(1)}, u32[]{:S(2)}, u32[]{:S(2)}) collective-permute-start(bf16[352,2048]{1,0:T(8,128)(2,1)} %collective-permute-done.14.refs_11_), channel_id=1, source_target_pairs={{0,1},{1,0},{2,3},{3,2},{4,5},{5,4},{6,7},{7,6},{8,9},{9,8},{10,11... | collective-permute-start | bytes 4325384 | tf_op jit(solution)/shard_map/ppermute | solution.py:375
  101.9 21.6 %collective-permute-start.9 = (bf16[96,2048]{1,0:T(8,128)(2,1)}, bf16[96,2048]{1,0:T(8,128)(2,1)S(1)}, u32[]{:S(2)}, u32[]{:S(2)}) collective-permute-start(bf16[96,2048]{1,0:T(8,128)(2,1)} %get-tuple-element.29), channel_id=1, source_target_pairs={{0,14},{2,12},{4,10},{6,8},{8,6},{10,4},{12,2},{14,0},{16,30},{18,... | collective-permute-start | bytes 1179656 | tf_op jit(solution)/shard_map/ppermute | solution.py:410
  112.6 16.9 %collective-permute-start.10 = (bf16[96,2048]{1,0:T(8,128)(2,1)}, bf16[96,2048]{1,0:T(8,128)(2,1)S(1)}, u32[]{:S(2)}, u32[]{:S(2)}) collective-permute-start(bf16[96,2048]{1,0:T(8,128)(2,1)} %get-tuple-element.30), channel_id=1, source_target_pairs={{0,128},{2,130},{4,132},{6,134},{8,136},{10,138},{12,140},{14,142}... | collective-permute-start | bytes 1179656 | tf_op jit(solution)/shard_map/ppermute | solution.py:410
  170.0 25.3 %all-to-all-start = ((bf16[8,48,2048]{2,1,0:T(8,128)(2,1)}), bf16[8,48,2048]{2,1,0:T(8,128)(2,1)S(1)}, u32[]{:S(2)}, u32[]{:S(2)}) async-start(bf16[8,48,2048]{2,1,0:T(8,128)(2,1)} %expert.2), calls=%async_computation | async-start | bytes 3145728 | tf_op jit(solution)/shard_map/all_to_all | solution.py:423
  196.5 24.6 %all-to-all-start.1 = ((bf16[8,48,2048]{2,1,0:T(8,128)(2,1)}), bf16[8,48,2048]{2,1,0:T(8,128)(2,1)S(1)}, u32[]{:S(2)}, u32[]{:S(2)}) async-start(bf16[8,48,2048]{2,1,0:T(8,128)(2,1)} %expert.3), calls=%async_computation.1 | async-start | bytes 3145728 | tf_op jit(solution)/shard_map/all_to_all | solution.py:423
  204.5 58.4 %collective-permute-start.27 = (bf16[8,2,2,64,512]{4,3,2,1,0:T(8,128)(2,1)}, bf16[8,2,2,64,512]{4,3,2,1,0:T(8,128)(2,1)}, u32[]{:S(2)}, u32[]{:S(2)}) collective-permute-start(bf16[8,2,2,64,512]{4,3,2,1,0:T(8,128)(2,1)} %get-tuple-element.43), channel_id=1, source_target_pairs={{0,128},{16,144},{32,160},{48,176},{64,192},{80,208},{96,224},{112... | collective-permute-start | bytes 6291464 | tf_op jit(solution)/shard_map/ppermute | solution.py:450
  222.3 162.5 %all-to-all-start.2 = ((bf16[8,2,2,64,512]{4,3,2,1,0:T(8,128)(2,1)}), bf16[8,2,2,64,512]{4,3,2,1,0:T(8,128)(2,1)S(1)}, u32[]{:S(2)}, u32[]{:S(2)}) async-start(bf16[8,2,2,64,512]{4,3,2,1,0:T(8,128)(2,1)} %get-tuple-element.42), calls=%async_computation.2 | async-start | bytes 4194304 | tf_op jit(solution)/shard_map/all_to_all | solution.py:451
  235.4 54.1 %collective-permute-start.20 = (bf16[64,2048]{1,0:T(8,128)(2,1)}, bf16[64,2048]{1,0:T(8,128)(2,1)}, u32[]{:S(2)}, u32[]{:S(2)}) collective-permute-start(bf16[64,2048]{1,0:T(8,128)(2,1)} %get-tuple-element.34), channel_id=1, source_target_pairs={{0,16},{16,32},{32,48},{48,64},{64,80},{80,96},{96,112},{112,0},{1... | collective-permute-start | bytes 786440 | tf_op jit(solution)/shard_map/ppermute | solution.py:436
  265.6 86.9 %collective-permute-start.34 = (bf16[2,2,64,512]{3,2,1,0:T(8,128)(2,1)}, bf16[2,2,64,512]{3,2,1,0:T(8,128)(2,1)}, u32[]{:S(2)}, u32[]{:S(2)}) collective-permute-start(bf16[2,2,64,512]{3,2,1,0:T(8,128)(2,1)} %get-tuple-element.54), channel_id=1, source_target_pairs={{0,112},{16,0},{32,16},{48,32},{64,48},{80,64},{96,80},{112,96},{1... | collective-permute-start | bytes 786440 | tf_op jit(solution)/shard_map/ppermute | solution.py:462
  266.1 86.5 %collective-permute-start.33 = (bf16[2,2,64,512]{3,2,1,0:T(8,128)(2,1)}, bf16[2,2,64,512]{3,2,1,0:T(8,128)(2,1)}, u32[]{:S(2)}, u32[]{:S(2)}) collective-permute-start(bf16[2,2,64,512]{3,2,1,0:T(8,128)(2,1)} %get-tuple-element.55), channel_id=1, source_target_pairs={{0,96},{16,112},{32,0},{48,16},{64,32},{80,48},{96,64},{112,80},{1... | collective-permute-start | bytes 786440 | tf_op jit(solution)/shard_map/ppermute | solution.py:462
  266.1 86.6 %collective-permute-start.32 = (bf16[2,2,64,512]{3,2,1,0:T(8,128)(2,1)}, bf16[2,2,64,512]{3,2,1,0:T(8,128)(2,1)}, u32[]{:S(2)}, u32[]{:S(2)}) collective-permute-start(bf16[2,2,64,512]{3,2,1,0:T(8,128)(2,1)} %get-tuple-element.56), channel_id=1, source_target_pairs={{0,80},{16,96},{32,112},{48,0},{64,16},{80,32},{96,48},{112,64},{1... | collective-permute-start | bytes 786440 | tf_op jit(solution)/shard_map/ppermute | solution.py:462
  272.5 82.2 %collective-permute-start.31 = (bf16[2,2,64,512]{3,2,1,0:T(8,128)(2,1)}, bf16[2,2,64,512]{3,2,1,0:T(8,128)(2,1)}, u32[]{:S(2)}, u32[]{:S(2)}) collective-permute-start(bf16[2,2,64,512]{3,2,1,0:T(8,128)(2,1)} %get-tuple-element.57), channel_id=1, source_target_pairs={{0,64},{16,80},{32,96},{48,112},{64,0},{80,16},{96,32},{112,48},{1... | collective-permute-start | bytes 786440 | tf_op jit(solution)/shard_map/ppermute | solution.py:462
  289.5 36.7 %collective-permute-start.24 = (bf16[64,2048]{1,0:T(8,128)(2,1)}, bf16[64,2048]{1,0:T(8,128)(2,1)S(1)}, u32[]{:S(2)}, u32[]{:S(2)}) collective-permute-start(bf16[64,2048]{1,0:T(8,128)(2,1)} %get-tuple-element.38), channel_id=1, source_target_pairs={{16,0},{32,16},{48,32},{64,48},{80,64},{96,80},{112,96},{0,112},{1... | collective-permute-start | bytes 786440 | tf_op jit(solution)/shard_map/ppermute | solution.py:440
  351.8 19.9 %collective-permute-start.30 = (bf16[2,2,64,512]{3,2,1,0:T(8,128)(2,1)S(1)}, bf16[2,2,64,512]{3,2,1,0:T(8,128)(2,1)S(1)}, u32[]{:S(2)}, u32[]{:S(2)}) collective-permute-start(bf16[2,2,64,512]{3,2,1,0:T(8,128)(2,1)S(1)} %copy-done.16), channel_id=1, source_target_pairs={{0,48},{16,64},{32,80},{48,96},{64,112},{80,0},{96,16},{112,32},{1... | collective-permute-start | bytes 786440 | tf_op jit(solution)/shard_map/ppermute | solution.py:462
  352.5 27.3 %collective-permute-start.29 = (bf16[2,2,64,512]{3,2,1,0:T(8,128)(2,1)S(1)}, bf16[2,2,64,512]{3,2,1,0:T(8,128)(2,1)S(1)}, u32[]{:S(2)}, u32[]{:S(2)}) collective-permute-start(bf16[2,2,64,512]{3,2,1,0:T(8,128)(2,1)S(1)} %copy-done.15), channel_id=1, source_target_pairs={{0,32},{16,48},{32,64},{48,80},{64,96},{80,112},{96,0},{112,16},{1... | collective-permute-start | bytes 786440 | tf_op jit(solution)/shard_map/ppermute | solution.py:462
  352.5 32.2 %collective-permute-start.28 = (bf16[2,2,64,512]{3,2,1,0:T(8,128)(2,1)S(1)}, bf16[2,2,64,512]{3,2,1,0:T(8,128)(2,1)}, u32[]{:S(2)}, u32[]{:S(2)}) collective-permute-start(bf16[2,2,64,512]{3,2,1,0:T(8,128)(2,1)S(1)} %get-tuple-element.60), channel_id=1, source_target_pairs={{0,16},{16,32},{32,48},{48,64},{64,80},{80,96},{96,112},{112,0},{1... | collective-permute-start | bytes 786440 | tf_op jit(solution)/shard_map/ppermute | solution.py:462
  352.6 37.4 %collective-permute-start.26 = (bf16[64,2048]{1,0:T(8,128)(2,1)}, bf16[64,2048]{1,0:T(8,128)(2,1)S(1)}, u32[]{:S(2)}, u32[]{:S(2)}) collective-permute-start(bf16[64,2048]{1,0:T(8,128)(2,1)} %add_convert_fusion.1), channel_id=1, source_target_pairs={{16,0},{32,16},{48,32},{64,48},{80,64},{96,80},{112,96},{0,112},{1... | collective-permute-start | bytes 786440 | tf_op jit(solution)/shard_map/ppermute | solution.py:440
  354.6 35.4 %collective-permute-start.23 = (bf16[64,2048]{1,0:T(8,128)(2,1)}, bf16[64,2048]{1,0:T(8,128)(2,1)}, u32[]{:S(2)}, u32[]{:S(2)}) collective-permute-start(bf16[64,2048]{1,0:T(8,128)(2,1)} %add_convert_fusion.3), channel_id=1, source_target_pairs={{0,16},{16,32},{32,48},{48,64},{64,80},{80,96},{96,112},{112,0},{1... | collective-permute-start | bytes 786440 | tf_op jit(solution)/shard_map/ppermute | solution.py:436
  (45 other events, 683.1 us)

commit v6 on v5

--- a/solution.py
+++ b/solution.py
@@ -32,16 +32,17 @@
     return (peer >> 2) * 32 + z * 4 + (peer & 3)
 
 
-def row_keys(group, rows, lanes):
+def row_keys(rows, lanes):
     index = iota((NEAR * rows, lanes), 0)
     source = divide(index, rows)
-    return ((group * NEAR + source) * 16 + index - source * rows).astype(F32)
-
-
-def pack_kernel(rows, place_ref, *refs):
-    blocks = refs[:ZS]
-    outs = refs[ZS : ZS + PEERS]
-    key_ref, whi_ref, wlo_ref, tok, side = refs[ZS + PEERS :]
+    return (source * 16 + index - source * rows).astype(F32)
+
+
+def pack_kernel(rows, ready, place_ref, *refs):
+    blocks = refs[:NEAR]
+    early = refs[NEAR : NEAR + ready]
+    outs = refs[NEAR + ready : NEAR + ready + PEERS]
+    key_ref, whi_ref, wlo_ref, tok, side, mask = refs[NEAR + ready + PEERS :]
     toks = blocks[0].shape[0]
     wide = tok.shape[1]
     experts = key_ref.shape[0]
@@ -78,65 +79,71 @@
         wlo_ref[:, here] = jnp.concatenate(lows, axis=1)
         return 0
 
-    lax.fori_loop(0, ZS // 2, route, 0)
-    span = NEAR * toks
+    lax.fori_loop(0, NEAR // 2, route, 0)
     part = NEAR * rows
-
-    def one(g, _):
-        keys = row_keys(g, rows, span)
-        lanes = pl.ds(pl.multiple_of(g * span, span), span)
-        masks = []
-        for m in range(PEERS):
-            row = key_ref[pl.ds(expert_of(me ^ m, z), 1), lanes]
-            masks.append(jnp.where(row == keys, 1.0, 0.0).astype(BF16))
-        mask = jnp.concatenate(masks, axis=0)
-        to = pl.ds(pl.multiple_of(g * part, part), part)
-
-        def columns(c, _):
-            here = pl.ds(pl.multiple_of(c * 512, 512), 512)
-            y = dot(mask, tok[lanes, here], ((1,), (0,)))
-            for m, out in enumerate(outs):
-                out[to, here] = y[m * part : (m + 1) * part, :].astype(BF16)
-            return 0
-
-        lax.fori_loop(0, wide // 512, columns, 0)
-        return 0
-
-    lax.fori_loop(0, ZS // NEAR, one, 0)
-
-
-def pack(place, blocks, wide, experts, rows):
+    keys = row_keys(rows, NEAR * toks)
+
+    def fill(m, _):
+        row = key_ref[pl.ds(expert_of(me ^ m, z), 1), :]
+        to = pl.ds(pl.multiple_of(m * part, part), part)
+        mask[to, :] = jnp.where(row == keys, 1.0, 0.0).astype(BF16)
+        return 0
+
+    lax.fori_loop(0, PEERS, fill, 0)
+
+    def columns(c, _):
+        here = pl.ds(pl.multiple_of(c * 512, 512), 512)
+        y = dot(mask[...], tok[:, here], ((1,), (0,)))
+        for m, out in enumerate(outs):
+            out[:part, here] = y[m * part : (m + 1) * part, :].astype(BF16)
+        return 0
+
+    lax.fori_loop(0, wide // 512, columns, 0)
+    for out, ref in zip(outs, early):
+        out[part:, :] = ref[...]
+
+
+def pack(place, blocks, early, wide, experts, rows):
     toks = blocks[0].shape[0]
-    shape = jax.ShapeDtypeStruct((ZS * rows, wide), BF16)
-    small = jax.ShapeDtypeStruct((experts, ZS * toks), F32)
+    groups = 2 if early else 1
+    shape = jax.ShapeDtypeStruct((groups * NEAR * rows, wide), BF16)
+    small = jax.ShapeDtypeStruct((experts, NEAR * toks), F32)
     vm = pl.BlockSpec(memory_space=pltpu.VMEM)
     return pl.pallas_call(
-        functools.partial(pack_kernel, rows),
-        in_specs=[pl.BlockSpec(memory_space=pltpu.SMEM)] + [vm] * ZS,
+        functools.partial(pack_kernel, rows, len(early)),
+        in_specs=[pl.BlockSpec(memory_space=pltpu.SMEM)] + [vm] * (NEAR + len(early)),
         out_specs=[vm] * (PEERS + 3),
         out_shape=[shape] * PEERS + [small] * 3,
-        scratch_shapes=[pltpu.VMEM((ZS * toks, wide), BF16), pltpu.VMEM((ZS, toks, 128), F32)],
+        scratch_shapes=[
+            pltpu.VMEM((NEAR * toks, wide), BF16),
+            pltpu.VMEM((NEAR, toks, 128), F32),
+            pltpu.VMEM((PEERS * NEAR * rows, NEAR * toks), BF16),
+        ],
         name="pack",
-    )(place, *blocks)
-
-
-def weigh_kernel(rows, group, place_ref, key_ref, whi_ref, wlo_ref, ret_ref, *outs):
+    )(place, *blocks, *early)
+
+
+def weigh_kernel(rows, place_ref, key_ref, whi_ref, wlo_ref, ret_ref, *refs):
+    *outs, left = refs
     z = place_ref[1]
     span = key_ref.shape[1]
     toks = outs[0].shape[0]
-    keys = row_keys(group, rows, span)
-    pieces = []
-    for j in range(PEERS):
+    keys = row_keys(rows, span)
+    part = keys.shape[0]
+
+    def fill(j, _):
         e = expert_of(j, z)
+        to = pl.ds(pl.multiple_of(j * part, part), part)
         hit = key_ref[pl.ds(e, 1), :] == keys
-        high = jnp.where(hit, whi_ref[pl.ds(e, 1), :], 0.0).astype(BF16)
-        low = jnp.where(hit, wlo_ref[pl.ds(e, 1), :], 0.0).astype(BF16)
-        pieces.append(jnp.concatenate([high, low], axis=1))
-    left = jnp.concatenate(pieces, axis=0)
+        left[to, :span] = jnp.where(hit, whi_ref[pl.ds(e, 1), :], 0.0).astype(BF16)
+        left[to, span:] = jnp.where(hit, wlo_ref[pl.ds(e, 1), :], 0.0).astype(BF16)
+        return 0
+
+    lax.fori_loop(0, PEERS, fill, 0)
 
     def columns(c, _):
         here = pl.ds(pl.multiple_of(c * 512, 512), 512)
-        y = dot(left, ret_ref[:, here], ((0,), (0,)))
+        y = dot(left[...], ret_ref[:, here], ((0,), (0,)))
         y = y[:span] + y[span:]
         for o, out in enumerate(outs):
             out[:, here] = y[o * toks : (o + 1) * toks, :].astype(out.dtype)
@@ -145,23 +152,17 @@
     lax.fori_loop(0, ret_ref.shape[1] // 512, columns, 0)
 
 
-def weigh(place, keys, whi, wlo, ret, group, rows, kinds):
-    experts, lanes = keys.shape
-    toks = lanes // ZS
-    small = pl.BlockSpec((experts, lanes * NEAR // ZS), lambda i: (0, group))
+def weigh(place, keys, whi, wlo, ret, rows, kinds):
+    _, lanes = keys.shape
+    toks = lanes // NEAR
     wide = ret.shape[1]
+    vm = pl.BlockSpec(memory_space=pltpu.VMEM)
     return pl.pallas_call(
-        functools.partial(weigh_kernel, rows, group),
-        grid=(1,),
-        in_specs=[
-            pl.BlockSpec(memory_space=pltpu.SMEM),
-            small,
-            small,
-            small,
-            pl.BlockSpec(ret.shape, lambda i: (0, 0)),
-        ],
-        out_specs=[pl.BlockSpec((toks, wide), lambda i: (0, 0))] * NEAR,
+        functools.partial(weigh_kernel, rows),
+        in_specs=[pl.BlockSpec(memory_space=pltpu.SMEM)] + [vm] * 4,
+        out_specs=[vm] * NEAR,
         out_shape=[jax.ShapeDtypeStruct((toks, wide), kind) for kind in kinds],
+        scratch_shapes=[pltpu.VMEM((ret.shape[0], 2 * lanes), BF16)],
         name="weigh",
     )(place, keys, whi, wlo, ret)
 
@@ -393,7 +394,10 @@
     there = lax.axis_index("tp")
     me = (here // ZS) * 4 + there // 2
     place = jnp.stack([me, here % ZS, here // ZS, there]).astype(jnp.int32)
-    *packed, keys, whi, wlo = pack(place, blocks, wide, experts_all, rows)
+    *packed, keys, whi, wlo = pack(place, blocks[NEAR:], [], wide, experts_all, rows)
+    routes = [(keys, whi, wlo)]
+    *packed, keys, whi, wlo = pack(place, blocks[:NEAR], packed, wide, experts_all, rows)
+    routes.insert(0, (keys, whi, wlo))
 
     def kind_of(group):
         return (group ^ (group >> 1)) & 1
@@ -429,7 +433,7 @@
             tiled=True,
         )
         kinds = (BF16, BF16, F32, F32) if group == 0 else (F32,) * NEAR
-        sums += weigh(place, keys, whi, wlo, back.reshape(-1, wide), group, rows, kinds)
+        sums += weigh(place, *routes[group], back.reshape(-1, wide), rows, kinds)
 
     rising, falling = sums[0], sums[1]
     for local in (sums[2], sums[4], sums[6], None):
@@ -468,8 +472,6 @@
 
 
 def solution(mesh):
-
-
     return jax.shard_map(
         shards,
         mesh=mesh,

time: 394 us -> 394 us (level)
    pallas_call x3 -> x4, Pallas kernels: 18.3 us -> 20.9 us  [the longest x2 11.4 us: pack(): pl.pallas_call(functools.partial(pack_kernel, rows, len(early)), in_specs...]
  transfers between devices with their start and end apart: 38 -> 38, of which waited for: 23 -> 22; matrix products, arithmetic and copies ran while one was open for 2% -> 2% of each run, Pallas kernels for 10% -> 11%
where the time goes in v6:
time: 394 us; the launch traced here: 392 us
  waiting for transfers between devices  252 us (64%)
  starting transfers between devices  61.8 us (16%)
  Pallas kernels  57.6 us (15%)
  local copies, waits for them, and re-layouts  13 us (3%)
  other arithmetic  6.69 us (2%)
    ppermute x3, waiting for transfers between devices, shards(): got = lax.ppermute(piece, 'tp', swap)  48.9 us
    ppermute x7, waiting for transfers between devices, shards(): lax.ppermute(packed[m], ('pre', 'tp'), [(g, peer_of(g, m)) for g in range...  45.9 us
    ppermute x3, waiting for transfers between devices, shards(): falling = lax.ppermute(falling, 'pre', down)  43.7 us
    pallas_call x2, Pallas kernels, expert(): pl.pallas_call(expert_kernel, grid=(1,), in_specs=[pl.BlockSpec(memory_sp...  28.3 us
    ppermute x4, waiting for transfers between devices, shards(): rising = lax.ppermute(rising, 'pre', up)  27.9 us
    ppermute x7, waiting for transfers between devices, shards(): lax.ppermute(cross[n], 'pre', [(i, i // ZS * ZS + (i + n) % ZS) for i in...  25.8 us
    ppermute x1, waiting for transfers between devices, shards(): lax.ppermute(cross, 'pre', [(i, (i + ZS) % sources) for i in range(source...  24.7 us
    all_to_all x2, waiting for transfers between devices, shards(): lax.all_to_all(result, ('pre', 'tp'), split_axis=0, concat_axis=0, axis_i...  21.2 us
  transfers between devices with their start and end apart: 38, of which 22 were waited for; matrix products, arithmetic and copies ran while one was open for 2% of the time, Pallas kernels for 11%

profile of v6, /device:TPU:96, one launch (start us, length us, event | category | flops | bytes accessed | tf_op | source)
XLA Modules:
  0.0 391.7 jit_solution(5733113780290808078)
XLA Ops:
  11.0 5.1 %collective-permute-done.refs_1_ = bf16[64,2176]{1,0:T(8,128)(2,1)S(1)} collective-permute-done((bf16[64,2176]{1,0:T(8,128)(2,1)S(1)}, bf16[64,2176]{1,0:T(8,128)(2,1)S(1)}, u32[]{:S(2)}, u32[]{:S(2)}) %collective-permute-start) | collective-permute-done | bytes 278560 | tf_op jit(solution)/shard_map/ppermute | solution.py:388
  36.2 5.2 %pack.2 = (bf16[48,2048]{1,0:T(8,128)(2,1)}, bf16[48,2048]{1,0:T(8,128)(2,1)}, bf16[48,2048]{1,0:T(8,128)(2,1)}, bf16[48,2048]{1,0:T(8,128)(2,1)}, bf16[48,2048]...) custom-call(s32[4]{0:T(128)} %pad_add_fusion.place_ref, ...), custom_call_target="tpu_custom_call" | custom-call | tf_op jit(solution)/shard_map/pack/pallas_call | solution.py:112
  41.4 6.3 %pack.3 = (bf16[96,2048]{1,0:T(8,128)(2,1)}, bf16[96,2048]{1,0:T(8,128)(2,1)}, bf16[96,2048]{1,0:T(8,128)(2,1)}, bf16[96,2048]{1,0:T(8,128)(2,1)}, bf16[96,2048]...) custom-call(s32[4]{0:T(128)} %pad_add_fusion.place_ref, ...), custom_call_target="tpu_custom_call" | custom-call | tf_op jit(solution)/shard_map/pack/pallas_call | solution.py:112
  50.0 19.1 %collective-permute-done.15.refs_12_ = bf16[352,2048]{1,0:T(8,128)(2,1)} collective-permute-done((bf16[352,2048]{1,0:T(8,128)(2,1)S(1)}, bf16[352,2048]{1,0:T(8,128)(2,1)}, u32[]{:S(2)}, u32[]{:S(2)}) %collective-permute-start.15) | collective-permute-done | bytes 1441824 | tf_op jit(solution)/shard_map/ppermute | solution.py:374
  69.1 29.8 %collective-permute-done.14.refs_11_ = bf16[352,2048]{1,0:T(8,128)(2,1)} collective-permute-done((bf16[352,2048]{1,0:T(8,128)(2,1)S(1)}, bf16[352,2048]{1,0:T(8,128)(2,1)}, u32[]{:S(2)}, u32[]{:S(2)}) %collective-permute-start.14) | collective-permute-done | bytes 1441824 | tf_op jit(solution)/shard_map/ppermute | solution.py:374
  104.9 7.7 %collective-permute-done.8.refs_2_ = bf16[96,2048]{1,0:T(8,128)(2,1)S(1)} collective-permute-done((bf16[96,2048]{1,0:T(8,128)(2,1)}, bf16[96,2048]{1,0:T(8,128)(2,1)S(1)}, u32[]{:S(2)}, u32[]{:S(2)}) %collective-permute-start.8) | collective-permute-done | bytes 393248 | tf_op jit(solution)/shard_map/ppermute | solution.py:414
  114.1 9.4 %collective-permute-done.9.refs_3_ = bf16[96,2048]{1,0:T(8,128)(2,1)S(1)} collective-permute-done((bf16[96,2048]{1,0:T(8,128)(2,1)}, bf16[96,2048]{1,0:T(8,128)(2,1)S(1)}, u32[]{:S(2)}, u32[]{:S(2)}) %collective-permute-start.9) | collective-permute-done | bytes 393248 | tf_op jit(solution)/shard_map/ppermute | solution.py:414
  124.6 4.9 %collective-permute-done.10.refs_4_ = bf16[96,2048]{1,0:T(8,128)(2,1)S(1)} collective-permute-done((bf16[96,2048]{1,0:T(8,128)(2,1)}, bf16[96,2048]{1,0:T(8,128)(2,1)S(1)}, u32[]{:S(2)}, u32[]{:S(2)}) %collective-permute-start.10) | collective-permute-done | bytes 393248 | tf_op jit(solution)/shard_map/ppermute | solution.py:414
  130.0 9.9 %collective-permute-done.11.refs_5_ = bf16[96,2048]{1,0:T(8,128)(2,1)S(1)} collective-permute-done((bf16[96,2048]{1,0:T(8,128)(2,1)}, bf16[96,2048]{1,0:T(8,128)(2,1)S(1)}, u32[]{:S(2)}, u32[]{:S(2)}) %collective-permute-start.11) | collective-permute-done | bytes 393248 | tf_op jit(solution)/shard_map/ppermute | solution.py:414
  141.1 13.0 %collective-permute-done.13.refs_7_ = bf16[96,2048]{1,0:T(8,128)(2,1)S(1)} collective-permute-done((bf16[96,2048]{1,0:T(8,128)(2,1)}, bf16[96,2048]{1,0:T(8,128)(2,1)S(1)}, u32[]{:S(2)}, u32[]{:S(2)}) %collective-permute-start.13) | collective-permute-done | bytes 393248 | tf_op jit(solution)/shard_map/ppermute | solution.py:414
  155.8 14.1 %expert.2 = bf16[8,48,2048]{2,1,0:T(8,128)(2,1)} custom-call(s32[4]{0:T(128)} %pad_add_fusion.place_ref, bf16[96,2048]{1,0:T(8,128)(2,1)} %get-tuple-element.45.refs_0_, bf16[96,2048]{1,0:T(8,128)(2,1)} %copy-done.24, bf16[96,2048]{1,0:T(8,128)(2,1)} %copy-done.25, bf16[96,2048]{1,0:T(8,128)(2,1)} %copy-done.26, bf16[96,2048]{1,0:T(8,128)(2,1)} %copy-done.27, ...), custom_call_target="tpu_custom_call" | custom-call | flops 6643777536 | bytes 20447232 | tf_op jit(solution)/shard_map/expert/pallas_call | solution.py:228
  173.5 14.2 %expert.3 = bf16[8,48,2048]{2,1,0:T(8,128)(2,1)} custom-call(s32[4]{0:T(128)} %pad_add_fusion.place_ref, bf16[96,2048]{1,0:T(8,128)(2,1)} %get-tuple-element.45.refs_0_, bf16[96,2048]{1,0:T(8,128)(2,1)} %copy-done.24, bf16[96,2048]{1,0:T(8,128)(2,1)} %copy-done.25, bf16[96,2048]{1,0:T(8,128)(2,1)} %copy-done.26, bf16[96,2048]{1,0:T(8,128)(2,1)} %copy-done.27, ...), custom_call_target="tpu_custom_call" | custom-call | flops 6643777536 | bytes 20447232 | tf_op jit(solution)/shard_map/expert/pallas_call | solution.py:228
  187.7 7.5 %all-to-all-done = bf16[8,48,2048]{2,1,0:T(8,128)(2,1)S(1)} async-done(((bf16[8,48,2048]{2,1,0:T(8,128)(2,1)}), bf16[8,48,2048]{2,1,0:T(8,128)(2,1)S(1)}, u32[]{:S(2)}, u32[]{:S(2)}) %all-to-all-start) | async-done | bytes 1572896 | tf_op jit(solution)/shard_map/all_to_all | solution.py:427
  207.3 13.7 %all-to-all-done.1 = bf16[8,48,2048]{2,1,0:T(8,128)(2,1)S(1)} async-done(((bf16[8,48,2048]{2,1,0:T(8,128)(2,1)}), bf16[8,48,2048]{2,1,0:T(8,128)(2,1)S(1)}, u32[]{:S(2)}, u32[]{:S(2)}) %all-to-all-start.1) | async-done | bytes 1572896 | tf_op jit(solution)/shard_map/all_to_all | solution.py:427
  222.2 7.7 %all-to-all-start.2 = ((bf16[8,2,2,64,512]{4,3,2,1,0:T(8,128)(2,1)}), bf16[8,2,2,64,512]{4,3,2,1,0:T(8,128)(2,1)S(1)}, u32[]{:S(2)}, u32[]{:S(2)}) async-start(bf16[8,2,2,64,512]{4,3,2,1,0:T(8,128)(2,1)} %get-tuple-element.64), calls=%async_computation.2 | async-start | bytes 4194304 | tf_op jit(solution)/shard_map/all_to_all | solution.py:455
  238.0 24.7 %collective-permute-done.27 = bf16[8,2,2,64,512]{4,3,2,1,0:T(8,128)(2,1)} collective-permute-done((bf16[8,2,2,64,512]{4,3,2,1,0:T(8,128)(2,1)}, bf16[8,2,2,64,512]{4,3,2,1,0:T(8,128)(2,1)}, u32[]{:S(2)}, u32[]{:S(2)}) %collective-permute-start.27) | collective-permute-done | bytes 2097184 | tf_op jit(solution)/shard_map/ppermute | solution.py:454
  265.8 6.4 %collective-permute-start.32 = (bf16[2,2,64,512]{3,2,1,0:T(8,128)(2,1)}, bf16[2,2,64,512]{3,2,1,0:T(8,128)(2,1)}, u32[]{:S(2)}, u32[]{:S(2)}) collective-permute-start(bf16[2,2,64,512]{3,2,1,0:T(8,128)(2,1)} %get-tuple-element.78), channel_id=1, source_target_pairs={{0,80},{16,96},{32,112},{48,0},{64,16},{80,32},{96,48},{112,64},{1... | collective-permute-start | bytes 786440 | tf_op jit(solution)/shard_map/ppermute | solution.py:466
  277.4 12.0 %collective-permute-done.20 = bf16[64,2048]{1,0:T(8,128)(2,1)} collective-permute-done((bf16[64,2048]{1,0:T(8,128)(2,1)}, bf16[64,2048]{1,0:T(8,128)(2,1)}, u32[]{:S(2)}, u32[]{:S(2)}) %collective-permute-start.20) | collective-permute-done | bytes 262176 | tf_op jit(solution)/shard_map/ppermute | solution.py:440
  290.5 35.6 %collective-permute-done.24 = bf16[64,2048]{1,0:T(8,128)(2,1)S(1)} collective-permute-done((bf16[64,2048]{1,0:T(8,128)(2,1)}, bf16[64,2048]{1,0:T(8,128)(2,1)S(1)}, u32[]{:S(2)}, u32[]{:S(2)}) %collective-permute-start.24) | collective-permute-done | bytes 262176 | tf_op jit(solution)/shard_map/ppermute | solution.py:444
  326.8 7.2 %collective-permute-done.21 = bf16[64,2048]{1,0:T(8,128)(2,1)S(1)} collective-permute-done((bf16[64,2048]{1,0:T(8,128)(2,1)S(1)}, bf16[64,2048]{1,0:T(8,128)(2,1)S(1)}, u32[]{:S(2)}, u32[]{:S(2)}) %collective-permute-start.21) | collective-permute-done | bytes 262176 | tf_op jit(solution)/shard_map/ppermute | solution.py:440
  334.0 8.1 %collective-permute-done.25 = bf16[64,2048]{1,0:T(8,128)(2,1)S(1)} collective-permute-done((bf16[64,2048]{1,0:T(8,128)(2,1)S(1)}, bf16[64,2048]{1,0:T(8,128)(2,1)S(1)}, u32[]{:S(2)}, u32[]{:S(2)}) %collective-permute-start.25) | collective-permute-done | bytes 262176 | tf_op jit(solution)/shard_map/ppermute | solution.py:444
  342.9 8.7 %collective-permute-done.22 = bf16[64,2048]{1,0:T(8,128)(2,1)S(1)} collective-permute-done((bf16[64,2048]{1,0:T(8,128)(2,1)S(1)}, bf16[64,2048]{1,0:T(8,128)(2,1)S(1)}, u32[]{:S(2)}, u32[]{:S(2)}) %collective-permute-start.22) | collective-permute-done | bytes 262176 | tf_op jit(solution)/shard_map/ppermute | solution.py:440
  358.1 13.3 %collective-permute-done.30.refs_3_ = bf16[2,2,64,512]{3,2,1,0:T(8,128)(2,1)S(1)} collective-permute-done((bf16[2,2,64,512]{3,2,1,0:T(8,128)(2,1)S(1)}, bf16[2,2,64,512]{3,2,1,0:T(8,128)(2,1)S(1)}, u32[]{:S(2)}, u32[]{:S(2)}) %collective-permute-start.30) | collective-permute-done | bytes 262176 | tf_op jit(solution)/shard_map/ppermute | solution.py:466
  371.4 8.3 %collective-permute-done.29.refs_2_ = bf16[2,2,64,512]{3,2,1,0:T(8,128)(2,1)S(1)} collective-permute-done((bf16[2,2,64,512]{3,2,1,0:T(8,128)(2,1)S(1)}, bf16[2,2,64,512]{3,2,1,0:T(8,128)(2,1)S(1)}, u32[]{:S(2)}, u32[]{:S(2)}) %collective-permute-start.29) | collective-permute-done | bytes 262176 | tf_op jit(solution)/shard_map/ppermute | solution.py:466
  (150 shorter events, 98.9 us)
Async XLA Ops:
  3.4 46.5 %collective-permute-start.16 = (bf16[352,2048]{1,0:T(8,128)(2,1)}, bf16[352,2048]{1,0:T(8,128)(2,1)}, u32[]{:S(2)}, u32[]{:S(2)}) collective-permute-start(bf16[352,2048]{1,0:T(8,128)(2,1)} %constant_dynamic-slice_fusion.1), channel_id=1, source_target_pairs={{0,2},{2,0},{4,6},{6,4},{8,10},{10,8},{12,14},{14,12},{1,3},{3,1},... | collective-permute-start | bytes 4325384 | tf_op jit(solution)/shard_map/ppermute | solution.py:374
  5.2 63.9 %collective-permute-start.15 = (bf16[352,2048]{1,0:T(8,128)(2,1)S(1)}, bf16[352,2048]{1,0:T(8,128)(2,1)}, u32[]{:S(2)}, u32[]{:S(2)}) collective-permute-start(bf16[352,2048]{1,0:T(8,128)(2,1)S(1)} %dynamic-slice_bitcast_fusion), channel_id=1, source_target_pairs={{0,2},{2,0},{4,6},{6,4},{8,10},{10,8},{12,14},{14,12},{1,3},{3,1},... | collective-permute-start | bytes 4325384 | tf_op jit(solution)/shard_map/ppermute | solution.py:374
  5.9 93.0 %collective-permute-start.14 = (bf16[352,2048]{1,0:T(8,128)(2,1)S(1)}, bf16[352,2048]{1,0:T(8,128)(2,1)}, u32[]{:S(2)}, u32[]{:S(2)}) collective-permute-start(bf16[352,2048]{1,0:T(8,128)(2,1)S(1)} %dynamic-slice_bitcast_fusion.1), channel_id=1, source_target_pairs={{0,2},{2,0},{4,6},{6,4},{8,10},{10,8},{12,14},{14,12},{1,3},{3,1},... | collective-permute-start | bytes 4325384 | tf_op jit(solution)/shard_map/ppermute | solution.py:374
  47.7 54.2 %collective-permute-start.7 = (bf16[96,2048]{1,0:T(8,128)(2,1)}, bf16[96,2048]{1,0:T(8,128)(2,1)S(1)}, u32[]{:S(2)}, u32[]{:S(2)}) collective-permute-start(bf16[96,2048]{1,0:T(8,128)(2,1)} %get-tuple-element.46), channel_id=1, source_target_pairs={{0,6},{2,4},{4,2},{6,0},{8,14},{10,12},{12,10},{14,8},{16,22},{18,... | collective-permute-start | bytes 1179656 | tf_op jit(solution)/shard_map/ppermute | solution.py:414
  50.0 104.2 %collective-permute-start.19 = (bf16[352,2048]{1,0:T(8,128)(2,1)}, bf16[352,2048]{1,0:T(8,128)(2,1)}, u32[]{:S(2)}, u32[]{:S(2)}) collective-permute-start(bf16[352,2048]{1,0:T(8,128)(2,1)} %collective-permute-done.16.refs_13_), channel_id=1, source_target_pairs={{0,1},{1,0},{2,3},{3,2},{4,5},{5,4},{6,7},{7,6},{8,9},{9,8},{10,11... | collective-permute-start | bytes 4325384 | tf_op jit(solution)/shard_map/ppermute | solution.py:376
  69.1 85.0 %collective-permute-start.18 = (bf16[352,2048]{1,0:T(8,128)(2,1)}, bf16[352,2048]{1,0:T(8,128)(2,1)S(1)}, u32[]{:S(2)}, u32[]{:S(2)}) collective-permute-start(bf16[352,2048]{1,0:T(8,128)(2,1)} %collective-permute-done.15.refs_12_), channel_id=1, source_target_pairs={{0,1},{1,0},{2,3},{3,2},{4,5},{5,4},{6,7},{7,6},{8,9},{9,8},{10,11... | collective-permute-start | bytes 4325384 | tf_op jit(solution)/shard_map/ppermute | solution.py:376
  98.9 55.3 %collective-permute-start.17 = (bf16[352,2048]{1,0:T(8,128)(2,1)}, bf16[352,2048]{1,0:T(8,128)(2,1)S(1)}, u32[]{:S(2)}, u32[]{:S(2)}) collective-permute-start(bf16[352,2048]{1,0:T(8,128)(2,1)} %collective-permute-done.14.refs_11_), channel_id=1, source_target_pairs={{0,1},{1,0},{2,3},{3,2},{4,5},{5,4},{6,7},{7,6},{8,9},{9,8},{10,11... | collective-permute-start | bytes 4325384 | tf_op jit(solution)/shard_map/ppermute | solution.py:376
  101.9 21.6 %collective-permute-start.9 = (bf16[96,2048]{1,0:T(8,128)(2,1)}, bf16[96,2048]{1,0:T(8,128)(2,1)S(1)}, u32[]{:S(2)}, u32[]{:S(2)}) collective-permute-start(bf16[96,2048]{1,0:T(8,128)(2,1)} %get-tuple-element.48), channel_id=1, source_target_pairs={{0,14},{2,12},{4,10},{6,8},{8,6},{10,4},{12,2},{14,0},{16,30},{18,... | collective-permute-start | bytes 1179656 | tf_op jit(solution)/shard_map/ppermute | solution.py:414
  112.6 16.9 %collective-permute-start.10 = (bf16[96,2048]{1,0:T(8,128)(2,1)}, bf16[96,2048]{1,0:T(8,128)(2,1)S(1)}, u32[]{:S(2)}, u32[]{:S(2)}) collective-permute-start(bf16[96,2048]{1,0:T(8,128)(2,1)} %get-tuple-element.49), channel_id=1, source_target_pairs={{0,128},{2,130},{4,132},{6,134},{8,136},{10,138},{12,140},{14,142}... | collective-permute-start | bytes 1179656 | tf_op jit(solution)/shard_map/ppermute | solution.py:414
  169.9 25.3 %all-to-all-start = ((bf16[8,48,2048]{2,1,0:T(8,128)(2,1)}), bf16[8,48,2048]{2,1,0:T(8,128)(2,1)S(1)}, u32[]{:S(2)}, u32[]{:S(2)}) async-start(bf16[8,48,2048]{2,1,0:T(8,128)(2,1)} %expert.2), calls=%async_computation | async-start | bytes 3145728 | tf_op jit(solution)/shard_map/all_to_all | solution.py:427
  196.4 24.6 %all-to-all-start.1 = ((bf16[8,48,2048]{2,1,0:T(8,128)(2,1)}), bf16[8,48,2048]{2,1,0:T(8,128)(2,1)S(1)}, u32[]{:S(2)}, u32[]{:S(2)}) async-start(bf16[8,48,2048]{2,1,0:T(8,128)(2,1)} %expert.3), calls=%async_computation.1 | async-start | bytes 3145728 | tf_op jit(solution)/shard_map/all_to_all | solution.py:427
  204.4 58.4 %collective-permute-start.27 = (bf16[8,2,2,64,512]{4,3,2,1,0:T(8,128)(2,1)}, bf16[8,2,2,64,512]{4,3,2,1,0:T(8,128)(2,1)}, u32[]{:S(2)}, u32[]{:S(2)}) collective-permute-start(bf16[8,2,2,64,512]{4,3,2,1,0:T(8,128)(2,1)} %get-tuple-element.65), channel_id=1, source_target_pairs={{0,128},{16,144},{32,160},{48,176},{64,192},{80,208},{96,224},{112... | collective-permute-start | bytes 6291464 | tf_op jit(solution)/shard_map/ppermute | solution.py:454
  222.2 162.4 %all-to-all-start.2 = ((bf16[8,2,2,64,512]{4,3,2,1,0:T(8,128)(2,1)}), bf16[8,2,2,64,512]{4,3,2,1,0:T(8,128)(2,1)S(1)}, u32[]{:S(2)}, u32[]{:S(2)}) async-start(bf16[8,2,2,64,512]{4,3,2,1,0:T(8,128)(2,1)} %get-tuple-element.64), calls=%async_computation.2 | async-start | bytes 4194304 | tf_op jit(solution)/shard_map/all_to_all | solution.py:455
  235.4 54.1 %collective-permute-start.20 = (bf16[64,2048]{1,0:T(8,128)(2,1)}, bf16[64,2048]{1,0:T(8,128)(2,1)}, u32[]{:S(2)}, u32[]{:S(2)}) collective-permute-start(bf16[64,2048]{1,0:T(8,128)(2,1)} %get-tuple-element.53), channel_id=1, source_target_pairs={{0,16},{16,32},{32,48},{48,64},{64,80},{80,96},{96,112},{112,0},{1... | collective-permute-start | bytes 786440 | tf_op jit(solution)/shard_map/ppermute | solution.py:440
  265.6 86.8 %collective-permute-start.34 = (bf16[2,2,64,512]{3,2,1,0:T(8,128)(2,1)}, bf16[2,2,64,512]{3,2,1,0:T(8,128)(2,1)}, u32[]{:S(2)}, u32[]{:S(2)}) collective-permute-start(bf16[2,2,64,512]{3,2,1,0:T(8,128)(2,1)} %get-tuple-element.76), channel_id=1, source_target_pairs={{0,112},{16,0},{32,16},{48,32},{64,48},{80,64},{96,80},{112,96},{1... | collective-permute-start | bytes 786440 | tf_op jit(solution)/shard_map/ppermute | solution.py:466
  265.8 86.6 %collective-permute-start.33 = (bf16[2,2,64,512]{3,2,1,0:T(8,128)(2,1)}, bf16[2,2,64,512]{3,2,1,0:T(8,128)(2,1)}, u32[]{:S(2)}, u32[]{:S(2)}) collective-permute-start(bf16[2,2,64,512]{3,2,1,0:T(8,128)(2,1)} %get-tuple-element.77), channel_id=1, source_target_pairs={{0,96},{16,112},{32,0},{48,16},{64,32},{80,48},{96,64},{112,80},{1... | collective-permute-start | bytes 786440 | tf_op jit(solution)/shard_map/ppermute | solution.py:466
  265.8 86.7 %collective-permute-start.32 = (bf16[2,2,64,512]{3,2,1,0:T(8,128)(2,1)}, bf16[2,2,64,512]{3,2,1,0:T(8,128)(2,1)}, u32[]{:S(2)}, u32[]{:S(2)}) collective-permute-start(bf16[2,2,64,512]{3,2,1,0:T(8,128)(2,1)} %get-tuple-element.78), channel_id=1, source_target_pairs={{0,80},{16,96},{32,112},{48,0},{64,16},{80,32},{96,48},{112,64},{1... | collective-permute-start | bytes 786440 | tf_op jit(solution)/shard_map/ppermute | solution.py:466
  272.2 82.3 %collective-permute-start.31 = (bf16[2,2,64,512]{3,2,1,0:T(8,128)(2,1)}, bf16[2,2,64,512]{3,2,1,0:T(8,128)(2,1)}, u32[]{:S(2)}, u32[]{:S(2)}) collective-permute-start(bf16[2,2,64,512]{3,2,1,0:T(8,128)(2,1)} %get-tuple-element.79), channel_id=1, source_target_pairs={{0,64},{16,80},{32,96},{48,112},{64,0},{80,16},{96,32},{112,48},{1... | collective-permute-start | bytes 786440 | tf_op jit(solution)/shard_map/ppermute | solution.py:466
  289.4 36.7 %collective-permute-start.24 = (bf16[64,2048]{1,0:T(8,128)(2,1)}, bf16[64,2048]{1,0:T(8,128)(2,1)S(1)}, u32[]{:S(2)}, u32[]{:S(2)}) collective-permute-start(bf16[64,2048]{1,0:T(8,128)(2,1)} %get-tuple-element.60), channel_id=1, source_target_pairs={{16,0},{32,16},{48,32},{64,48},{80,64},{96,80},{112,96},{0,112},{1... | collective-permute-start | bytes 786440 | tf_op jit(solution)/shard_map/ppermute | solution.py:444
  351.6 19.8 %collective-permute-start.30 = (bf16[2,2,64,512]{3,2,1,0:T(8,128)(2,1)S(1)}, bf16[2,2,64,512]{3,2,1,0:T(8,128)(2,1)S(1)}, u32[]{:S(2)}, u32[]{:S(2)}) collective-permute-start(bf16[2,2,64,512]{3,2,1,0:T(8,128)(2,1)S(1)} %copy-done.16), channel_id=1, source_target_pairs={{0,48},{16,64},{32,80},{48,96},{64,112},{80,0},{96,16},{112,32},{1... | collective-permute-start | bytes 786440 | tf_op jit(solution)/shard_map/ppermute | solution.py:466
  352.4 27.3 %collective-permute-start.29 = (bf16[2,2,64,512]{3,2,1,0:T(8,128)(2,1)S(1)}, bf16[2,2,64,512]{3,2,1,0:T(8,128)(2,1)S(1)}, u32[]{:S(2)}, u32[]{:S(2)}) collective-permute-start(bf16[2,2,64,512]{3,2,1,0:T(8,128)(2,1)S(1)} %copy-done.15), channel_id=1, source_target_pairs={{0,32},{16,48},{32,64},{48,80},{64,96},{80,112},{96,0},{112,16},{1... | collective-permute-start | bytes 786440 | tf_op jit(solution)/shard_map/ppermute | solution.py:466
  352.4 32.2 %collective-permute-start.28 = (bf16[2,2,64,512]{3,2,1,0:T(8,128)(2,1)S(1)}, bf16[2,2,64,512]{3,2,1,0:T(8,128)(2,1)}, u32[]{:S(2)}, u32[]{:S(2)}) collective-permute-start(bf16[2,2,64,512]{3,2,1,0:T(8,128)(2,1)S(1)} %get-tuple-element.82), channel_id=1, source_target_pairs={{0,16},{16,32},{32,48},{48,64},{64,80},{80,96},{96,112},{112,0},{1... | collective-permute-start | bytes 786440 | tf_op jit(solution)/shard_map/ppermute | solution.py:466
  352.5 37.5 %collective-permute-start.26 = (bf16[64,2048]{1,0:T(8,128)(2,1)}, bf16[64,2048]{1,0:T(8,128)(2,1)S(1)}, u32[]{:S(2)}, u32[]{:S(2)}) collective-permute-start(bf16[64,2048]{1,0:T(8,128)(2,1)} %add_convert_fusion.1), channel_id=1, source_target_pairs={{16,0},{32,16},{48,32},{64,48},{80,64},{96,80},{112,96},{0,112},{1... | collective-permute-start | bytes 786440 | tf_op jit(solution)/shard_map/ppermute | solution.py:444
  354.5 35.5 %collective-permute-start.23 = (bf16[64,2048]{1,0:T(8,128)(2,1)}, bf16[64,2048]{1,0:T(8,128)(2,1)}, u32[]{:S(2)}, u32[]{:S(2)}) collective-permute-start(bf16[64,2048]{1,0:T(8,128)(2,1)} %add_convert_fusion.3), channel_id=1, source_target_pairs={{0,16},{16,32},{32,48},{48,64},{64,80},{80,96},{96,112},{112,0},{1... | collective-permute-start | bytes 786440 | tf_op jit(solution)/shard_map/ppermute | solution.py:440
  (45 other events, 698.8 us)

commit v7 on v6

--- a/solution.py
+++ b/solution.py
@@ -196,7 +196,13 @@
         xs[m * part : (m + 1) * part, :] = xin[m][...]
 
     me = place_ref[0]
-    acc[...] = jnp.zeros_like(acc)
+
+    def clear(m, _):
+        here = pl.ds(pl.multiple_of(m * part, part), part)
+        acc[here, :] = jnp.zeros((part, acc.shape[1]), F32)
+        return 0
+
+    lax.fori_loop(0, PEERS, clear, 0)
     for copy in copies[:3]:
         copy.wait()
 
@@ -215,8 +221,12 @@
         return 0
 
     lax.fori_loop(0, 2, run, 0)
-    for m in range(PEERS):
-        o_ref[me ^ m] = acc[m * part : (m + 1) * part, :].astype(BF16)
+
+    def leave(m, _):
+        o_ref[me ^ m] = acc[pl.ds(pl.multiple_of(m * part, part), part), :].astype(BF16)
+        return 0
+
+    lax.fori_loop(0, PEERS, leave, 0)
 
 
 def expert(place, x, own, first, second, group, rows):
@@ -251,7 +261,7 @@
     )(place, *x, *own, *first, *second)
 
 
-def leave_kernel(place_ref, table_ref, in_ref, same_ref, cross_ref, used):
+def leave_kernel(place_ref, table_ref, in_ref, same_ref, first_ref, later_ref, used):
     z, x, column = place_ref[1], place_ref[2], place_ref[3]
     blk_dev = in_ref.shape[1]
 
@@ -271,9 +281,13 @@
         def _():
             same_ref[far, rank] = in_ref[:, i]
 
-        @pl.when(dest // ZS != x)
+        @pl.when((dest // ZS != x) & (rank == 0))
         def _():
-            cross_ref[(far - z) & (ZS - 1), rank] = in_ref[:, i]
+            first_ref[(far - z) & (ZS - 1)] = in_ref[:, i]
+
+        @pl.when((dest // ZS != x) & (rank == 1))
+        def _():
+            later_ref[(far - z) & (ZS - 1)] = in_ref[:, i]
 
         return 0
 
@@ -285,18 +299,54 @@
     smem = pl.BlockSpec(memory_space=pltpu.SMEM)
     vm = pl.BlockSpec(memory_space=pltpu.VMEM)
     shape = jax.ShapeDtypeStruct((ZS, spare, layers, blk, wide), cache.dtype)
+    single = jax.ShapeDtypeStruct((ZS, layers, blk, wide), cache.dtype)
     return pl.pallas_call(
         leave_kernel,
         in_specs=[smem, smem, vm],
-        out_specs=[vm, vm],
-        out_shape=[shape, shape],
+        out_specs=[vm, vm, vm],
+        out_shape=[shape, single, single],
         scratch_shapes=[pltpu.SMEM((2 * ZS,), jnp.int32)],
         name="gather_out",
     )(place, table, cache)
 
 
+def join_kernel(first_ref, later_ref, *outs):
+    for n, out in enumerate(outs):
+        out[0] = first_ref[n + 1]
+        out[1] = later_ref[n + 1]
+
+
+def join(first, later):
+    vm = pl.BlockSpec(memory_space=pltpu.VMEM)
+    return pl.pallas_call(
+        join_kernel,
+        in_specs=[vm] * 2,
+        out_specs=[vm] * (ZS - 1),
+        out_shape=[jax.ShapeDtypeStruct((2,) + first.shape[1:], first.dtype)] * (ZS - 1),
+        name="join",
+    )(first, later)
+
+
+def collect_kernel(later_ref, *refs):
+    out = refs[-1]
+    out[0] = later_ref[0]
+    for n, ref in enumerate(refs[:-1]):
+        out[n + 1] = ref[1]
+
+
+def collect(later, moved):
+    vm = pl.BlockSpec(memory_space=pltpu.VMEM)
+    return pl.pallas_call(
+        collect_kernel,
+        in_specs=[vm] * ZS,
+        out_specs=vm,
+        out_shape=jax.ShapeDtypeStruct(later.shape, later.dtype),
+        name="collect",
+    )(later, *moved)
+
+
 def arrive_kernel(place_ref, slot_ref, same_ref, *refs):
-    crossed, out_ref = refs[:ZS], refs[ZS]
+    crossed, beyond_ref, out_ref = refs[:ZS], refs[ZS], refs[ZS + 1]
     z, x = place_ref[1], place_ref[2]
     spare = same_ref.shape[1]
 
@@ -314,21 +364,21 @@
 
     lax.fori_loop(0, ZS, one, 0)
     for n in range(ZS):
-        for i in range(spare):
-            put((1 - x) * ZS + ((z - n) & (ZS - 1)), i, crossed[n].at[i])
-
-
-def gather_in(place, slots, same, crossed, blk_dev):
+        put((1 - x) * ZS + ((z - n) & (ZS - 1)), 0, crossed[n].at[0])
+        put((1 - x) * ZS + ((z - n) & (ZS - 1)), 1, beyond_ref.at[n])
+
+
+def gather_in(place, slots, same, crossed, beyond, blk_dev):
     _, _, layers, blk, wide = same.shape
     smem = pl.BlockSpec(memory_space=pltpu.SMEM)
     vm = pl.BlockSpec(memory_space=pltpu.VMEM)
     return pl.pallas_call(
         arrive_kernel,
-        in_specs=[smem, smem] + [vm] * (ZS + 1),
+        in_specs=[smem, smem] + [vm] * (ZS + 2),
         out_specs=vm,
         out_shape=jax.ShapeDtypeStruct((layers, blk_dev, blk, wide), same.dtype),
         name="gather_in",
-    )(place, slots, same, *crossed)
+    )(place, slots, same, *crossed, beyond)
 
 
 def arrival_slots(handover_table, sources, blk_dev, spare):
@@ -450,8 +500,9 @@
     sources = lax.axis_size("pre")
     spare = blk_dev // sources + 1
     in_slots = arrival_slots(handover_table, sources, blk_dev, spare)
-    same, cross = gather_out(place, handover_table, prefill_cache[:, 0], spare)
-    cross = lax.ppermute(cross, "pre", [(i, (i + ZS) % sources) for i in range(sources)])
+    same, first_cross, later = gather_out(place, handover_table, prefill_cache[:, 0], spare)
+    across = [(i, (i + ZS) % sources) for i in range(sources)]
+    first_cross = lax.ppermute(first_cross, "pre", across)
     same = lax.all_to_all(
         same,
         "pre",
@@ -460,14 +511,17 @@
         axis_index_groups=[list(range(x * ZS, (x + 1) * ZS)) for x in range(sources // ZS)],
         tiled=True,
     )
-    crossed = [cross[0]]
-    for n in range(1, ZS):
+    crossed = []
+    for n, both in enumerate(join(first_cross, later)):
         crossed.append(
             lax.ppermute(
-                cross[n], "pre", [(i, i // ZS * ZS + (i + n) % ZS) for i in range(sources)]
+                both, "pre", [(i, i // ZS * ZS + (i + n + 1) % ZS) for i in range(sources)]
             )
         )
-    decode_cache = gather_in(place, in_slots, same, crossed, blk_dev)[:, None]
+    rest = collect(later, crossed)
+    crossed = [first_cross] + crossed
+    rest = lax.ppermute(rest, "pre", across)
+    decode_cache = gather_in(place, in_slots, same, crossed, rest, blk_dev)[:, None]
     return (moe_output, decode_cache)
 
 

time: 394 us -> 366 us (0.929)
  waiting for transfers between devices: 252 us -> 209 us
  starting transfers between devices: 61.8 us -> 71.8 us
  Pallas kernels: 57.6 us -> 63.9 us
    ppermute x3, waiting for transfers between devices: 43.7 us -> 2.15 us  [shards(): falling = lax.ppermute(falling, 'pre', down)]
    ppermute x4, waiting for transfers between devices: 27.9 us -> 9.76 us  [shards(): rising = lax.ppermute(rising, 'pre', up)]
    ppermute x8 -> x9, waiting for transfers between devices: 50.6 us -> 67.5 us  [the longest x7 57.2 us: shards(): lax.ppermute(both, 'pre', [(i, i // ZS * ZS + (i + n + 1) % ZS) for i in...]
    pallas_call x1 -> x3, Pallas kernels: 3.97 us -> 10.1 us  [the longest x1 4.5 us: gather_in(): pl.pallas_call(arrive_kernel, in_specs=[smem, smem] + [vm] * (ZS + 2), ou...]
    ppermute x3, starting transfers between devices: 2.01 us -> 7.92 us  [shards(): falling = lax.ppermute(falling, 'pre', down)]
    ppermute x8 -> x9, starting transfers between devices: 9.05 us -> 14.5 us  [the longest x7 12.6 us: shards(): lax.ppermute(both, 'pre', [(i, i // ZS * ZS + (i + n + 1) % ZS) for i in...]
  transfers between devices with their start and end apart: 38 -> 39, of which waited for: 22 -> 22; matrix products, arithmetic and copies ran while one was open for 2% -> 2% of each run, Pallas kernels for 11% -> 14%
where the time goes in v7:
time: 366 us; the launch traced here: 365 us
  waiting for transfers between devices  209 us (57%)
  starting transfers between devices  71.8 us (20%)
  Pallas kernels  63.9 us (17%)
  local copies, waits for them, and re-layouts  11.4 us (3%)
  other arithmetic  8.03 us (2%)
    ppermute x7, waiting for transfers between devices, shards(): lax.ppermute(both, 'pre', [(i, i // ZS * ZS + (i + n + 1) % ZS) for i in...  57.2 us
    ppermute x3, waiting for transfers between devices, shards(): got = lax.ppermute(piece, 'tp', swap)  48.8 us
    ppermute x7, waiting for transfers between devices, shards(): lax.ppermute(packed[m], ('pre', 'tp'), [(g, peer_of(g, m)) for g in range...  45.9 us
    pallas_call x2, Pallas kernels, expert(): pl.pallas_call(expert_kernel, grid=(1,), in_specs=[pl.BlockSpec(memory_sp...  28.3 us
    all_to_all x2, waiting for transfers between devices, shards(): lax.all_to_all(result, ('pre', 'tp'), split_axis=0, concat_axis=0, axis_i...  21.2 us
    ppermute x4, starting transfers between devices, shards(): below.append(lax.ppermute(below[-1], 'pre', up))  14.4 us
    ppermute x4, waiting for transfers between devices, shards(): below.append(lax.ppermute(below[-1], 'pre', up))  13.5 us
    ppermute x7, starting transfers between devices, shards(): lax.ppermute(both, 'pre', [(i, i // ZS * ZS + (i + n + 1) % ZS) for i in...  12.6 us
  transfers between devices with their start and end apart: 39, of which 22 were waited for; matrix products, arithmetic and copies ran while one was open for 2% of the time, Pallas kernels for 14%

profile of v7, /device:TPU:96, one launch (start us, length us, event | category | flops | bytes accessed | tf_op | source)
XLA Modules:
  0.0 365.0 jit_solution(3084409596828731628)
XLA Ops:
  11.0 5.1 %collective-permute-done.refs_1_ = bf16[64,2176]{1,0:T(8,128)(2,1)S(1)} collective-permute-done((bf16[64,2176]{1,0:T(8,128)(2,1)S(1)}, bf16[64,2176]{1,0:T(8,128)(2,1)S(1)}, u32[]{:S(2)}, u32[]{:S(2)}) %collective-permute-start) | collective-permute-done | bytes 278560 | tf_op jit(solution)/shard_map/ppermute | solution.py:438
  36.2 5.1 %pack.2 = (bf16[48,2048]{1,0:T(8,128)(2,1)}, bf16[48,2048]{1,0:T(8,128)(2,1)}, bf16[48,2048]{1,0:T(8,128)(2,1)}, bf16[48,2048]{1,0:T(8,128)(2,1)}, bf16[48,2048]...) custom-call(s32[4]{0:T(128)} %pad_add_fusion.place_ref, ...), custom_call_target="tpu_custom_call" | custom-call | tf_op jit(solution)/shard_map/pack/pallas_call | solution.py:112
  41.4 6.4 %pack.3 = (bf16[96,2048]{1,0:T(8,128)(2,1)}, bf16[96,2048]{1,0:T(8,128)(2,1)}, bf16[96,2048]{1,0:T(8,128)(2,1)}, bf16[96,2048]{1,0:T(8,128)(2,1)}, bf16[96,2048]...) custom-call(s32[4]{0:T(128)} %pad_add_fusion.place_ref, ...), custom_call_target="tpu_custom_call" | custom-call | tf_op jit(solution)/shard_map/pack/pallas_call | solution.py:112
  50.0 19.1 %collective-permute-done.15.refs_12_ = bf16[352,2048]{1,0:T(8,128)(2,1)} collective-permute-done((bf16[352,2048]{1,0:T(8,128)(2,1)S(1)}, bf16[352,2048]{1,0:T(8,128)(2,1)}, u32[]{:S(2)}, u32[]{:S(2)}) %collective-permute-start.15) | collective-permute-done | bytes 1441824 | tf_op jit(solution)/shard_map/ppermute | solution.py:424
  69.1 29.8 %collective-permute-done.14.refs_11_ = bf16[352,2048]{1,0:T(8,128)(2,1)} collective-permute-done((bf16[352,2048]{1,0:T(8,128)(2,1)S(1)}, bf16[352,2048]{1,0:T(8,128)(2,1)}, u32[]{:S(2)}, u32[]{:S(2)}) %collective-permute-start.14) | collective-permute-done | bytes 1441824 | tf_op jit(solution)/shard_map/ppermute | solution.py:424
  104.9 7.7 %collective-permute-done.8.refs_2_ = bf16[96,2048]{1,0:T(8,128)(2,1)S(1)} collective-permute-done((bf16[96,2048]{1,0:T(8,128)(2,1)}, bf16[96,2048]{1,0:T(8,128)(2,1)S(1)}, u32[]{:S(2)}, u32[]{:S(2)}) %collective-permute-start.8) | collective-permute-done | bytes 393248 | tf_op jit(solution)/shard_map/ppermute | solution.py:464
  114.1 9.4 %collective-permute-done.9.refs_3_ = bf16[96,2048]{1,0:T(8,128)(2,1)S(1)} collective-permute-done((bf16[96,2048]{1,0:T(8,128)(2,1)}, bf16[96,2048]{1,0:T(8,128)(2,1)S(1)}, u32[]{:S(2)}, u32[]{:S(2)}) %collective-permute-start.9) | collective-permute-done | bytes 393248 | tf_op jit(solution)/shard_map/ppermute | solution.py:464
  124.6 4.9 %collective-permute-done.10.refs_4_ = bf16[96,2048]{1,0:T(8,128)(2,1)S(1)} collective-permute-done((bf16[96,2048]{1,0:T(8,128)(2,1)}, bf16[96,2048]{1,0:T(8,128)(2,1)S(1)}, u32[]{:S(2)}, u32[]{:S(2)}) %collective-permute-start.10) | collective-permute-done | bytes 393248 | tf_op jit(solution)/shard_map/ppermute | solution.py:464
  130.0 9.9 %collective-permute-done.11.refs_5_ = bf16[96,2048]{1,0:T(8,128)(2,1)S(1)} collective-permute-done((bf16[96,2048]{1,0:T(8,128)(2,1)}, bf16[96,2048]{1,0:T(8,128)(2,1)S(1)}, u32[]{:S(2)}, u32[]{:S(2)}) %collective-permute-start.11) | collective-permute-done | bytes 393248 | tf_op jit(solution)/shard_map/ppermute | solution.py:464
  141.1 13.0 %collective-permute-done.13.refs_7_ = bf16[96,2048]{1,0:T(8,128)(2,1)S(1)} collective-permute-done((bf16[96,2048]{1,0:T(8,128)(2,1)}, bf16[96,2048]{1,0:T(8,128)(2,1)S(1)}, u32[]{:S(2)}, u32[]{:S(2)}) %collective-permute-start.13) | collective-permute-done | bytes 393248 | tf_op jit(solution)/shard_map/ppermute | solution.py:464
  155.9 14.1 %expert.2 = bf16[8,48,2048]{2,1,0:T(8,128)(2,1)} custom-call(s32[4]{0:T(128)} %pad_add_fusion.place_ref, bf16[96,2048]{1,0:T(8,128)(2,1)} %get-tuple-element.53.refs_0_, bf16[96,2048]{1,0:T(8,128)(2,1)} %copy-done.24, bf16[96,2048]{1,0:T(8,128)(2,1)} %copy-done.25, bf16[96,2048]{1,0:T(8,128)(2,1)} %copy-done.26, bf16[96,2048]{1,0:T(8,128)(2,1)} %copy-done.27, ...), custom_call_target="tpu_custom_call" | custom-call | flops 6643777536 | bytes 20447232 | tf_op jit(solution)/shard_map/expert/pallas_call | solution.py:238
  173.6 14.2 %expert.3 = bf16[8,48,2048]{2,1,0:T(8,128)(2,1)} custom-call(s32[4]{0:T(128)} %pad_add_fusion.place_ref, bf16[96,2048]{1,0:T(8,128)(2,1)} %get-tuple-element.53.refs_0_, bf16[96,2048]{1,0:T(8,128)(2,1)} %copy-done.24, bf16[96,2048]{1,0:T(8,128)(2,1)} %copy-done.25, bf16[96,2048]{1,0:T(8,128)(2,1)} %copy-done.26, bf16[96,2048]{1,0:T(8,128)(2,1)} %copy-done.27, ...), custom_call_target="tpu_custom_call" | custom-call | flops 6643777536 | bytes 20447232 | tf_op jit(solution)/shard_map/expert/pallas_call | solution.py:238
  187.8 7.5 %all-to-all-done = bf16[8,48,2048]{2,1,0:T(8,128)(2,1)S(1)} async-done(((bf16[8,48,2048]{2,1,0:T(8,128)(2,1)}), bf16[8,48,2048]{2,1,0:T(8,128)(2,1)S(1)}, u32[]{:S(2)}, u32[]{:S(2)}) %all-to-all-start) | async-done | bytes 1572896 | tf_op jit(solution)/shard_map/all_to_all | solution.py:477
  207.4 13.7 %all-to-all-done.1 = bf16[8,48,2048]{2,1,0:T(8,128)(2,1)S(1)} async-done(((bf16[8,48,2048]{2,1,0:T(8,128)(2,1)}), bf16[8,48,2048]{2,1,0:T(8,128)(2,1)S(1)}, u32[]{:S(2)}, u32[]{:S(2)}) %all-to-all-start.1) | async-done | bytes 1572896 | tf_op jit(solution)/shard_map/all_to_all | solution.py:477
  222.3 7.7 %all-to-all-start.2 = ((bf16[8,2,2,64,512]{4,3,2,1,0:T(8,128)(2,1)}), bf16[8,2,2,64,512]{4,3,2,1,0:T(8,128)(2,1)S(1)}, u32[]{:S(2)}, u32[]{:S(2)}) async-start(bf16[8,2,2,64,512]{4,3,2,1,0:T(8,128)(2,1)} %get-tuple-element.72), calls=%async_computation.2 | async-start | bytes 4194304 | tf_op jit(solution)/shard_map/all_to_all | solution.py:506
  230.0 10.3 %collective-permute-done.27.first_ref.refs_0_ = bf16[8,2,64,512]{3,2,1,0:T(8,128)(2,1)S(1)} collective-permute-done((bf16[8,2,64,512]{3,2,1,0:T(8,128)(2,1)}, bf16[8,2,64,512]{3,2,1,0:T(8,128)(2,1)S(1)}, u32[]{:S(2)}, u32[]{:S(2)}) %collective-permute-start.27) | collective-permute-done | bytes 1048608 | tf_op jit(solution)/shard_map/ppermute | solution.py:505
  249.3 5.0 %collective-permute-start.31 = (bf16[2,2,64,512]{3,2,1,0:T(8,128)(2,1)}, bf16[2,2,64,512]{3,2,1,0:T(8,128)(2,1)S(1)}, u32[]{:S(2)}, u32[]{:S(2)}) collective-permute-start(bf16[2,2,64,512]{3,2,1,0:T(8,128)(2,1)} %get-tuple-element.78), channel_id=1, source_target_pairs={{0,64},{16,80},{32,96},{48,112},{64,0},{80,16},{96,32},{112,48},{1... | collective-permute-start | bytes 786440 | tf_op jit(solution)/shard_map/ppermute | solution.py:517
  258.9 25.1 %collective-permute-done.28.refs_0_.refs_1_ = bf16[2,2,64,512]{3,2,1,0:T(8,128)(2,1)S(1)} collective-permute-done((bf16[2,2,64,512]{3,2,1,0:T(8,128)(2,1)}, bf16[2,2,64,512]{3,2,1,0:T(8,128)(2,1)S(1)}, u32[]{:S(2)}, u32[]{:S(2)}) %collective-permute-start.28) | collective-permute-done | bytes 262176 | tf_op jit(solution)/shard_map/ppermute | solution.py:517
  284.0 9.1 %collective-permute-done.29.refs_1_.refs_2_ = bf16[2,2,64,512]{3,2,1,0:T(8,128)(2,1)S(1)} collective-permute-done((bf16[2,2,64,512]{3,2,1,0:T(8,128)(2,1)}, bf16[2,2,64,512]{3,2,1,0:T(8,128)(2,1)S(1)}, u32[]{:S(2)}, u32[]{:S(2)}) %collective-permute-start.29) | collective-permute-done | bytes 262176 | tf_op jit(solution)/shard_map/ppermute | solution.py:517
  295.6 20.6 %collective-permute-done.30.refs_2_.refs_3_ = bf16[2,2,64,512]{3,2,1,0:T(8,128)(2,1)S(1)} collective-permute-done((bf16[2,2,64,512]{3,2,1,0:T(8,128)(2,1)}, bf16[2,2,64,512]{3,2,1,0:T(8,128)(2,1)S(1)}, u32[]{:S(2)}, u32[]{:S(2)}) %collective-permute-start.30) | collective-permute-done | bytes 262176 | tf_op jit(solution)/shard_map/ppermute | solution.py:517
  323.5 4.9 %collective-permute-start.24 = (bf16[64,2048]{1,0:T(8,128)(2,1)}, bf16[64,2048]{1,0:T(8,128)(2,1)S(1)}, u32[]{:S(2)}, u32[]{:S(2)}) collective-permute-start(bf16[64,2048]{1,0:T(8,128)(2,1)} %get-tuple-element.68), channel_id=1, source_target_pairs={{16,0},{32,16},{48,32},{64,48},{80,64},{96,80},{112,96},{0,112},{1... | collective-permute-start | bytes 786440 | tf_op jit(solution)/shard_map/ppermute | solution.py:494
  328.4 4.8 %weigh.3 = (f32[64,2048]{1,0:T(8,128)}, f32[64,2048]{1,0:T(8,128)}, f32[64,2048]{1,0:T(8,128)}, f32[64,2048]{1,0:T(8,128)}) custom-call(s32[4]{0:T(128)} %pad_add_fusion.place_ref, f32[64,256]{1,0:T(8,128)} %get-tuple-element.63.key_ref, f32[64,256]{1,0:T(8,128)} %get-tuple-element.64.whi_ref, f32[64,256]{1,0:T(8,128)} %get-tuple-element.65.wlo_ref, ...), custom_call_target="tpu_custom_call" | custom-call | tf_op jit(solution)/shard_map/weigh/pallas_call | solution.py:160
  338.6 4.9 %collective-permute-done.21 = bf16[64,2048]{1,0:T(8,128)(2,1)S(1)} collective-permute-done((bf16[64,2048]{1,0:T(8,128)(2,1)S(1)}, bf16[64,2048]{1,0:T(8,128)(2,1)S(1)}, u32[]{:S(2)}, u32[]{:S(2)}) %collective-permute-start.21) | collective-permute-done | bytes 262176 | tf_op jit(solution)/shard_map/ppermute | solution.py:490
  347.8 4.8 %collective-permute-done.22 = bf16[64,2048]{1,0:T(8,128)(2,1)S(1)} collective-permute-done((bf16[64,2048]{1,0:T(8,128)(2,1)S(1)}, bf16[64,2048]{1,0:T(8,128)(2,1)S(1)}, u32[]{:S(2)}, u32[]{:S(2)}) %collective-permute-start.22) | collective-permute-done | bytes 262176 | tf_op jit(solution)/shard_map/ppermute | solution.py:490
  (153 shorter events, 106.9 us)
Async XLA Ops:
  3.4 46.6 %collective-permute-start.16 = (bf16[352,2048]{1,0:T(8,128)(2,1)}, bf16[352,2048]{1,0:T(8,128)(2,1)}, u32[]{:S(2)}, u32[]{:S(2)}) collective-permute-start(bf16[352,2048]{1,0:T(8,128)(2,1)} %constant_dynamic-slice_fusion.1), channel_id=1, source_target_pairs={{0,2},{2,0},{4,6},{6,4},{8,10},{10,8},{12,14},{14,12},{1,3},{3,1},... | collective-permute-start | bytes 4325384 | tf_op jit(solution)/shard_map/ppermute | solution.py:424
  5.2 63.9 %collective-permute-start.15 = (bf16[352,2048]{1,0:T(8,128)(2,1)S(1)}, bf16[352,2048]{1,0:T(8,128)(2,1)}, u32[]{:S(2)}, u32[]{:S(2)}) collective-permute-start(bf16[352,2048]{1,0:T(8,128)(2,1)S(1)} %dynamic-slice_bitcast_fusion), channel_id=1, source_target_pairs={{0,2},{2,0},{4,6},{6,4},{8,10},{10,8},{12,14},{14,12},{1,3},{3,1},... | collective-permute-start | bytes 4325384 | tf_op jit(solution)/shard_map/ppermute | solution.py:424
  5.9 93.0 %collective-permute-start.14 = (bf16[352,2048]{1,0:T(8,128)(2,1)S(1)}, bf16[352,2048]{1,0:T(8,128)(2,1)}, u32[]{:S(2)}, u32[]{:S(2)}) collective-permute-start(bf16[352,2048]{1,0:T(8,128)(2,1)S(1)} %dynamic-slice_bitcast_fusion.1), channel_id=1, source_target_pairs={{0,2},{2,0},{4,6},{6,4},{8,10},{10,8},{12,14},{14,12},{1,3},{3,1},... | collective-permute-start | bytes 4325384 | tf_op jit(solution)/shard_map/ppermute | solution.py:424
  47.8 54.1 %collective-permute-start.7 = (bf16[96,2048]{1,0:T(8,128)(2,1)}, bf16[96,2048]{1,0:T(8,128)(2,1)S(1)}, u32[]{:S(2)}, u32[]{:S(2)}) collective-permute-start(bf16[96,2048]{1,0:T(8,128)(2,1)} %get-tuple-element.54), channel_id=1, source_target_pairs={{0,6},{2,4},{4,2},{6,0},{8,14},{10,12},{12,10},{14,8},{16,22},{18,... | collective-permute-start | bytes 1179656 | tf_op jit(solution)/shard_map/ppermute | solution.py:464
  50.0 104.1 %collective-permute-start.19 = (bf16[352,2048]{1,0:T(8,128)(2,1)}, bf16[352,2048]{1,0:T(8,128)(2,1)}, u32[]{:S(2)}, u32[]{:S(2)}) collective-permute-start(bf16[352,2048]{1,0:T(8,128)(2,1)} %collective-permute-done.16.refs_13_), channel_id=1, source_target_pairs={{0,1},{1,0},{2,3},{3,2},{4,5},{5,4},{6,7},{7,6},{8,9},{9,8},{10,11... | collective-permute-start | bytes 4325384 | tf_op jit(solution)/shard_map/ppermute | solution.py:426
  69.1 85.0 %collective-permute-start.18 = (bf16[352,2048]{1,0:T(8,128)(2,1)}, bf16[352,2048]{1,0:T(8,128)(2,1)S(1)}, u32[]{:S(2)}, u32[]{:S(2)}) collective-permute-start(bf16[352,2048]{1,0:T(8,128)(2,1)} %collective-permute-done.15.refs_12_), channel_id=1, source_target_pairs={{0,1},{1,0},{2,3},{3,2},{4,5},{5,4},{6,7},{7,6},{8,9},{9,8},{10,11... | collective-permute-start | bytes 4325384 | tf_op jit(solution)/shard_map/ppermute | solution.py:426
  98.9 55.3 %collective-permute-start.17 = (bf16[352,2048]{1,0:T(8,128)(2,1)}, bf16[352,2048]{1,0:T(8,128)(2,1)S(1)}, u32[]{:S(2)}, u32[]{:S(2)}) collective-permute-start(bf16[352,2048]{1,0:T(8,128)(2,1)} %collective-permute-done.14.refs_11_), channel_id=1, source_target_pairs={{0,1},{1,0},{2,3},{3,2},{4,5},{5,4},{6,7},{7,6},{8,9},{9,8},{10,11... | collective-permute-start | bytes 4325384 | tf_op jit(solution)/shard_map/ppermute | solution.py:426
  101.9 21.6 %collective-permute-start.9 = (bf16[96,2048]{1,0:T(8,128)(2,1)}, bf16[96,2048]{1,0:T(8,128)(2,1)S(1)}, u32[]{:S(2)}, u32[]{:S(2)}) collective-permute-start(bf16[96,2048]{1,0:T(8,128)(2,1)} %get-tuple-element.56), channel_id=1, source_target_pairs={{0,14},{2,12},{4,10},{6,8},{8,6},{10,4},{12,2},{14,0},{16,30},{18,... | collective-permute-start | bytes 1179656 | tf_op jit(solution)/shard_map/ppermute | solution.py:464
  112.6 16.9 %collective-permute-start.10 = (bf16[96,2048]{1,0:T(8,128)(2,1)}, bf16[96,2048]{1,0:T(8,128)(2,1)S(1)}, u32[]{:S(2)}, u32[]{:S(2)}) collective-permute-start(bf16[96,2048]{1,0:T(8,128)(2,1)} %get-tuple-element.57), channel_id=1, source_target_pairs={{0,128},{2,130},{4,132},{6,134},{8,136},{10,138},{12,140},{14,142}... | collective-permute-start | bytes 1179656 | tf_op jit(solution)/shard_map/ppermute | solution.py:464
  123.4 16.5 %collective-permute-start.11 = (bf16[96,2048]{1,0:T(8,128)(2,1)}, bf16[96,2048]{1,0:T(8,128)(2,1)S(1)}, u32[]{:S(2)}, u32[]{:S(2)}) collective-permute-start(bf16[96,2048]{1,0:T(8,128)(2,1)} %get-tuple-element.58), channel_id=1, source_target_pairs={{0,134},{2,132},{4,130},{6,128},{8,142},{10,140},{12,138},{14,136}... | collective-permute-start | bytes 1179656 | tf_op jit(solution)/shard_map/ppermute | solution.py:464
  170.0 25.3 %all-to-all-start = ((bf16[8,48,2048]{2,1,0:T(8,128)(2,1)}), bf16[8,48,2048]{2,1,0:T(8,128)(2,1)S(1)}, u32[]{:S(2)}, u32[]{:S(2)}) async-start(bf16[8,48,2048]{2,1,0:T(8,128)(2,1)} %expert.2), calls=%async_computation | async-start | bytes 3145728 | tf_op jit(solution)/shard_map/all_to_all | solution.py:477
  196.5 24.6 %all-to-all-start.1 = ((bf16[8,48,2048]{2,1,0:T(8,128)(2,1)}), bf16[8,48,2048]{2,1,0:T(8,128)(2,1)S(1)}, u32[]{:S(2)}, u32[]{:S(2)}) async-start(bf16[8,48,2048]{2,1,0:T(8,128)(2,1)} %expert.3), calls=%async_computation.1 | async-start | bytes 3145728 | tf_op jit(solution)/shard_map/all_to_all | solution.py:477
  204.6 35.7 %collective-permute-start.27 = (bf16[8,2,64,512]{3,2,1,0:T(8,128)(2,1)}, bf16[8,2,64,512]{3,2,1,0:T(8,128)(2,1)S(1)}, u32[]{:S(2)}, u32[]{:S(2)}) collective-permute-start(bf16[8,2,64,512]{3,2,1,0:T(8,128)(2,1)} %get-tuple-element.73), channel_id=1, source_target_pairs={{0,128},{16,144},{32,160},{48,176},{64,192},{80,208},{96,224},{112... | collective-permute-start | bytes 3145736 | tf_op jit(solution)/shard_map/ppermute | solution.py:505
  222.3 134.0 %all-to-all-start.2 = ((bf16[8,2,2,64,512]{4,3,2,1,0:T(8,128)(2,1)}), bf16[8,2,2,64,512]{4,3,2,1,0:T(8,128)(2,1)S(1)}, u32[]{:S(2)}, u32[]{:S(2)}) async-start(bf16[8,2,2,64,512]{4,3,2,1,0:T(8,128)(2,1)} %get-tuple-element.72), calls=%async_computation.2 | async-start | bytes 4194304 | tf_op jit(solution)/shard_map/all_to_all | solution.py:506
  244.1 40.0 %collective-permute-start.28 = (bf16[2,2,64,512]{3,2,1,0:T(8,128)(2,1)}, bf16[2,2,64,512]{3,2,1,0:T(8,128)(2,1)S(1)}, u32[]{:S(2)}, u32[]{:S(2)}) collective-permute-start(bf16[2,2,64,512]{3,2,1,0:T(8,128)(2,1)} %get-tuple-element.75), channel_id=1, source_target_pairs={{0,16},{16,32},{32,48},{48,64},{64,80},{80,96},{96,112},{112,0},{1... | collective-permute-start | bytes 786440 | tf_op jit(solution)/shard_map/ppermute | solution.py:517
  247.2 46.0 %collective-permute-start.29 = (bf16[2,2,64,512]{3,2,1,0:T(8,128)(2,1)}, bf16[2,2,64,512]{3,2,1,0:T(8,128)(2,1)S(1)}, u32[]{:S(2)}, u32[]{:S(2)}) collective-permute-start(bf16[2,2,64,512]{3,2,1,0:T(8,128)(2,1)} %get-tuple-element.76), channel_id=1, source_target_pairs={{0,32},{16,48},{32,64},{48,80},{64,96},{80,112},{96,0},{112,16},{1... | collective-permute-start | bytes 786440 | tf_op jit(solution)/shard_map/ppermute | solution.py:517
  248.7 67.6 %collective-permute-start.30 = (bf16[2,2,64,512]{3,2,1,0:T(8,128)(2,1)}, bf16[2,2,64,512]{3,2,1,0:T(8,128)(2,1)S(1)}, u32[]{:S(2)}, u32[]{:S(2)}) collective-permute-start(bf16[2,2,64,512]{3,2,1,0:T(8,128)(2,1)} %get-tuple-element.77), channel_id=1, source_target_pairs={{0,48},{16,64},{32,80},{48,96},{64,112},{80,0},{96,16},{112,32},{1... | collective-permute-start | bytes 786440 | tf_op jit(solution)/shard_map/ppermute | solution.py:517
  249.3 68.9 %collective-permute-start.31 = (bf16[2,2,64,512]{3,2,1,0:T(8,128)(2,1)}, bf16[2,2,64,512]{3,2,1,0:T(8,128)(2,1)S(1)}, u32[]{:S(2)}, u32[]{:S(2)}) collective-permute-start(bf16[2,2,64,512]{3,2,1,0:T(8,128)(2,1)} %get-tuple-element.78), channel_id=1, source_target_pairs={{0,64},{16,80},{32,96},{48,112},{64,0},{80,16},{96,32},{112,48},{1... | collective-permute-start | bytes 786440 | tf_op jit(solution)/shard_map/ppermute | solution.py:517
  254.3 63.9 %collective-permute-start.32 = (bf16[2,2,64,512]{3,2,1,0:T(8,128)(2,1)}, bf16[2,2,64,512]{3,2,1,0:T(8,128)(2,1)S(1)}, u32[]{:S(2)}, u32[]{:S(2)}) collective-permute-start(bf16[2,2,64,512]{3,2,1,0:T(8,128)(2,1)} %get-tuple-element.79), channel_id=1, source_target_pairs={{0,80},{16,96},{32,112},{48,0},{64,16},{80,32},{96,48},{112,64},{1... | collective-permute-start | bytes 786440 | tf_op jit(solution)/shard_map/ppermute | solution.py:517
  284.0 34.3 %collective-permute-start.33 = (bf16[2,2,64,512]{3,2,1,0:T(8,128)(2,1)}, bf16[2,2,64,512]{3,2,1,0:T(8,128)(2,1)}, u32[]{:S(2)}, u32[]{:S(2)}) collective-permute-start(bf16[2,2,64,512]{3,2,1,0:T(8,128)(2,1)} %get-tuple-element.80), channel_id=1, source_target_pairs={{0,96},{16,112},{32,0},{48,16},{64,32},{80,48},{96,64},{112,80},{1... | collective-permute-start | bytes 786440 | tf_op jit(solution)/shard_map/ppermute | solution.py:517
  293.2 27.5 %collective-permute-start.34 = (bf16[2,2,64,512]{3,2,1,0:T(8,128)(2,1)}, bf16[2,2,64,512]{3,2,1,0:T(8,128)(2,1)}, u32[]{:S(2)}, u32[]{:S(2)}) collective-permute-start(bf16[2,2,64,512]{3,2,1,0:T(8,128)(2,1)} %get-tuple-element.81), channel_id=1, source_target_pairs={{0,112},{16,0},{32,16},{48,32},{64,48},{80,64},{96,80},{112,96},{1... | collective-permute-start | bytes 786440 | tf_op jit(solution)/shard_map/ppermute | solution.py:517
  316.2 16.9 %collective-permute-start.20 = (bf16[64,2048]{1,0:T(8,128)(2,1)}, bf16[64,2048]{1,0:T(8,128)(2,1)}, u32[]{:S(2)}, u32[]{:S(2)}) collective-permute-start(bf16[64,2048]{1,0:T(8,128)(2,1)} %get-tuple-element.61), channel_id=1, source_target_pairs={{0,16},{16,32},{32,48},{48,64},{64,80},{80,96},{96,112},{112,0},{1... | collective-permute-start | bytes 786440 | tf_op jit(solution)/shard_map/ppermute | solution.py:490
  323.5 32.8 %collective-permute-start.35 = (bf16[8,2,64,512]{3,2,1,0:T(8,128)(2,1)}, bf16[8,2,64,512]{3,2,1,0:T(8,128)(2,1)S(1)}, u32[]{:S(2)}, u32[]{:S(2)}) collective-permute-start(bf16[8,2,64,512]{3,2,1,0:T(8,128)(2,1)} %collect.1), channel_id=1, source_target_pairs={{0,128},{16,144},{32,160},{48,176},{64,192},{80,208},{96,224},{112... | collective-permute-start | bytes 3145736 | tf_op jit(solution)/shard_map/ppermute | solution.py:523
  347.2 15.9 %collective-permute-start.26 = (bf16[64,2048]{1,0:T(8,128)(2,1)}, bf16[64,2048]{1,0:T(8,128)(2,1)S(1)}, u32[]{:S(2)}, u32[]{:S(2)}) collective-permute-start(bf16[64,2048]{1,0:T(8,128)(2,1)} %add_convert_fusion.1), channel_id=1, source_target_pairs={{16,0},{32,16},{48,32},{64,48},{80,64},{96,80},{112,96},{0,112},{1... | collective-permute-start | bytes 786440 | tf_op jit(solution)/shard_map/ppermute | solution.py:494
  (46 other events, 542.8 us)
